TPU v7x, 128 devices: a whole 4x4x4 slice. The times are simulated.
128 devices in a mesh: pool: 32 (over y, x, core), head: 4 (over z).
Axes of the slice: x: 4, y: 4, z: 4, core: 2. Of those that a mesh axis runs over, the one named last changes fastest.
Arguments:
- x_rows: bfloat16 [1024, 4096], P('pool'), may hold values from -3 to 3
- query: bfloat16 [1024, 4096], P('pool', 'head'), may hold values from -170 to 170
- key_cache: bfloat16 [1024, 4, 512, 128], P('pool', 'head'), may hold values from -6 to 6
- value_cache: bfloat16 [1024, 4, 512, 128], P('pool', 'head'), may hold values from -6 to 6
- new_key: bfloat16 [1024, 512], P('pool', 'head'), may hold values from -6 to 6
- new_value: bfloat16 [1024, 512], P('pool', 'head'), may hold values from -6 to 6
- lengths: int32 [1024], P('pool'), may hold values from 2 to 512, as said below
- out_proj: bfloat16 [4096, 4096], P('head'), may hold values from -0.5 to 0.5
- norm_gain: float32 [4096], replicated, may hold values from 0.5 to 1.5
- expert_ids: int32 [1024, 8], P('pool'), may hold values from 0 to 63, all different within a row; in each aligned block of 32 rows (0 to 31, 32 to 63, ...) at most 8 rows name the same one
- gate_weights: float32 [1024, 8], P('pool'), may hold values from 0.05 to 1
- w_gate: bfloat16 [64, 4096, 1024], P('pool', None, 'head'), may hold values from -0.09375 to 0.09375
- w_up: bfloat16 [64, 4096, 1024], P('pool', None, 'head'), may hold values from -0.09375 to 0.09375
- w_down: bfloat16 [64, 1024, 4096], P('pool', 'head'), may hold values from -0.1875 to 0.1875
Outputs:
- layer_out: bfloat16 [1024, 4096], P('pool', 'head')
Inputs may be any that keep to these rules, and one draw needn't show every extreme that they name: `expert_ids`: within the 32 requests of one index of pool, no expert is named by more than 8 pairs, a bound that some block reaches. `lengths`: request 0 uses all 512 slots.
All inputs are finite; a program needn't handle non-finite values.
Results may differ from a plain program's by a relative error of at most 0.017.
Values may be sent and summed in bfloat16 or wider, within the bound.
No kernel may reach another device: no remote copies, remote signals or barrier semaphores. Data moves between devices by JAX's collectives and lax.ppermute only.
A program may use at most 128 MiB of HBM per device.

v0:
```python
import jax
import jax.numpy as jnp
from jax import lax
from jax.experimental import pallas as pl
from jax.experimental.pallas import tpu as pltpu
from jax.sharding import PartitionSpec as P


F32 = jnp.float32
BF16 = jnp.bfloat16
GROUP = 8
HEAD, ROW, COLUMN, CORE = range(4)
FAR_ORDER = ((2, 0), (2, 1), (1, 0), (3, 0), (1, 1), (3, 1), (0, 1))


def attend_kernel(lengths, place, q_ref, k_ref, v_ref, nk_ref, nv_ref, proj_hbm, *outs):
    *out_refs, rows_ref, proj_ref, sems = outs
    step = pl.program_id(0)
    steps = pl.num_programs(0)
    parts = sems.shape[0]
    depth = proj_ref.shape[0] // parts

    def part(i):
        cut = pl.ds(i * depth, depth)
        return pltpu.make_async_copy(proj_hbm.at[cut], proj_ref.at[cut], sems.at[i])

    @pl.when(step == 0)
    def _():
        for i in range(parts):
            part(i).start()

    size = nk_ref.shape[1]
    heads = q_ref.shape[1] // size
    slots = k_ref.shape[2]
    scale = size ** (-0.5)
    base = pl.multiple_of(step * GROUP, GROUP)
    queries = q_ref[pl.ds(base, GROUP), :].astype(F32)
    new_keys = nk_ref[pl.ds(base, GROUP), :].astype(F32)
    new_values = nv_ref[pl.ds(base, GROUP), :].astype(F32)
    slot_of = lax.broadcasted_iota(jnp.int32, (heads, slots), 1)
    done = []
    blank = jnp.zeros((heads, size), F32)
    for j in range(0, GROUP, 2):
        pair = [
            jnp.concatenate([queries[k : k + 1, i * size : (i + 1) * size] for i in range(heads)], 0)
            for k in (j, j + 1)
        ]
        spread = jnp.concatenate(
            [jnp.concatenate([pair[0], blank], 1), jnp.concatenate([blank, pair[1]], 1)], 0
        )
        keys = jnp.concatenate([k_ref[j, 0], k_ref[j + 1, 0]], 1)
        values = jnp.concatenate([v_ref[j, 0], v_ref[j + 1, 0]], 1)
        scores = (
            lax.dot_general(
                spread.astype(BF16), keys, (((1,), (1,)), ((), ())), preferred_element_type=F32
            )
            * scale
        )
        fresh = [
            jnp.sum(pair[k] * new_keys[j + k : j + k + 1], 1, keepdims=True) for k in range(2)
        ]
        fresh = jnp.concatenate(fresh, 0) * scale
        live = jnp.concatenate([slot_of < lengths[base + j + k] for k in range(2)], 0)
        scores = jnp.where(live, scores, -1e30)
        highest = jnp.maximum(jnp.max(scores, 1, keepdims=True), fresh)
        weights = jnp.where(live, jnp.exp(scores - highest), 0.0)
        own = jnp.exp(fresh - highest)
        total = jnp.sum(weights, 1, keepdims=True) + own
        share = 1.0 / total
        probs = (weights * share).astype(BF16)
        own = (own * share).astype(BF16).astype(F32)
        mixed = jnp.dot(probs, values, preferred_element_type=F32)
        for k in range(2):
            rows = slice(k * heads, (k + 1) * heads)
            part_sum = mixed[rows, k * size : (k + 1) * size] + own[rows] * new_values[j + k : j + k + 1]
            done.append(jnp.concatenate([part_sum[i : i + 1] for i in range(heads)], 1))
    rows_ref[pl.ds(base, GROUP), :] = jnp.concatenate(done, 0)

    @pl.when(step == steps - 1)
    def _():
        attn = rows_ref[...].astype(BF16)
        for i in range(parts):
            part(i).wait()
        groups = len(out_refs)
        share = out_refs[0].shape[1]
        for ahead in [*range(1, groups), 0]:
            column = lax.rem(place[HEAD] + ahead, groups) * share
            weight = proj_ref[:, pl.ds(pl.multiple_of(column, share), share)]
            terms = jnp.dot(attn, weight, preferred_element_type=F32)
            out_refs[ahead][...] = terms.astype(out_refs[ahead].dtype)


def in_hbm(value):
    return pltpu.with_memory_space_constraint(value, pltpu.HBM)


def in_vmem(values):
    return [pltpu.with_memory_space_constraint(value, pltpu.VMEM) for value in values]


def attend_project(query, key_cache, value_cache, new_key, new_value, lengths, place, out_proj, groups):
    rows, wide = query.shape
    size = new_key.shape[1]
    slots = key_cache.shape[2]
    share = out_proj.shape[1] // groups
    whole = lambda shape: pl.BlockSpec(shape, lambda s, *_: (0, 0))
    cache = pl.BlockSpec((GROUP, 1, slots, size), lambda s, *_: (s, 0, 0, 0))
    return pl.pallas_call(
        attend_kernel,
        out_shape=[
            jax.ShapeDtypeStruct((rows, share), BF16 if ahead else F32) for ahead in range(groups)
        ],
        grid_spec=pltpu.PrefetchScalarGridSpec(
            num_scalar_prefetch=2,
            grid=(rows // GROUP,),
            in_specs=[
                whole((rows, wide)),
                cache,
                cache,
                whole((rows, size)),
                whole((rows, size)),
                pl.BlockSpec(memory_space=pl.ANY),
            ],
            out_specs=[whole((rows, share))] * groups,
            scratch_shapes=[
                pltpu.VMEM((rows, wide), F32),
                pltpu.VMEM(out_proj.shape, BF16),
                pltpu.SemaphoreType.DMA((4,)),
            ],
        ),
        compiler_params=pltpu.CompilerParams(
            dimension_semantics=("arbitrary",), vmem_limit_bytes=24 << 20
        ),
        name="attend_project",
    )(
        in_hbm(lengths),
        place,
        in_hbm(query),
        in_hbm(key_cache),
        in_hbm(value_cache),
        in_hbm(new_key),
        in_hbm(new_value),
        in_hbm(out_proj),
    )


def norm_kernel(place, own_ref, *refs):
    *other_refs, gain_ref, ids_ref, first_ref, second_ref = refs
    groups = 1 + len(other_refs)
    rows, share = own_ref.shape
    blocks = [own_ref[...]] + [ref[...].astype(F32) for ref in other_refs]
    square = sum(jnp.sum(block * block, 1, keepdims=True) for block in blocks)
    inverse = lax.rsqrt(square / (groups * share) + 1e-06)
    half = groups // 2
    for back, block in enumerate(blocks):
        gain = gain_ref[lax.rem(place[HEAD] + groups - back, groups)]
        out_ref = (first_ref, second_ref)[back // half]
        cut = (back % half) * share
        out_ref[:rows, cut : cut + share] = (block * inverse * gain).astype(BF16)
    for out_ref in (first_ref, second_ref):
        out_ref[rows:, :] = jnp.zeros((ids_ref.shape[0], half * share), BF16)
        out_ref[rows:, : ids_ref.shape[1]] = ids_ref[...]


def norm_rows(own, others, norm_gain, ids, place):
    rows, share = own.shape
    groups = 1 + len(others)
    gains = norm_gain.reshape(groups, 1, share)
    shape = jax.ShapeDtypeStruct((rows + ids.shape[0], groups // 2 * share), BF16)
    vmem = pl.BlockSpec(memory_space=pltpu.VMEM)
    return pl.pallas_call(
        norm_kernel,
        out_shape=[shape, shape],
        in_specs=[pl.BlockSpec(memory_space=pltpu.SMEM)] + [vmem] * (groups + 2),
        out_specs=[vmem, vmem],
        compiler_params=pltpu.CompilerParams(vmem_limit_bytes=8 << 20),
        name="norm_rows",
    )(place, *in_vmem([own, *others]), gains, ids)


def pick_kernel(place, *refs):
    count = 4
    pools = (place[ROW], place[COLUMN], place[CORE])
    slots, near, cores = refs[-1].shape[0], count, 2
    targets = count * cores
    depth = 32
    lanes = near * depth
    total = targets * slots
    line = lax.broadcasted_iota(jnp.int32, (total, lanes), 0)
    lane = lax.broadcasted_iota(jnp.int32, (total, lanes), 1)
    step, flip = line >> 7, (line >> 6) & 1
    expert, source, rank = (line >> 5) & 1, (line >> 3) & 3, line & 7
    core = pools[2] ^ flip
    upper_line = lax.broadcasted_iota(jnp.int32, (lanes, lanes), 0)
    upper_lane = lax.broadcasted_iota(jnp.int32, (lanes, lanes), 1)
    earlier = ((upper_line < upper_lane) & ((upper_line >> 5) == (upper_lane >> 5))).astype(F32)
    id_lane = lax.broadcasted_iota(jnp.int32, (8, lanes), 1) >> 5
    for half in range(2):
        ins = refs[half * near : (half + 1) * near]
        outs = refs[(2 + 2 * half) * near : (4 + 2 * half) * near]
        if half == 0:
            target = ((pools[0] + step) & 3) * 8 + pools[1] * 2 + core
        else:
            target = pools[0] * 8 + ((pools[1] + step) & 3) * 2 + core
        wanted = (target * 2 + expert).astype(F32)
        ids = jnp.zeros((8, lanes), F32)
        for back, ref in enumerate(ins):
            ids = jnp.where(id_lane == back, ref[depth:, :lanes].astype(F32), ids)
        hit = ids[0:1] == wanted
        for k in range(1, 8):
            hit = hit | (ids[k : k + 1] == wanted)
        hits = jnp.where(hit, 1.0, 0.0).astype(BF16)
        order = jnp.dot(hits, earlier.astype(BF16), preferred_element_type=F32)
        chosen = hit & (order == rank.astype(F32)) & ((lane >> 5) == source)
        table = jnp.where(chosen, 1.0, 0.0).astype(BF16)
        rows = jnp.concatenate([ref[:depth, :] for ref in ins], 0)
        picked = jnp.dot(table, rows, preferred_element_type=F32).astype(BF16)
        for i, out_ref in enumerate(outs):
            out_ref[...] = picked[i * slots : (i + 1) * slots]


def pick_rows(first, second, place):
    width = first[0].shape[1]
    shape = jax.ShapeDtypeStruct((64, width), BF16)
    vmem = pl.BlockSpec(memory_space=pltpu.VMEM)
    out = pl.pallas_call(
        pick_kernel,
        out_shape=[shape] * 16,
        in_specs=[pl.BlockSpec(memory_space=pltpu.SMEM)] + [vmem] * 8,
        out_specs=[vmem] * 16,
        compiler_params=pltpu.CompilerParams(vmem_limit_bytes=16 << 20),
        name="pick_rows",
    )(place, *in_vmem([*first, *second]))
    return out[:8], out[8:]


def load_kernel(*refs):
    *ins, first_sem = refs
    count = len(ins) // 2
    copies = [
        pltpu.make_async_copy(source.at[e], target.at[e], first_sem.at[i, e])
        for i, (source, target) in enumerate(zip(ins[:count], ins[count:]))
        for e in range(source.shape[0])
    ]
    for copy in copies:
        copy.start()
    for copy in copies:
        copy.wait()


def load(*values):
    return pl.pallas_call(
        load_kernel,
        out_shape=[pltpu.VMEM(value.shape, value.dtype) for value in values],
        in_specs=[pl.BlockSpec(memory_space=pl.ANY)] * len(values),
        out_specs=[pl.BlockSpec(memory_space=pltpu.VMEM)] * len(values),
        scratch_shapes=[pltpu.SemaphoreType.DMA((len(values), values[0].shape[0]))],
        compiler_params=pltpu.CompilerParams(vmem_limit_bytes=1 << 20),
        name="load",
    )(*[in_hbm(value) for value in values])


def gate_up_kernel(place, *refs):
    first, second = refs[:8], refs[8:16]
    gate_ref, up_ref, act_ref, sum_ref = refs[16:]
    experts, width, units = gate_ref.shape
    share = first[0].shape[1] // 2
    groups = width // share
    rows = act_ref.shape[1]
    kinds = 2
    half = groups // 2
    for e in range(experts):
        sums = {}
        for back in range(groups):
            source = (first, second)[back // half]
            cut = slice((back % half) * share, (back % half + 1) * share)
            x = jnp.concatenate([ref[e * 32 : (e + 1) * 32, cut] for ref in source], 0)
            depth = lax.rem(place[HEAD] + groups - back, groups) * share
            depth = pl.ds(pl.multiple_of(depth, share), share)
            for kind, ref in enumerate((gate_ref, up_ref)):
                term = jnp.dot(x, ref[e, depth, :], preferred_element_type=F32)
                key = (kind, back // half)
                sums[key] = sums[key] + term if key in sums else term
        for dy in range(4):
            for dc in range(2):
                for dx in range(4):
                    pool = (
                        ((place[ROW] + 4 - dy) & 3) * 8
                        + ((place[COLUMN] + 4 - dx) & 3) * 2
                        + (place[CORE] ^ dc)
                    )
                    a = ((dy * 2 + dc) * 4 + dx) * 8
                    b = ((dx * 2 + dc) * 4 + dy) * 8
                    for kind in range(kinds):
                        sum_ref[kind, pool] = (
                            sums[kind, 0][a : a + 8] + sums[kind, 1][b : b + 8]
                        )
        gate = sum_ref[0].reshape(rows, units)
        up = sum_ref[1].reshape(rows, units)
        act_ref[e] = (gate / (1.0 + jnp.exp(-gate)) * up).astype(act_ref.dtype)


def gate_up(first, second, w_gate, w_up, place, pools, capacity):
    experts, _, units = w_gate.shape
    rows = pools * capacity
    vmem = pl.BlockSpec(memory_space=pltpu.VMEM)
    return pl.pallas_call(
        gate_up_kernel,
        out_shape=jax.ShapeDtypeStruct((experts, rows, units), BF16),
        in_specs=[pl.BlockSpec(memory_space=pltpu.SMEM)] + [vmem] * 18,
        out_specs=vmem,
        scratch_shapes=[pltpu.VMEM((2, pools, capacity, units), F32)],
        compiler_params=pltpu.CompilerParams(vmem_limit_bytes=12 << 20),
        name="gate_up",
    )(place, *in_vmem([*first, *second, w_gate, w_up]))


def down_kernel(*refs):
    *ins, out_ref = refs
    count = len(ins) // 2
    total = 0.0
    for act_ref, weight_ref in zip(ins[:count], ins[count:]):
        total = total + jnp.dot(act_ref[0], weight_ref[0], preferred_element_type=F32)
    out_ref[...] = total.astype(out_ref.dtype).reshape(out_ref.shape)


def down(acts, weights, pools, capacity):
    experts, rows, units = acts[0].shape
    share = weights[0].shape[2]
    return pl.pallas_call(
        down_kernel,
        out_shape=jax.ShapeDtypeStruct((pools, experts * capacity, share), BF16),
        grid=(experts,),
        in_specs=[pl.BlockSpec((1, rows, units), lambda e: (e, 0, 0))] * len(acts)
        + [pl.BlockSpec((1, units, share), lambda e: (e, 0, 0))] * len(weights),
        out_specs=pl.BlockSpec((pools, capacity, share), lambda e: (0, e, 0)),
        compiler_params=pltpu.CompilerParams(
            dimension_semantics=("arbitrary",), vmem_limit_bytes=16 << 20
        ),
        name="down",
    )(*in_vmem([*acts, *weights]))


def route_slots(expert_ids, capacity):
    flat = expert_ids.reshape(-1)
    order = jnp.arange(flat.shape[0])
    earlier = (flat[:, None] == flat[None, :]) & (order[None, :] < order[:, None])
    rank = jnp.sum(earlier.astype(jnp.int32), 1)
    return (flat * capacity + rank).reshape(expert_ids.shape)


def turned(value, step):
    groups = lax.axis_size("head")
    return lax.ppermute(value, "head", [(i, (i + step) % groups) for i in range(groups)])


def moved_in_plane(value, dy, dx, dc):
    pairs = []
    for y in range(4):
        for x in range(4):
            for c in range(2):
                to = (y + dy) % 4 * 8 + (x + dx) % 4 * 2 + (c ^ dc)
                pairs.append((y * 8 + x * 2 + c, to))
    return lax.ppermute(value, "pool", pairs)


def body(
    x_rows,
    query,
    key_cache,
    value_cache,
    new_key,
    new_value,
    lengths,
    out_proj,
    norm_gain,
    expert_ids,
    gate_weights,
    w_gate,
    w_up,
    w_down,
):
    pools = lax.axis_size("pool")
    groups = lax.axis_size("head")
    rows, width = x_rows.shape
    share = width // groups
    experts = w_gate.shape[0]
    capacity = max(2, 2 * expert_ids.shape[0] * expert_ids.shape[1] // (pools * experts))
    slots = experts * capacity
    head = lax.axis_index("head")
    steps = range(1, groups)

    pool = lax.axis_index("pool")
    place = jnp.stack([head, pool >> 3, (pool >> 1) & 3, pool & 1]).astype(jnp.int32)
    own, *away = attend_project(
        query, key_cache, value_cache, new_key, new_value, lengths, place, out_proj, groups
    )
    others = [turned(piece, step) for step, piece in zip(steps, away)]
    slot = route_slots(expert_ids, capacity)
    matching = jnp.arange(pools * slots)[:, None, None] == slot[None, :, :]
    take = jnp.sum(jnp.where(matching, gate_weights[None, :, :], 0.0), 2).T
    take_high = take.astype(BF16)
    take_low = (take - take_high.astype(F32)).astype(BF16)
    ids = jnp.tile(expert_ids.T.astype(BF16), (1, 128 // rows))
    columns = [
        lax.dynamic_slice_in_dim(w_down, lax.rem(head + step, groups) * share, share, 2)
        for step in range(groups)
    ]
    others, columns = lax.optimization_barrier((others, columns))
    hidden = lax.dynamic_slice_in_dim(x_rows, head * share, share, 1).astype(F32) + own
    for other in others:
        hidden = hidden + other.astype(F32)
    slices = [turned(hidden.astype(BF16), step) for step in steps]
    moved = [turned(piece, step) for step, piece in zip(steps, columns[1:])]
    first, second = norm_rows(hidden, slices, norm_gain, ids, place)
    along_x = [first] + [moved_in_plane(first, 0, step, 0) for step in (1, 2, 3)]
    along_y = [second] + [moved_in_plane(second, step, 0, 0) for step in (1, 2, 3)]
    for_y, for_x = pick_rows(along_x, along_y, place)
    ways = [(step, flip) for step in range(4) for flip in range(2)]
    from_y, from_x = list(for_y), list(for_x)
    for step, flip in FAR_ORDER:
        way = ways.index((step, flip))
        from_y[way] = moved_in_plane(for_y[way], step, 0, flip)
        from_x[way] = moved_in_plane(for_x[way], 0, step, flip)
    gate_near, up_near = load(w_gate, w_up)
    act = gate_up(from_y, from_x, gate_near, up_near, place, pools, capacity)
    acts = [act] + [turned(act, step) for step in steps]
    produced = down(acts, [columns[0]] + moved, pools, capacity)
    returned = lax.all_to_all(produced, "pool", split_axis=0, concat_axis=0, tiled=True)
    returned = returned.reshape(pools * slots, share)
    moe = jnp.dot(take_high, returned, preferred_element_type=F32) + jnp.dot(
        take_low, returned, preferred_element_type=F32
    )
    return (hidden + moe).astype(BF16)


def solution(mesh):
    placed = (
        P("pool", None),
        P("pool", "head"),
        P("pool", "head", None, None),
        P("pool", "head", None, None),
        P("pool", "head"),
        P("pool", "head"),
        P("pool"),
        P("head", None),
        P(),
        P("pool", None),
        P("pool", None),
        P("pool", None, "head"),
        P("pool", None, "head"),
        P("pool", "head", None),
    )
    return jax.shard_map(
        body, mesh=mesh, in_specs=placed, out_specs=P("pool", "head"), check_vma=False
    )
```

profile of v0, /device:TPU:0, one launch (start us, length us, event | category | flops | bytes accessed | tf_op | source)
XLA Modules:
  0.0 173.7 jit_solution(7182888225873180879)
XLA Ops:
  0.1 13.9 %attend_project.1 = (f32[32,1024]{1,0:T(8,128)S(1)}, bf16[32,1024]{1,0:T(8,128)(2,1)S(1)}, bf16[32,1024]{1,0:T(8,128)(2,1)S(1)}, bf16[32,1024]{1,0:T(8,128)(2,1)S(1)}) custom-call(s32[32]{0:T(128)} %lengths.1, s32[4]{0:T(128)S(1)} %pad_add_fusion.place, bf16[32,1024]{1,0:T(8,128)(2,1)} %q_ref.1, bf16[32,1,512,128]{3,2,1,0:T(8,128)(2,1)} %k_ref.1, ...), custom_call_target="tpu_custom_call" | custom-call | tf_op jit(solution)/shard_map/attend_project/pallas_call | solution.py:108
  14.0 2.1 %collective-permute-start = (bf16[32,1024]{1,0:T(8,128)(2,1)S(1)}, bf16[32,1024]{1,0:T(8,128)(2,1)S(1)}, u32[]{:S(2)}, u32[]{:S(2)}) collective-permute-start(bf16[32,1024]{1,0:T(8,128)(2,1)S(1)} %get-tuple-element.37), channel_id=1, source_target_pairs={{0,1},{1,2},{2,3},{3,0},{4,5},{5,6},{6,7},{7,4},{8,9},{9,10},{10,1... | collective-permute-start | bytes 196616 | tf_op jit(solution)/shard_map/ppermute | solution.py:354
  16.1 3.6 %collective-permute-start.1 = (bf16[32,1024]{1,0:T(8,128)(2,1)S(1)}, bf16[32,1024]{1,0:T(8,128)(2,1)S(1)}, u32[]{:S(2)}, u32[]{:S(2)}) collective-permute-start(bf16[32,1024]{1,0:T(8,128)(2,1)S(1)} %get-tuple-element.38), channel_id=1, source_target_pairs={{0,2},{1,3},{2,0},{3,1},{4,6},{5,7},{6,4},{7,5},{8,10},{9,11},{10,... | collective-permute-start | bytes 196616 | tf_op jit(solution)/shard_map/ppermute | solution.py:354
  20.7 4.1 %constant_dynamic-slice_fusion = (bf16[2,256,1024]{2,1,0:T(8,128)(2,1)S(1)}, bf16[2,256,1024]{2,1,0:T(8,128)(2,1)}, bf16[2,256,1024]{2,1,0:T(8,128)(2,1)S(1)}, bf16[2,256,1024]{2,1,0:T(8,128)(2,1)}) fusion(bf16[2,256,4096]{2,1,0:T(8,128)(2,1)} %param.27, s32[]{:T(128)S(6)} %select_n.23, s32[]{:T(128)S(6)} %select_n.21, s32[]{:T(128)S(6)} %select_n.20, ...), kind=kLoop, calls=%fused_computation.15 | loop fusion | bytes 8388624 | tf_op jit(solution)/shard_map/dynamic_slice | solution.py:406
  26.8 1.8 %collective-permute-start.4 = (bf16[32,1024]{1,0:T(8,128)(2,1)S(1)}, bf16[32,1024]{1,0:T(8,128)(2,1)S(1)}, u32[]{:S(2)}, u32[]{:S(2)}) collective-permute-start(bf16[32,1024]{1,0:T(8,128)(2,1)S(1)} %get-tuple-element.67), channel_id=1, source_target_pairs={{0,2},{1,3},{2,0},{3,1},{4,6},{5,7},{6,4},{7,5},{8,10},{9,11},{10,... | collective-permute-start | bytes 196616 | tf_op jit(solution)/shard_map/ppermute | solution.py:354
  29.7 1.6 collective-permute-done.3.refs_0_
  33.6 3.3 %collective-permute-start.10 = (bf16[40,2048]{1,0:T(8,128)(2,1)S(1)}, bf16[40,2048]{1,0:T(8,128)(2,1)S(1)}, u32[]{:S(2)}, u32[]{:S(2)}) collective-permute-start(bf16[40,2048]{1,0:T(8,128)(2,1)S(1)} %get-tuple-element.44.refs_4_), channel_id=1, source_target_pairs={{0,64},{4,68},{8,72},{12,76},{16,80},{20,84},{24,88},{28,92},{32,9... | collective-permute-start | bytes 491528 | tf_op jit(solution)/shard_map/ppermute | solution.py:364
  37.9 1.5 collective-permute-start.6
  39.4 2.7 %collective-permute-start.7 = (bf16[40,2048]{1,0:T(8,128)(2,1)S(1)}, bf16[40,2048]{1,0:T(8,128)(2,1)S(1)}, u32[]{:S(2)}, u32[]{:S(2)}) collective-permute-start(bf16[40,2048]{1,0:T(8,128)(2,1)S(1)} %get-tuple-element.43.refs_0_), channel_id=1, source_target_pairs={{0,16},{4,20},{8,24},{12,28},{16,0},{20,4},{24,8},{28,12},{32,48},... | collective-permute-start | bytes 491528 | tf_op jit(solution)/shard_map/ppermute | solution.py:364
  45.2 1.9 %collective-permute-done.7.refs_2_ = bf16[40,2048]{1,0:T(8,128)(2,1)S(1)} collective-permute-done((bf16[40,2048]{1,0:T(8,128)(2,1)S(1)}, bf16[40,2048]{1,0:T(8,128)(2,1)S(1)}, u32[]{:S(2)}, u32[]{:S(2)}) %collective-permute-start.7) | collective-permute-done | bytes 163872 | tf_op jit(solution)/shard_map/ppermute | solution.py:364
  47.5 2.6 %collective-permute-done.9.refs_5_ = bf16[40,2048]{1,0:T(8,128)(2,1)S(1)} collective-permute-done((bf16[40,2048]{1,0:T(8,128)(2,1)S(1)}, bf16[40,2048]{1,0:T(8,128)(2,1)S(1)}, u32[]{:S(2)}, u32[]{:S(2)}) %collective-permute-start.9) | collective-permute-done | bytes 163872 | tf_op jit(solution)/shard_map/ppermute | solution.py:364
  50.1 2.3 %pick_rows.1 = (bf16[64,2048]{1,0:T(8,128)(2,1)S(1)}, bf16[64,2048]{1,0:T(8,128)(2,1)S(1)}, bf16[64,2048]{1,0:T(8,128)(2,1)S(1)}, bf16[64,2048]{1,0:T(8,128)(2,1...) custom-call(s32[4]{0:T(128)S(1)} %pad_add_fusion.place, ...), custom_call_target="tpu_custom_call" | custom-call | tf_op jit(solution)/shard_map/pick_rows/pallas_call | solution.py:226
  52.8 4.3 %collective-permute-start.15 = (bf16[64,2048]{1,0:T(8,128)(2,1)S(1)}, bf16[64,2048]{1,0:T(8,128)(2,1)S(1)}, u32[]{:S(2)}, u32[]{:S(2)}) collective-permute-start(bf16[64,2048]{1,0:T(8,128)(2,1)S(1)} %get-tuple-element.49), channel_id=1, source_target_pairs={{0,64},{4,68},{8,72},{12,76},{16,80},{20,84},{24,88},{28,92},{32,9... | collective-permute-start | bytes 786440 | tf_op jit(solution)/shard_map/ppermute | solution.py:364
  57.0 1.8 %collective-permute-start.17 = (bf16[64,2048]{1,0:T(8,128)(2,1)S(1)}, bf16[64,2048]{1,0:T(8,128)(2,1)S(1)}, u32[]{:S(2)}, u32[]{:S(2)}) collective-permute-start(bf16[64,2048]{1,0:T(8,128)(2,1)S(1)} %get-tuple-element.51), channel_id=1, source_target_pairs={{0,96},{4,100},{8,104},{12,108},{16,112},{20,116},{24,120},{28,124... | collective-permute-start | bytes 786440 | tf_op jit(solution)/shard_map/ppermute | solution.py:364
  58.9 4.1 %collective-permute-done.13.refs_2_ = bf16[64,2048]{1,0:T(8,128)(2,1)S(1)} collective-permute-done((bf16[64,2048]{1,0:T(8,128)(2,1)S(1)}, bf16[64,2048]{1,0:T(8,128)(2,1)S(1)}, u32[]{:S(2)}, u32[]{:S(2)}) %collective-permute-start.13) | collective-permute-done | bytes 262176 | tf_op jit(solution)/shard_map/ppermute | solution.py:364
  63.0 15.8 %collective-permute-done.14.refs_3_ = bf16[64,2048]{1,0:T(8,128)(2,1)S(1)} collective-permute-done((bf16[64,2048]{1,0:T(8,128)(2,1)S(1)}, bf16[64,2048]{1,0:T(8,128)(2,1)S(1)}, u32[]{:S(2)}, u32[]{:S(2)}) %collective-permute-start.14) | collective-permute-done | bytes 262176 | tf_op jit(solution)/shard_map/ppermute | solution.py:364
  79.7 3.6 %collective-permute-start.22 = (bf16[64,2048]{1,0:T(8,128)(2,1)S(1)}, bf16[64,2048]{1,0:T(8,128)(2,1)S(1)}, u32[]{:S(2)}, u32[]{:S(2)}) collective-permute-start(bf16[64,2048]{1,0:T(8,128)(2,1)S(1)} %get-tuple-element.57), channel_id=1, source_target_pairs={{0,16},{4,20},{8,24},{12,28},{16,0},{20,4},{24,8},{28,12},{32,48},... | collective-permute-start | bytes 786440 | tf_op jit(solution)/shard_map/ppermute | solution.py:364
  84.9 4.6 %collective-permute-done.20.refs_10_ = bf16[64,2048]{1,0:T(8,128)(2,1)S(1)} collective-permute-done((bf16[64,2048]{1,0:T(8,128)(2,1)S(1)}, bf16[64,2048]{1,0:T(8,128)(2,1)S(1)}, u32[]{:S(2)}, u32[]{:S(2)}) %collective-permute-start.20) | collective-permute-done | bytes 262176 | tf_op jit(solution)/shard_map/ppermute | solution.py:364
  89.5 1.8 %collective-permute-start.30 = (bf16[2,256,1024]{2,1,0:T(8,128)(2,1)}, bf16[2,256,1024]{2,1,0:T(8,128)(2,1)S(1)}, u32[]{:S(2)}, u32[]{:S(2)}) collective-permute-start(bf16[2,256,1024]{2,1,0:T(8,128)(2,1)} %get-tuple-element.65), channel_id=1, source_target_pairs={{0,2},{1,3},{2,0},{3,1},{4,6},{5,7},{6,4},{7,5},{8,10},{9,11},{10,... | collective-permute-start | bytes 3145736 | tf_op jit(solution)/shard_map/ppermute | solution.py:354
  91.2 13.4 %collective-permute-done.21.refs_11_ = bf16[64,2048]{1,0:T(8,128)(2,1)S(1)} collective-permute-done((bf16[64,2048]{1,0:T(8,128)(2,1)S(1)}, bf16[64,2048]{1,0:T(8,128)(2,1)S(1)}, u32[]{:S(2)}, u32[]{:S(2)}) %collective-permute-start.21) | collective-permute-done | bytes 262176 | tf_op jit(solution)/shard_map/ppermute | solution.py:364
  104.7 2.7 %collective-permute-start.31 = (bf16[2,256,1024]{2,1,0:T(8,128)(2,1)S(1)}, bf16[2,256,1024]{2,1,0:T(8,128)(2,1)S(1)}, u32[]{:S(2)}, u32[]{:S(2)}) collective-permute-start(bf16[2,256,1024]{2,1,0:T(8,128)(2,1)S(1)} %get-tuple-element.66), channel_id=1, source_target_pairs={{0,3},{1,0},{2,1},{3,2},{4,7},{5,4},{6,5},{7,6},{8,11},{9,8},{10,9... | collective-permute-start | bytes 3145736 | tf_op jit(solution)/shard_map/ppermute | solution.py:354
  107.7 3.5 %load.1 = (bf16[2,4096,256]{2,1,0:T(8,128)(2,1)S(1)}, bf16[2,4096,256]{2,1,0:T(8,128)(2,1)S(1)}) custom-call(bf16[2,4096,256]{2,1,0:T(8,128)(2,1)} %refs_0_.1, bf16[2,4096,256]{2,1,0:T(8,128)(2,1)} %refs_1_.1), custom_call_target="tpu_custom_call" | custom-call | tf_op jit(solution)/shard_map/load/pallas_call | solution.py:252
  111.2 5.3 %collective-permute-done.24.refs_14_ = bf16[64,2048]{1,0:T(8,128)(2,1)S(1)} collective-permute-done((bf16[64,2048]{1,0:T(8,128)(2,1)S(1)}, bf16[64,2048]{1,0:T(8,128)(2,1)S(1)}, u32[]{:S(2)}, u32[]{:S(2)}) %collective-permute-start.24) | collective-permute-done | bytes 262176 | tf_op jit(solution)/shard_map/ppermute | solution.py:364
  116.5 5.0 %collective-permute-done.25.refs_15_ = bf16[64,2048]{1,0:T(8,128)(2,1)S(1)} collective-permute-done((bf16[64,2048]{1,0:T(8,128)(2,1)S(1)}, bf16[64,2048]{1,0:T(8,128)(2,1)S(1)}, u32[]{:S(2)}, u32[]{:S(2)}) %collective-permute-start.25) | collective-permute-done | bytes 262176 | tf_op jit(solution)/shard_map/ppermute | solution.py:364
  121.5 3.0 %gate_up.1.refs_0_ = bf16[2,256,256]{2,1,0:T(8,128)(2,1)S(1)} custom-call(s32[4]{0:T(128)S(1)} %pad_add_fusion.place, bf16[64,2048]{1,0:T(8,128)(2,1)S(1)} %get-tuple-element.45.refs_0_, bf16[64,2048]{1,0:T(8,128)(2,1)S(1)} %collective-permute-done.12.refs_1_, bf16[64,2048]{1,0:T(8,128)(2,1)S(1)} %collective-permute-done.13.refs_2_, ...), custom_call_target="tpu_custom_call" | custom-call | tf_op jit(solution)/shard_map/gate_up/pallas_call | solution.py:307
  124.7 2.0 %collective-permute-start.27 = (bf16[2,256,256]{2,1,0:T(8,128)(2,1)S(1)}, bf16[2,256,256]{2,1,0:T(8,128)(2,1)S(1)}, u32[]{:S(2)}, u32[]{:S(2)}) collective-permute-start(bf16[2,256,256]{2,1,0:T(8,128)(2,1)S(1)} %gate_up.1.refs_0_), channel_id=1, source_target_pairs={{0,2},{1,3},{2,0},{3,1},{4,6},{5,7},{6,4},{7,5},{8,10},{9,11},{10,... | collective-permute-start | bytes 786440 | tf_op jit(solution)/shard_map/ppermute | solution.py:354
  126.7 13.3 %collective-permute-done.26.refs_1_ = bf16[2,256,256]{2,1,0:T(8,128)(2,1)S(1)} collective-permute-done((bf16[2,256,256]{2,1,0:T(8,128)(2,1)S(1)}, bf16[2,256,256]{2,1,0:T(8,128)(2,1)S(1)}, u32[]{:S(2)}, u32[]{:S(2)}) %collective-permute-start.26) | collective-permute-done | bytes 262176 | tf_op jit(solution)/shard_map/ppermute | solution.py:354
  140.6 4.4 %collective-permute-done.27.refs_2_ = bf16[2,256,256]{2,1,0:T(8,128)(2,1)S(1)} collective-permute-done((bf16[2,256,256]{2,1,0:T(8,128)(2,1)S(1)}, bf16[2,256,256]{2,1,0:T(8,128)(2,1)S(1)}, u32[]{:S(2)}, u32[]{:S(2)}) %collective-permute-start.27) | collective-permute-done | bytes 262176 | tf_op jit(solution)/shard_map/ppermute | solution.py:354
  145.0 3.4 %collective-permute-done.28.refs_3_ = bf16[2,256,256]{2,1,0:T(8,128)(2,1)S(1)} collective-permute-done((bf16[2,256,256]{2,1,0:T(8,128)(2,1)S(1)}, bf16[2,256,256]{2,1,0:T(8,128)(2,1)S(1)}, u32[]{:S(2)}, u32[]{:S(2)}) %collective-permute-start.28) | collective-permute-done | bytes 262176 | tf_op jit(solution)/shard_map/ppermute | solution.py:354
  148.5 2.3 %down.1 = bf16[32,16,1024]{2,1,0:T(8,128)(2,1)} custom-call(bf16[2,256,256]{2,1,0:T(8,128)(2,1)S(1)} %gate_up.1.refs_0_, bf16[2,256,256]{2,1,0:T(8,128)(2,1)S(1)} %collective-permute-done.26.refs_1_, bf16[2,256,256]{2,1,0:T(8,128)(2,1)S(1)} %collective-permute-done.27.refs_2_, bf16[2,256,256]{2,1,0:T(8,128)(2,1)S(1)} %collective-permute-done.28.refs_3_, ...), custom_call_target="tpu_custom_call" | custom-call | tf_op jit(solution)/shard_map/down/pallas_call | solution.py:330
  150.7 4.5 %all-to-all-start = ((bf16[32,16,1024]{2,1,0:T(8,128)(2,1)}), bf16[32,16,1024]{2,1,0:T(8,128)(2,1)S(1)}, u32[]{:S(2)}, u32[]{:S(2)}) async-start(bf16[32,16,1024]{2,1,0:T(8,128)(2,1)} %down.1), calls=%async_computation | async-start | bytes 2097152 | tf_op jit(solution)/shard_map/all_to_all | solution.py:429
  156.0 16.4 %all-to-all-done = bf16[32,16,1024]{2,1,0:T(8,128)(2,1)S(1)} async-done(((bf16[32,16,1024]{2,1,0:T(8,128)(2,1)}), bf16[32,16,1024]{2,1,0:T(8,128)(2,1)S(1)}, u32[]{:S(2)}, u32[]{:S(2)}) %all-to-all-start) | async-done | bytes 1048608 | tf_op jit(solution)/shard_map/all_to_all | solution.py:429
  (61 shorter events, 16.9 us)
Async XLA Ops:
  14.0 10.8 %collective-permute-start = (bf16[32,1024]{1,0:T(8,128)(2,1)S(1)}, bf16[32,1024]{1,0:T(8,128)(2,1)S(1)}, u32[]{:S(2)}, u32[]{:S(2)}) collective-permute-start(bf16[32,1024]{1,0:T(8,128)(2,1)S(1)} %get-tuple-element.37), channel_id=1, source_target_pairs={{0,1},{1,2},{2,3},{3,0},{4,5},{5,6},{6,7},{7,4},{8,9},{9,10},{10,1... | collective-permute-start | bytes 196616 | tf_op jit(solution)/shard_map/ppermute | solution.py:354
  16.1 8.7 %collective-permute-start.1 = (bf16[32,1024]{1,0:T(8,128)(2,1)S(1)}, bf16[32,1024]{1,0:T(8,128)(2,1)S(1)}, u32[]{:S(2)}, u32[]{:S(2)}) collective-permute-start(bf16[32,1024]{1,0:T(8,128)(2,1)S(1)} %get-tuple-element.38), channel_id=1, source_target_pairs={{0,2},{1,3},{2,0},{3,1},{4,6},{5,7},{6,4},{7,5},{8,10},{9,11},{10,... | collective-permute-start | bytes 196616 | tf_op jit(solution)/shard_map/ppermute | solution.py:354
  19.7 5.1 %collective-permute-start.2 = (bf16[32,1024]{1,0:T(8,128)(2,1)S(1)}, bf16[32,1024]{1,0:T(8,128)(2,1)S(1)}, u32[]{:S(2)}, u32[]{:S(2)}) collective-permute-start(bf16[32,1024]{1,0:T(8,128)(2,1)S(1)} %get-tuple-element.39), channel_id=1, source_target_pairs={{0,3},{1,0},{2,1},{3,2},{4,7},{5,4},{6,5},{7,6},{8,11},{9,8},{10,9... | collective-permute-start | bytes 196616 | tf_op jit(solution)/shard_map/ppermute | solution.py:354
  25.7 5.5 %collective-permute-start.3 = (bf16[32,1024]{1,0:T(8,128)(2,1)S(1)}, bf16[32,1024]{1,0:T(8,128)(2,1)S(1)}, u32[]{:S(2)}, u32[]{:S(2)}) collective-permute-start(bf16[32,1024]{1,0:T(8,128)(2,1)S(1)} %get-tuple-element.67), channel_id=1, source_target_pairs={{0,1},{1,2},{2,3},{3,0},{4,5},{5,6},{6,7},{7,4},{8,9},{9,10},{10,1... | collective-permute-start | bytes 196616 | tf_op jit(solution)/shard_map/ppermute | solution.py:354
  26.8 5.8 %collective-permute-start.4 = (bf16[32,1024]{1,0:T(8,128)(2,1)S(1)}, bf16[32,1024]{1,0:T(8,128)(2,1)S(1)}, u32[]{:S(2)}, u32[]{:S(2)}) collective-permute-start(bf16[32,1024]{1,0:T(8,128)(2,1)S(1)} %get-tuple-element.67), channel_id=1, source_target_pairs={{0,2},{1,3},{2,0},{3,1},{4,6},{5,7},{6,4},{7,5},{8,10},{9,11},{10,... | collective-permute-start | bytes 196616 | tf_op jit(solution)/shard_map/ppermute | solution.py:354
  33.6 10.0 %collective-permute-start.10 = (bf16[40,2048]{1,0:T(8,128)(2,1)S(1)}, bf16[40,2048]{1,0:T(8,128)(2,1)S(1)}, u32[]{:S(2)}, u32[]{:S(2)}) collective-permute-start(bf16[40,2048]{1,0:T(8,128)(2,1)S(1)} %get-tuple-element.44.refs_4_), channel_id=1, source_target_pairs={{0,64},{4,68},{8,72},{12,76},{16,80},{20,84},{24,88},{28,92},{32,9... | collective-permute-start | bytes 491528 | tf_op jit(solution)/shard_map/ppermute | solution.py:364
  36.9 7.7 %collective-permute-start.11 = (bf16[40,2048]{1,0:T(8,128)(2,1)S(1)}, bf16[40,2048]{1,0:T(8,128)(2,1)S(1)}, u32[]{:S(2)}, u32[]{:S(2)}) collective-permute-start(bf16[40,2048]{1,0:T(8,128)(2,1)S(1)} %get-tuple-element.44.refs_4_), channel_id=1, source_target_pairs={{0,96},{4,100},{8,104},{12,108},{16,112},{20,116},{24,120},{28,124... | collective-permute-start | bytes 491528 | tf_op jit(solution)/shard_map/ppermute | solution.py:364
  37.9 7.3 %collective-permute-start.6 = (bf16[40,2048]{1,0:T(8,128)(2,1)S(1)}, bf16[40,2048]{1,0:T(8,128)(2,1)S(1)}, u32[]{:S(2)}, u32[]{:S(2)}) collective-permute-start(bf16[40,2048]{1,0:T(8,128)(2,1)S(1)} %get-tuple-element.43.refs_0_), channel_id=1, source_target_pairs={{0,8},{4,12},{8,16},{12,20},{16,24},{20,28},{24,0},{28,4},{32,40},... | collective-permute-start | bytes 491528 | tf_op jit(solution)/shard_map/ppermute | solution.py:364
  39.4 7.8 %collective-permute-start.7 = (bf16[40,2048]{1,0:T(8,128)(2,1)S(1)}, bf16[40,2048]{1,0:T(8,128)(2,1)S(1)}, u32[]{:S(2)}, u32[]{:S(2)}) collective-permute-start(bf16[40,2048]{1,0:T(8,128)(2,1)S(1)} %get-tuple-element.43.refs_0_), channel_id=1, source_target_pairs={{0,16},{4,20},{8,24},{12,28},{16,0},{20,4},{24,8},{28,12},{32,48},... | collective-permute-start | bytes 491528 | tf_op jit(solution)/shard_map/ppermute | solution.py:364
  42.1 5.3 %collective-permute-start.8 = (bf16[40,2048]{1,0:T(8,128)(2,1)S(1)}, bf16[40,2048]{1,0:T(8,128)(2,1)S(1)}, u32[]{:S(2)}, u32[]{:S(2)}) collective-permute-start(bf16[40,2048]{1,0:T(8,128)(2,1)S(1)} %get-tuple-element.43.refs_0_), channel_id=1, source_target_pairs={{0,24},{4,28},{8,0},{12,4},{16,8},{20,12},{24,16},{28,20},{32,56},... | collective-permute-start | bytes 491528 | tf_op jit(solution)/shard_map/ppermute | solution.py:364
  43.6 6.5 %collective-permute-start.9 = (bf16[40,2048]{1,0:T(8,128)(2,1)S(1)}, bf16[40,2048]{1,0:T(8,128)(2,1)S(1)}, u32[]{:S(2)}, u32[]{:S(2)}) collective-permute-start(bf16[40,2048]{1,0:T(8,128)(2,1)S(1)} %get-tuple-element.44.refs_4_), channel_id=1, source_target_pairs={{0,32},{4,36},{8,40},{12,44},{16,48},{20,52},{24,56},{28,60},{32,6... | collective-permute-start | bytes 491528 | tf_op jit(solution)/shard_map/ppermute | solution.py:364
  52.4 4.6 %collective-permute-start.12 = (bf16[64,2048]{1,0:T(8,128)(2,1)S(1)}, bf16[64,2048]{1,0:T(8,128)(2,1)S(1)}, u32[]{:S(2)}, u32[]{:S(2)}) collective-permute-start(bf16[64,2048]{1,0:T(8,128)(2,1)S(1)} %get-tuple-element.46), channel_id=1, source_target_pairs={{0,4},{4,0},{8,12},{12,8},{16,20},{20,16},{24,28},{28,24},{32,36},... | collective-permute-start | bytes 786440 | tf_op jit(solution)/shard_map/ppermute | solution.py:364
  52.5 10.5 %collective-permute-start.13 = (bf16[64,2048]{1,0:T(8,128)(2,1)S(1)}, bf16[64,2048]{1,0:T(8,128)(2,1)S(1)}, u32[]{:S(2)}, u32[]{:S(2)}) collective-permute-start(bf16[64,2048]{1,0:T(8,128)(2,1)S(1)} %get-tuple-element.47), channel_id=1, source_target_pairs={{0,32},{4,36},{8,40},{12,44},{16,48},{20,52},{24,56},{28,60},{32,6... | collective-permute-start | bytes 786440 | tf_op jit(solution)/shard_map/ppermute | solution.py:364
  52.6 26.1 %collective-permute-start.14 = (bf16[64,2048]{1,0:T(8,128)(2,1)S(1)}, bf16[64,2048]{1,0:T(8,128)(2,1)S(1)}, u32[]{:S(2)}, u32[]{:S(2)}) collective-permute-start(bf16[64,2048]{1,0:T(8,128)(2,1)S(1)} %get-tuple-element.48), channel_id=1, source_target_pairs={{0,36},{4,32},{8,44},{12,40},{16,52},{20,48},{24,60},{28,56},{32,6... | collective-permute-start | bytes 786440 | tf_op jit(solution)/shard_map/ppermute | solution.py:364
  52.8 26.3 %collective-permute-start.15 = (bf16[64,2048]{1,0:T(8,128)(2,1)S(1)}, bf16[64,2048]{1,0:T(8,128)(2,1)S(1)}, u32[]{:S(2)}, u32[]{:S(2)}) collective-permute-start(bf16[64,2048]{1,0:T(8,128)(2,1)S(1)} %get-tuple-element.49), channel_id=1, source_target_pairs={{0,64},{4,68},{8,72},{12,76},{16,80},{20,84},{24,88},{28,92},{32,9... | collective-permute-start | bytes 786440 | tf_op jit(solution)/shard_map/ppermute | solution.py:364
  57.0 22.7 %collective-permute-start.16 = (bf16[64,2048]{1,0:T(8,128)(2,1)S(1)}, bf16[64,2048]{1,0:T(8,128)(2,1)S(1)}, u32[]{:S(2)}, u32[]{:S(2)}) collective-permute-start(bf16[64,2048]{1,0:T(8,128)(2,1)S(1)} %get-tuple-element.50), channel_id=1, source_target_pairs={{0,68},{4,64},{8,76},{12,72},{16,84},{20,80},{24,92},{28,88},{32,1... | collective-permute-start | bytes 786440 | tf_op jit(solution)/shard_map/ppermute | solution.py:364
  57.0 22.7 %collective-permute-start.17 = (bf16[64,2048]{1,0:T(8,128)(2,1)S(1)}, bf16[64,2048]{1,0:T(8,128)(2,1)S(1)}, u32[]{:S(2)}, u32[]{:S(2)}) collective-permute-start(bf16[64,2048]{1,0:T(8,128)(2,1)S(1)} %get-tuple-element.51), channel_id=1, source_target_pairs={{0,96},{4,100},{8,104},{12,108},{16,112},{20,116},{24,120},{28,124... | collective-permute-start | bytes 786440 | tf_op jit(solution)/shard_map/ppermute | solution.py:364
  63.0 20.3 %collective-permute-start.18 = (bf16[64,2048]{1,0:T(8,128)(2,1)S(1)}, bf16[64,2048]{1,0:T(8,128)(2,1)S(1)}, u32[]{:S(2)}, u32[]{:S(2)}) collective-permute-start(bf16[64,2048]{1,0:T(8,128)(2,1)S(1)} %get-tuple-element.52), channel_id=1, source_target_pairs={{0,100},{4,96},{8,108},{12,104},{16,116},{20,112},{24,124},{28,120... | collective-permute-start | bytes 786440 | tf_op jit(solution)/shard_map/ppermute | solution.py:364
  78.7 4.9 %collective-permute-start.19 = (bf16[64,2048]{1,0:T(8,128)(2,1)S(1)}, bf16[64,2048]{1,0:T(8,128)(2,1)S(1)}, u32[]{:S(2)}, u32[]{:S(2)}) collective-permute-start(bf16[64,2048]{1,0:T(8,128)(2,1)S(1)} %get-tuple-element.54), channel_id=1, source_target_pairs={{0,4},{4,0},{8,12},{12,8},{16,20},{20,16},{24,28},{28,24},{32,36},... | collective-permute-start | bytes 786440 | tf_op jit(solution)/shard_map/ppermute | solution.py:364
  79.1 10.4 %collective-permute-start.20 = (bf16[64,2048]{1,0:T(8,128)(2,1)S(1)}, bf16[64,2048]{1,0:T(8,128)(2,1)S(1)}, u32[]{:S(2)}, u32[]{:S(2)}) collective-permute-start(bf16[64,2048]{1,0:T(8,128)(2,1)S(1)} %get-tuple-element.55), channel_id=1, source_target_pairs={{0,8},{4,12},{8,16},{12,20},{16,24},{20,28},{24,0},{28,4},{32,40},... | collective-permute-start | bytes 786440 | tf_op jit(solution)/shard_map/ppermute | solution.py:364
  79.7 25.0 %collective-permute-start.21 = (bf16[64,2048]{1,0:T(8,128)(2,1)S(1)}, bf16[64,2048]{1,0:T(8,128)(2,1)S(1)}, u32[]{:S(2)}, u32[]{:S(2)}) collective-permute-start(bf16[64,2048]{1,0:T(8,128)(2,1)S(1)} %get-tuple-element.56), channel_id=1, source_target_pairs={{0,12},{4,8},{8,20},{12,16},{16,28},{20,24},{24,4},{28,0},{32,44},... | collective-permute-start | bytes 786440 | tf_op jit(solution)/shard_map/ppermute | solution.py:364
  79.7 27.6 %collective-permute-start.22 = (bf16[64,2048]{1,0:T(8,128)(2,1)S(1)}, bf16[64,2048]{1,0:T(8,128)(2,1)S(1)}, u32[]{:S(2)}, u32[]{:S(2)}) collective-permute-start(bf16[64,2048]{1,0:T(8,128)(2,1)S(1)} %get-tuple-element.57), channel_id=1, source_target_pairs={{0,16},{4,20},{8,24},{12,28},{16,0},{20,4},{24,8},{28,12},{32,48},... | collective-permute-start | bytes 786440 | tf_op jit(solution)/shard_map/ppermute | solution.py:364
  83.3 24.4 %collective-permute-start.23 = (bf16[64,2048]{1,0:T(8,128)(2,1)S(1)}, bf16[64,2048]{1,0:T(8,128)(2,1)S(1)}, u32[]{:S(2)}, u32[]{:S(2)}) collective-permute-start(bf16[64,2048]{1,0:T(8,128)(2,1)S(1)} %get-tuple-element.58), channel_id=1, source_target_pairs={{0,20},{4,16},{8,28},{12,24},{16,4},{20,0},{24,12},{28,8},{32,52},... | collective-permute-start | bytes 786440 | tf_op jit(solution)/shard_map/ppermute | solution.py:364
  83.6 64.8 %collective-permute-start.29 = (bf16[2,256,1024]{2,1,0:T(8,128)(2,1)}, bf16[2,256,1024]{2,1,0:T(8,128)(2,1)S(1)}, u32[]{:S(2)}, u32[]{:S(2)}) collective-permute-start(bf16[2,256,1024]{2,1,0:T(8,128)(2,1)} %get-tuple-element.64), channel_id=1, source_target_pairs={{0,1},{1,2},{2,3},{3,0},{4,5},{5,6},{6,7},{7,4},{8,9},{9,10},{10,1... | collective-permute-start | bytes 3145736 | tf_op jit(solution)/shard_map/ppermute | solution.py:354
  89.5 59.0 %collective-permute-start.30 = (bf16[2,256,1024]{2,1,0:T(8,128)(2,1)}, bf16[2,256,1024]{2,1,0:T(8,128)(2,1)S(1)}, u32[]{:S(2)}, u32[]{:S(2)}) collective-permute-start(bf16[2,256,1024]{2,1,0:T(8,128)(2,1)} %get-tuple-element.65), channel_id=1, source_target_pairs={{0,2},{1,3},{2,0},{3,1},{4,6},{5,7},{6,4},{7,5},{8,10},{9,11},{10,... | collective-permute-start | bytes 3145736 | tf_op jit(solution)/shard_map/ppermute | solution.py:354
  104.7 43.8 %collective-permute-start.31 = (bf16[2,256,1024]{2,1,0:T(8,128)(2,1)S(1)}, bf16[2,256,1024]{2,1,0:T(8,128)(2,1)S(1)}, u32[]{:S(2)}, u32[]{:S(2)}) collective-permute-start(bf16[2,256,1024]{2,1,0:T(8,128)(2,1)S(1)} %get-tuple-element.66), channel_id=1, source_target_pairs={{0,3},{1,0},{2,1},{3,2},{4,7},{5,4},{6,5},{7,6},{8,11},{9,8},{10,9... | collective-permute-start | bytes 3145736 | tf_op jit(solution)/shard_map/ppermute | solution.py:354
  107.3 9.2 %collective-permute-start.24 = (bf16[64,2048]{1,0:T(8,128)(2,1)S(1)}, bf16[64,2048]{1,0:T(8,128)(2,1)S(1)}, u32[]{:S(2)}, u32[]{:S(2)}) collective-permute-start(bf16[64,2048]{1,0:T(8,128)(2,1)S(1)} %get-tuple-element.59), channel_id=1, source_target_pairs={{0,24},{4,28},{8,0},{12,4},{16,8},{20,12},{24,16},{28,20},{32,56},... | collective-permute-start | bytes 786440 | tf_op jit(solution)/shard_map/ppermute | solution.py:364
  107.7 13.8 %collective-permute-start.25 = (bf16[64,2048]{1,0:T(8,128)(2,1)S(1)}, bf16[64,2048]{1,0:T(8,128)(2,1)S(1)}, u32[]{:S(2)}, u32[]{:S(2)}) collective-permute-start(bf16[64,2048]{1,0:T(8,128)(2,1)S(1)} %get-tuple-element.60), channel_id=1, source_target_pairs={{0,28},{4,24},{8,4},{12,0},{16,12},{20,8},{24,20},{28,16},{32,60},... | collective-permute-start | bytes 786440 | tf_op jit(solution)/shard_map/ppermute | solution.py:364
  124.6 15.4 %collective-permute-start.26 = (bf16[2,256,256]{2,1,0:T(8,128)(2,1)S(1)}, bf16[2,256,256]{2,1,0:T(8,128)(2,1)S(1)}, u32[]{:S(2)}, u32[]{:S(2)}) collective-permute-start(bf16[2,256,256]{2,1,0:T(8,128)(2,1)S(1)} %gate_up.1.refs_0_), channel_id=1, source_target_pairs={{0,1},{1,2},{2,3},{3,0},{4,5},{5,6},{6,7},{7,4},{8,9},{9,10},{10,1... | collective-permute-start | bytes 786440 | tf_op jit(solution)/shard_map/ppermute | solution.py:354
  124.7 20.3 %collective-permute-start.27 = (bf16[2,256,256]{2,1,0:T(8,128)(2,1)S(1)}, bf16[2,256,256]{2,1,0:T(8,128)(2,1)S(1)}, u32[]{:S(2)}, u32[]{:S(2)}) collective-permute-start(bf16[2,256,256]{2,1,0:T(8,128)(2,1)S(1)} %gate_up.1.refs_0_), channel_id=1, source_target_pairs={{0,2},{1,3},{2,0},{3,1},{4,6},{5,7},{6,4},{7,5},{8,10},{9,11},{10,... | collective-permute-start | bytes 786440 | tf_op jit(solution)/shard_map/ppermute | solution.py:354
  140.0 8.5 %collective-permute-start.28 = (bf16[2,256,256]{2,1,0:T(8,128)(2,1)S(1)}, bf16[2,256,256]{2,1,0:T(8,128)(2,1)S(1)}, u32[]{:S(2)}, u32[]{:S(2)}) collective-permute-start(bf16[2,256,256]{2,1,0:T(8,128)(2,1)S(1)} %gate_up.1.refs_0_), channel_id=1, source_target_pairs={{0,3},{1,0},{2,1},{3,2},{4,7},{5,4},{6,5},{7,6},{8,11},{9,8},{10,9... | collective-permute-start | bytes 786440 | tf_op jit(solution)/shard_map/ppermute | solution.py:354
  150.7 21.7 %all-to-all-start = ((bf16[32,16,1024]{2,1,0:T(8,128)(2,1)}), bf16[32,16,1024]{2,1,0:T(8,128)(2,1)S(1)}, u32[]{:S(2)}, u32[]{:S(2)}) async-start(bf16[32,16,1024]{2,1,0:T(8,128)(2,1)} %down.1), calls=%async_computation | async-start | bytes 2097152 | tf_op jit(solution)/shard_map/all_to_all | solution.py:429
  (4 other events, 56.5 us)
where the time goes:
time: 175 us; the launch traced here: 174 us
  waiting for transfers between devices  94.5 us (54%)
  starting transfers between devices  46.2 us (26%)
  Pallas kernels  25.7 us (15%)
  local copies, waits for them, and re-layouts  4.56 us (3%)
    ppermute x20, waiting for transfers between devices, moved_in_plane(): return lax.ppermute(value, 'pool', pairs)  53.7 us
    ppermute x12, waiting for transfers between devices, turned(): lax.ppermute(value, 'head', [(i, (i + step) % groups) for i in range(grou...  24.3 us
    ppermute x20, starting transfers between devices, moved_in_plane(): return lax.ppermute(value, 'pool', pairs)  22.6 us
    ppermute x12, starting transfers between devices, turned(): lax.ppermute(value, 'head', [(i, (i + step) % groups) for i in range(grou...  19 us
    all_to_all x1, waiting for transfers between devices, body(): lax.all_to_all(produced, 'pool', split_axis=0, concat_axis=0, tiled=True)  16.4 us
    pallas_call x1, Pallas kernels, attend_project(): pl.pallas_call(attend_kernel, out_shape=[jax.ShapeDtypeStruct((rows, shar...  13.9 us
    all_to_all x1, starting transfers between devices, body(): lax.all_to_all(produced, 'pool', split_axis=0, concat_axis=0, tiled=True)  4.53 us
    dynamic_slice x1, local copies, waits for them, and re-layouts, body(): lax.dynamic_slice_in_dim(w_down, lax.rem(head + step, groups) * share, sh...  4.12 us
  transfers between devices with their start and end apart: 33, of which 17 were waited for; matrix products, arithmetic and copies ran while one was open for 3% of the time, Pallas kernels for 4%

commit v1 on v0

--- a/solution.py
+++ b/solution.py
@@ -10,7 +10,8 @@
 BF16 = jnp.bfloat16
 GROUP = 8
 HEAD, ROW, COLUMN, CORE = range(4)
-FAR_ORDER = ((2, 0), (2, 1), (1, 0), (3, 0), (1, 1), (3, 1), (0, 1))
+NEAR_ORDER = (2, 1, 3, 0)
+FAR_ORDER = ((2, 0), (2, 1), (1, 0), (3, 0), (1, 1), (3, 1), (0, 1), (0, 0))
 
 
 def attend_kernel(lengths, place, q_ref, k_ref, v_ref, nk_ref, nv_ref, proj_hbm, *outs):
@@ -196,7 +197,7 @@
     earlier = ((upper_line < upper_lane) & ((upper_line >> 5) == (upper_lane >> 5))).astype(F32)
     id_lane = lax.broadcasted_iota(jnp.int32, (8, lanes), 1) >> 5
     for half in range(2):
-        ins = refs[half * near : (half + 1) * near]
+        ins = [refs[2 * NEAR_ORDER.index(back) + half] for back in range(near)]
         outs = refs[(2 + 2 * half) * near : (4 + 2 * half) * near]
         if half == 0:
             target = ((pools[0] + step) & 3) * 8 + pools[1] * 2 + core
@@ -230,7 +231,7 @@
         out_specs=[vmem] * 16,
         compiler_params=pltpu.CompilerParams(vmem_limit_bytes=16 << 20),
         name="pick_rows",
-    )(place, *in_vmem([*first, *second]))
+    )(place, *in_vmem([part[back] for back in NEAR_ORDER for part in (first, second)]))
     return out[:8], out[8:]
 
 
@@ -261,7 +262,9 @@
 
 
 def gate_up_kernel(place, *refs):
-    first, second = refs[:8], refs[8:16]
+    first, second = [None] * 8, [None] * 8
+    for i, (step, flip) in enumerate(FAR_ORDER):
+        first[step * 2 + flip], second[step * 2 + flip] = refs[2 * i : 2 * i + 2]
     gate_ref, up_ref, act_ref, sum_ref = refs[16:]
     experts, width, units = gate_ref.shape
     share = first[0].shape[1] // 2
@@ -312,7 +315,7 @@
         scratch_shapes=[pltpu.VMEM((2, pools, capacity, units), F32)],
         compiler_params=pltpu.CompilerParams(vmem_limit_bytes=12 << 20),
         name="gate_up",
-    )(place, *in_vmem([*first, *second, w_gate, w_up]))
+    )(place, *in_vmem([part[step * 2 + flip] for step, flip in FAR_ORDER for part in (first, second)]), *in_vmem([w_gate, w_up]))
 
 
 def down_kernel(*refs):
@@ -418,7 +421,7 @@
     for_y, for_x = pick_rows(along_x, along_y, place)
     ways = [(step, flip) for step in range(4) for flip in range(2)]
     from_y, from_x = list(for_y), list(for_x)
-    for step, flip in FAR_ORDER:
+    for step, flip in FAR_ORDER[:-1]:
         way = ways.index((step, flip))
         from_y[way] = moved_in_plane(for_y[way], step, 0, flip)
         from_x[way] = moved_in_plane(for_x[way], 0, step, flip)
@@ -451,6 +454,4 @@
         P("pool", None, "head"),
         P("pool", "head", None),
     )
-    return jax.shard_map(
-        body, mesh=mesh, in_specs=placed, out_specs=P("pool", "head"), check_vma=False
-    )
+    return jax.shard_map(body, mesh=mesh, in_specs=placed, out_specs=P("pool", "head"), check_vma=False)

time: 175 us -> 164 us (0.937)
  waiting for transfers between devices: 94.5 us -> 80.2 us
  starting transfers between devices: 46.2 us -> 49.8 us
    ppermute x20, waiting for transfers between devices: 53.7 us -> 16.8 us  [moved_in_plane(): return lax.ppermute(value, 'pool', pairs)]
    ppermute x12, waiting for transfers between devices: 24.3 us -> 47 us  [turned(): lax.ppermute(value, 'head', [(i, (i + step) % groups) for i in range(grou...]
    ppermute x20, starting transfers between devices: 22.6 us -> 25.1 us  [moved_in_plane(): return lax.ppermute(value, 'pool', pairs)]
  transfers between devices with their start and end apart: 33 -> 33, of which waited for: 17 -> 18; matrix products, arithmetic and copies ran while one was open for 3% -> 3% of each run, Pallas kernels for 4% -> 4%
where the time goes in v1:
time: 164 us; the launch traced here: 163 us
  waiting for transfers between devices  80.2 us (49%)
  starting transfers between devices  49.8 us (30%)
  Pallas kernels  25.8 us (16%)
  local copies, waits for them, and re-layouts  4.56 us (3%)
    ppermute x12, waiting for transfers between devices, turned(): lax.ppermute(value, 'head', [(i, (i + step) % groups) for i in range(grou...  47 us
    ppermute x20, starting transfers between devices, moved_in_plane(): return lax.ppermute(value, 'pool', pairs)  25.1 us
    ppermute x12, starting transfers between devices, turned(): lax.ppermute(value, 'head', [(i, (i + step) % groups) for i in range(grou...  19.8 us
    ppermute x20, waiting for transfers between devices, moved_in_plane(): return lax.ppermute(value, 'pool', pairs)  16.8 us
    all_to_all x1, waiting for transfers between devices, body(): lax.all_to_all(produced, 'pool', split_axis=0, concat_axis=0, tiled=True)  16.4 us
    pallas_call x1, Pallas kernels, attend_project(): pl.pallas_call(attend_kernel, out_shape=[jax.ShapeDtypeStruct((rows, shar...  13.9 us
    all_to_all x1, starting transfers between devices, body(): lax.all_to_all(produced, 'pool', split_axis=0, concat_axis=0, tiled=True)  4.91 us
    dynamic_slice x1, local copies, waits for them, and re-layouts, body(): lax.dynamic_slice_in_dim(w_down, lax.rem(head + step, groups) * share, sh...  4.12 us
  transfers between devices with their start and end apart: 33, of which 18 were waited for; matrix products, arithmetic and copies ran while one was open for 3% of the time, Pallas kernels for 4%

profile of v1, /device:TPU:0, one launch (start us, length us, event | category | flops | bytes accessed | tf_op | source)
XLA Modules:
  0.0 163.1 jit_solution(10240328354553968536)
XLA Ops:
  0.1 13.9 %attend_project.1 = (f32[32,1024]{1,0:T(8,128)S(1)}, bf16[32,1024]{1,0:T(8,128)(2,1)S(1)}, bf16[32,1024]{1,0:T(8,128)(2,1)S(1)}, bf16[32,1024]{1,0:T(8,128)(2,1)S(1)}) custom-call(s32[32]{0:T(128)} %lengths.1, s32[4]{0:T(128)S(1)} %pad_add_fusion.place, bf16[32,1024]{1,0:T(8,128)(2,1)} %q_ref.1, bf16[32,1,512,128]{3,2,1,0:T(8,128)(2,1)} %k_ref.1, ...), custom_call_target="tpu_custom_call" | custom-call | tf_op jit(solution)/shard_map/attend_project/pallas_call | solution.py:109
  14.0 2.1 %collective-permute-start = (bf16[32,1024]{1,0:T(8,128)(2,1)S(1)}, bf16[32,1024]{1,0:T(8,128)(2,1)S(1)}, u32[]{:S(2)}, u32[]{:S(2)}) collective-permute-start(bf16[32,1024]{1,0:T(8,128)(2,1)S(1)} %get-tuple-element.37), channel_id=1, source_target_pairs={{0,1},{1,2},{2,3},{3,0},{4,5},{5,6},{6,7},{7,4},{8,9},{9,10},{10,1... | collective-permute-start | bytes 196616 | tf_op jit(solution)/shard_map/ppermute | solution.py:357
  16.1 3.6 %collective-permute-start.1 = (bf16[32,1024]{1,0:T(8,128)(2,1)S(1)}, bf16[32,1024]{1,0:T(8,128)(2,1)S(1)}, u32[]{:S(2)}, u32[]{:S(2)}) collective-permute-start(bf16[32,1024]{1,0:T(8,128)(2,1)S(1)} %get-tuple-element.38), channel_id=1, source_target_pairs={{0,2},{1,3},{2,0},{3,1},{4,6},{5,7},{6,4},{7,5},{8,10},{9,11},{10,... | collective-permute-start | bytes 196616 | tf_op jit(solution)/shard_map/ppermute | solution.py:357
  20.7 4.1 %constant_dynamic-slice_fusion = (bf16[2,256,1024]{2,1,0:T(8,128)(2,1)S(1)}, bf16[2,256,1024]{2,1,0:T(8,128)(2,1)}, bf16[2,256,1024]{2,1,0:T(8,128)(2,1)S(1)}, bf16[2,256,1024]{2,1,0:T(8,128)(2,1)}) fusion(bf16[2,256,4096]{2,1,0:T(8,128)(2,1)} %param.27, s32[]{:T(128)S(6)} %select_n.23, s32[]{:T(128)S(6)} %select_n.21, s32[]{:T(128)S(6)} %select_n.20, ...), kind=kLoop, calls=%fused_computation.15 | loop fusion | bytes 8388624 | tf_op jit(solution)/shard_map/dynamic_slice | solution.py:409
  26.8 1.8 %collective-permute-start.4 = (bf16[32,1024]{1,0:T(8,128)(2,1)S(1)}, bf16[32,1024]{1,0:T(8,128)(2,1)S(1)}, u32[]{:S(2)}, u32[]{:S(2)}) collective-permute-start(bf16[32,1024]{1,0:T(8,128)(2,1)S(1)} %get-tuple-element.67), channel_id=1, source_target_pairs={{0,2},{1,3},{2,0},{3,1},{4,6},{5,7},{6,4},{7,5},{8,10},{9,11},{10,... | collective-permute-start | bytes 196616 | tf_op jit(solution)/shard_map/ppermute | solution.py:357
  29.7 1.6 collective-permute-done.3.refs_0_
  33.6 2.8 %collective-permute-start.10 = (bf16[40,2048]{1,0:T(8,128)(2,1)S(1)}, bf16[40,2048]{1,0:T(8,128)(2,1)S(1)}, u32[]{:S(2)}, u32[]{:S(2)}) collective-permute-start(bf16[40,2048]{1,0:T(8,128)(2,1)S(1)} %get-tuple-element.43.refs_6_), channel_id=1, source_target_pairs={{0,24},{4,28},{8,0},{12,4},{16,8},{20,12},{24,16},{28,20},{32,56},... | collective-permute-start | bytes 491528 | tf_op jit(solution)/shard_map/ppermute | solution.py:367
  37.2 3.0 %collective-permute-start.11 = (bf16[40,2048]{1,0:T(8,128)(2,1)S(1)}, bf16[40,2048]{1,0:T(8,128)(2,1)S(1)}, u32[]{:S(2)}, u32[]{:S(2)}) collective-permute-start(bf16[40,2048]{1,0:T(8,128)(2,1)S(1)} %get-tuple-element.44.refs_7_), channel_id=1, source_target_pairs={{0,96},{4,100},{8,104},{12,108},{16,112},{20,116},{24,120},{28,124... | collective-permute-start | bytes 491528 | tf_op jit(solution)/shard_map/ppermute | solution.py:367
  43.0 1.9 %collective-permute-done.11.refs_5_ = bf16[40,2048]{1,0:T(8,128)(2,1)S(1)} collective-permute-done((bf16[40,2048]{1,0:T(8,128)(2,1)S(1)}, bf16[40,2048]{1,0:T(8,128)(2,1)S(1)}, u32[]{:S(2)}, u32[]{:S(2)}) %collective-permute-start.11) | collective-permute-done | bytes 163872 | tf_op jit(solution)/shard_map/ppermute | solution.py:367
  44.9 2.2 %collective-permute-done.7.refs_1_ = bf16[40,2048]{1,0:T(8,128)(2,1)S(1)} collective-permute-done((bf16[40,2048]{1,0:T(8,128)(2,1)S(1)}, bf16[40,2048]{1,0:T(8,128)(2,1)S(1)}, u32[]{:S(2)}, u32[]{:S(2)}) %collective-permute-start.7) | collective-permute-done | bytes 163872 | tf_op jit(solution)/shard_map/ppermute | solution.py:367
  48.8 2.3 %pick_rows.1 = (bf16[64,2048]{1,0:T(8,128)(2,1)S(1)}, bf16[64,2048]{1,0:T(8,128)(2,1)S(1)}, bf16[64,2048]{1,0:T(8,128)(2,1)S(1)}, bf16[64,2048]{1,0:T(8,128)(2,1...) custom-call(s32[4]{0:T(128)S(1)} %pad_add_fusion.place, ...), custom_call_target="tpu_custom_call" | custom-call | tf_op jit(solution)/shard_map/pick_rows/pallas_call | solution.py:227
  51.1 1.6 collective-permute-start.12
  52.7 1.9 %collective-permute-start.13 = (bf16[64,2048]{1,0:T(8,128)(2,1)S(1)}, bf16[64,2048]{1,0:T(8,128)(2,1)S(1)}, u32[]{:S(2)}, u32[]{:S(2)}) collective-permute-start(bf16[64,2048]{1,0:T(8,128)(2,1)S(1)} %get-tuple-element.46), channel_id=1, source_target_pairs={{0,16},{4,20},{8,24},{12,28},{16,0},{20,4},{24,8},{28,12},{32,48},... | collective-permute-start | bytes 786440 | tf_op jit(solution)/shard_map/ppermute | solution.py:367
  54.5 3.4 %collective-permute-start.15 = (bf16[64,2048]{1,0:T(8,128)(2,1)S(1)}, bf16[64,2048]{1,0:T(8,128)(2,1)S(1)}, u32[]{:S(2)}, u32[]{:S(2)}) collective-permute-start(bf16[64,2048]{1,0:T(8,128)(2,1)S(1)} %get-tuple-element.48), channel_id=1, source_target_pairs={{0,20},{4,16},{8,28},{12,24},{16,4},{20,0},{24,12},{28,8},{32,52},... | collective-permute-start | bytes 786440 | tf_op jit(solution)/shard_map/ppermute | solution.py:367
  60.3 1.6 collective-permute-done.13.refs_1_
  62.5 2.3 %collective-permute-done.14.refs_2_ = bf16[64,2048]{1,0:T(8,128)(2,1)S(1)} collective-permute-done((bf16[64,2048]{1,0:T(8,128)(2,1)S(1)}, bf16[64,2048]{1,0:T(8,128)(2,1)S(1)}, u32[]{:S(2)}, u32[]{:S(2)}) %collective-permute-start.14) | collective-permute-done | bytes 262176 | tf_op jit(solution)/shard_map/ppermute | solution.py:367
  64.8 2.3 %collective-permute-start.19 = (bf16[64,2048]{1,0:T(8,128)(2,1)S(1)}, bf16[64,2048]{1,0:T(8,128)(2,1)S(1)}, u32[]{:S(2)}, u32[]{:S(2)}) collective-permute-start(bf16[64,2048]{1,0:T(8,128)(2,1)S(1)} %get-tuple-element.52), channel_id=1, source_target_pairs={{0,24},{4,28},{8,0},{12,4},{16,8},{20,12},{24,16},{28,20},{32,56},... | collective-permute-start | bytes 786440 | tf_op jit(solution)/shard_map/ppermute | solution.py:367
  68.1 2.2 %collective-permute-done.16.refs_4_ = bf16[64,2048]{1,0:T(8,128)(2,1)S(1)} collective-permute-done((bf16[64,2048]{1,0:T(8,128)(2,1)S(1)}, bf16[64,2048]{1,0:T(8,128)(2,1)S(1)}, u32[]{:S(2)}, u32[]{:S(2)}) %collective-permute-start.16) | collective-permute-done | bytes 262176 | tf_op jit(solution)/shard_map/ppermute | solution.py:367
  71.8 2.2 %collective-permute-start.23 = (bf16[64,2048]{1,0:T(8,128)(2,1)S(1)}, bf16[64,2048]{1,0:T(8,128)(2,1)S(1)}, u32[]{:S(2)}, u32[]{:S(2)}) collective-permute-start(bf16[64,2048]{1,0:T(8,128)(2,1)S(1)} %get-tuple-element.56), channel_id=1, source_target_pairs={{0,28},{4,24},{8,4},{12,0},{16,12},{20,8},{24,20},{28,16},{32,60},... | collective-permute-start | bytes 786440 | tf_op jit(solution)/shard_map/ppermute | solution.py:367
  76.1 1.7 %collective-permute-start.30 = (bf16[2,256,1024]{2,1,0:T(8,128)(2,1)}, bf16[2,256,1024]{2,1,0:T(8,128)(2,1)S(1)}, u32[]{:S(2)}, u32[]{:S(2)}) collective-permute-start(bf16[2,256,1024]{2,1,0:T(8,128)(2,1)} %get-tuple-element.65), channel_id=1, source_target_pairs={{0,2},{1,3},{2,0},{3,1},{4,6},{5,7},{6,4},{7,5},{8,10},{9,11},{10,... | collective-permute-start | bytes 3145736 | tf_op jit(solution)/shard_map/ppermute | solution.py:357
  77.8 2.1 %collective-permute-done.21.refs_9_ = bf16[64,2048]{1,0:T(8,128)(2,1)S(1)} collective-permute-done((bf16[64,2048]{1,0:T(8,128)(2,1)S(1)}, bf16[64,2048]{1,0:T(8,128)(2,1)S(1)}, u32[]{:S(2)}, u32[]{:S(2)}) %collective-permute-start.21) | collective-permute-done | bytes 262176 | tf_op jit(solution)/shard_map/ppermute | solution.py:367
  79.9 2.7 %collective-permute-start.31 = (bf16[2,256,1024]{2,1,0:T(8,128)(2,1)S(1)}, bf16[2,256,1024]{2,1,0:T(8,128)(2,1)S(1)}, u32[]{:S(2)}, u32[]{:S(2)}) collective-permute-start(bf16[2,256,1024]{2,1,0:T(8,128)(2,1)S(1)} %get-tuple-element.66), channel_id=1, source_target_pairs={{0,3},{1,0},{2,1},{3,2},{4,7},{5,4},{6,5},{7,6},{8,11},{9,8},{10,9... | collective-permute-start | bytes 3145736 | tf_op jit(solution)/shard_map/ppermute | solution.py:357
  83.1 3.5 %load.1 = (bf16[2,4096,256]{2,1,0:T(8,128)(2,1)S(1)}, bf16[2,4096,256]{2,1,0:T(8,128)(2,1)S(1)}) custom-call(bf16[2,4096,256]{2,1,0:T(8,128)(2,1)} %refs_0_.1, bf16[2,4096,256]{2,1,0:T(8,128)(2,1)} %refs_1_.1), custom_call_target="tpu_custom_call" | custom-call | tf_op jit(solution)/shard_map/load/pallas_call | solution.py:253
  86.6 3.1 %gate_up.1.refs_0_ = bf16[2,256,256]{2,1,0:T(8,128)(2,1)S(1)} custom-call(s32[4]{0:T(128)S(1)} %pad_add_fusion.place, bf16[64,2048]{1,0:T(8,128)(2,1)S(1)} %collective-permute-done.12.refs_0_, bf16[64,2048]{1,0:T(8,128)(2,1)S(1)} %collective-permute-done.13.refs_1_, bf16[64,2048]{1,0:T(8,128)(2,1)S(1)} %collective-permute-done.14.refs_2_, ...), custom_call_target="tpu_custom_call" | custom-call | tf_op jit(solution)/shard_map/gate_up/pallas_call | solution.py:310
  89.8 1.7 %collective-permute-start.27 = (bf16[2,256,256]{2,1,0:T(8,128)(2,1)S(1)}, bf16[2,256,256]{2,1,0:T(8,128)(2,1)S(1)}, u32[]{:S(2)}, u32[]{:S(2)}) collective-permute-start(bf16[2,256,256]{2,1,0:T(8,128)(2,1)S(1)} %gate_up.1.refs_0_), channel_id=1, source_target_pairs={{0,2},{1,3},{2,0},{3,1},{4,6},{5,7},{6,4},{7,5},{8,10},{9,11},{10,... | collective-permute-start | bytes 786440 | tf_op jit(solution)/shard_map/ppermute | solution.py:357
  91.5 37.1 %collective-permute-done.26.refs_1_ = bf16[2,256,256]{2,1,0:T(8,128)(2,1)S(1)} collective-permute-done((bf16[2,256,256]{2,1,0:T(8,128)(2,1)S(1)}, bf16[2,256,256]{2,1,0:T(8,128)(2,1)S(1)}, u32[]{:S(2)}, u32[]{:S(2)}) %collective-permute-start.26) | collective-permute-done | bytes 262176 | tf_op jit(solution)/shard_map/ppermute | solution.py:357
  128.6 2.2 %collective-permute-start.28 = (bf16[2,256,256]{2,1,0:T(8,128)(2,1)S(1)}, bf16[2,256,256]{2,1,0:T(8,128)(2,1)S(1)}, u32[]{:S(2)}, u32[]{:S(2)}) collective-permute-start(bf16[2,256,256]{2,1,0:T(8,128)(2,1)S(1)} %gate_up.1.refs_0_), channel_id=1, source_target_pairs={{0,3},{1,0},{2,1},{3,2},{4,7},{5,4},{6,5},{7,6},{8,11},{9,8},{10,9... | collective-permute-start | bytes 786440 | tf_op jit(solution)/shard_map/ppermute | solution.py:357
  130.7 4.4 %collective-permute-done.27.refs_2_ = bf16[2,256,256]{2,1,0:T(8,128)(2,1)S(1)} collective-permute-done((bf16[2,256,256]{2,1,0:T(8,128)(2,1)S(1)}, bf16[2,256,256]{2,1,0:T(8,128)(2,1)S(1)}, u32[]{:S(2)}, u32[]{:S(2)}) %collective-permute-start.27) | collective-permute-done | bytes 262176 | tf_op jit(solution)/shard_map/ppermute | solution.py:357
  135.1 2.3 %collective-permute-done.28.refs_3_ = bf16[2,256,256]{2,1,0:T(8,128)(2,1)S(1)} collective-permute-done((bf16[2,256,256]{2,1,0:T(8,128)(2,1)S(1)}, bf16[2,256,256]{2,1,0:T(8,128)(2,1)S(1)}, u32[]{:S(2)}, u32[]{:S(2)}) %collective-permute-start.28) | collective-permute-done | bytes 262176 | tf_op jit(solution)/shard_map/ppermute | solution.py:357
  137.5 2.3 %down.1 = bf16[32,16,1024]{2,1,0:T(8,128)(2,1)} custom-call(bf16[2,256,256]{2,1,0:T(8,128)(2,1)S(1)} %gate_up.1.refs_0_, bf16[2,256,256]{2,1,0:T(8,128)(2,1)S(1)} %collective-permute-done.26.refs_1_, bf16[2,256,256]{2,1,0:T(8,128)(2,1)S(1)} %collective-permute-done.27.refs_2_, bf16[2,256,256]{2,1,0:T(8,128)(2,1)S(1)} %collective-permute-done.28.refs_3_, ...), custom_call_target="tpu_custom_call" | custom-call | tf_op jit(solution)/shard_map/down/pallas_call | solution.py:333
  139.7 4.9 %all-to-all-start = ((bf16[32,16,1024]{2,1,0:T(8,128)(2,1)}), bf16[32,16,1024]{2,1,0:T(8,128)(2,1)S(1)}, u32[]{:S(2)}, u32[]{:S(2)}) async-start(bf16[32,16,1024]{2,1,0:T(8,128)(2,1)} %down.1), calls=%async_computation | async-start | bytes 2097152 | tf_op jit(solution)/shard_map/all_to_all | solution.py:432
  145.4 16.4 %all-to-all-done = bf16[32,16,1024]{2,1,0:T(8,128)(2,1)S(1)} async-done(((bf16[32,16,1024]{2,1,0:T(8,128)(2,1)}), bf16[32,16,1024]{2,1,0:T(8,128)(2,1)S(1)}, u32[]{:S(2)}, u32[]{:S(2)}) %all-to-all-start) | async-done | bytes 1048608 | tf_op jit(solution)/shard_map/all_to_all | solution.py:432
  (61 shorter events, 21.9 us)
Async XLA Ops:
  14.0 10.8 %collective-permute-start = (bf16[32,1024]{1,0:T(8,128)(2,1)S(1)}, bf16[32,1024]{1,0:T(8,128)(2,1)S(1)}, u32[]{:S(2)}, u32[]{:S(2)}) collective-permute-start(bf16[32,1024]{1,0:T(8,128)(2,1)S(1)} %get-tuple-element.37), channel_id=1, source_target_pairs={{0,1},{1,2},{2,3},{3,0},{4,5},{5,6},{6,7},{7,4},{8,9},{9,10},{10,1... | collective-permute-start | bytes 196616 | tf_op jit(solution)/shard_map/ppermute | solution.py:357
  16.1 8.7 %collective-permute-start.1 = (bf16[32,1024]{1,0:T(8,128)(2,1)S(1)}, bf16[32,1024]{1,0:T(8,128)(2,1)S(1)}, u32[]{:S(2)}, u32[]{:S(2)}) collective-permute-start(bf16[32,1024]{1,0:T(8,128)(2,1)S(1)} %get-tuple-element.38), channel_id=1, source_target_pairs={{0,2},{1,3},{2,0},{3,1},{4,6},{5,7},{6,4},{7,5},{8,10},{9,11},{10,... | collective-permute-start | bytes 196616 | tf_op jit(solution)/shard_map/ppermute | solution.py:357
  19.7 5.1 %collective-permute-start.2 = (bf16[32,1024]{1,0:T(8,128)(2,1)S(1)}, bf16[32,1024]{1,0:T(8,128)(2,1)S(1)}, u32[]{:S(2)}, u32[]{:S(2)}) collective-permute-start(bf16[32,1024]{1,0:T(8,128)(2,1)S(1)} %get-tuple-element.39), channel_id=1, source_target_pairs={{0,3},{1,0},{2,1},{3,2},{4,7},{5,4},{6,5},{7,6},{8,11},{9,8},{10,9... | collective-permute-start | bytes 196616 | tf_op jit(solution)/shard_map/ppermute | solution.py:357
  25.7 5.5 %collective-permute-start.3 = (bf16[32,1024]{1,0:T(8,128)(2,1)S(1)}, bf16[32,1024]{1,0:T(8,128)(2,1)S(1)}, u32[]{:S(2)}, u32[]{:S(2)}) collective-permute-start(bf16[32,1024]{1,0:T(8,128)(2,1)S(1)} %get-tuple-element.67), channel_id=1, source_target_pairs={{0,1},{1,2},{2,3},{3,0},{4,5},{5,6},{6,7},{7,4},{8,9},{9,10},{10,1... | collective-permute-start | bytes 196616 | tf_op jit(solution)/shard_map/ppermute | solution.py:357
  26.8 5.8 %collective-permute-start.4 = (bf16[32,1024]{1,0:T(8,128)(2,1)S(1)}, bf16[32,1024]{1,0:T(8,128)(2,1)S(1)}, u32[]{:S(2)}, u32[]{:S(2)}) collective-permute-start(bf16[32,1024]{1,0:T(8,128)(2,1)S(1)} %get-tuple-element.67), channel_id=1, source_target_pairs={{0,2},{1,3},{2,0},{3,1},{4,6},{5,7},{6,4},{7,5},{8,10},{9,11},{10,... | collective-permute-start | bytes 196616 | tf_op jit(solution)/shard_map/ppermute | solution.py:357
  28.6 4.3 %collective-permute-start.5 = (bf16[32,1024]{1,0:T(8,128)(2,1)S(1)}, bf16[32,1024]{1,0:T(8,128)(2,1)S(1)}, u32[]{:S(2)}, u32[]{:S(2)}) collective-permute-start(bf16[32,1024]{1,0:T(8,128)(2,1)S(1)} %get-tuple-element.67), channel_id=1, source_target_pairs={{0,3},{1,0},{2,1},{3,2},{4,7},{5,4},{6,5},{7,6},{8,11},{9,8},{10,9... | collective-permute-start | bytes 196616 | tf_op jit(solution)/shard_map/ppermute | solution.py:357
  33.6 8.2 %collective-permute-start.10 = (bf16[40,2048]{1,0:T(8,128)(2,1)S(1)}, bf16[40,2048]{1,0:T(8,128)(2,1)S(1)}, u32[]{:S(2)}, u32[]{:S(2)}) collective-permute-start(bf16[40,2048]{1,0:T(8,128)(2,1)S(1)} %get-tuple-element.43.refs_6_), channel_id=1, source_target_pairs={{0,24},{4,28},{8,0},{12,4},{16,8},{20,12},{24,16},{28,20},{32,56},... | collective-permute-start | bytes 491528 | tf_op jit(solution)/shard_map/ppermute | solution.py:367
  36.4 8.4 %collective-permute-start.6 = (bf16[40,2048]{1,0:T(8,128)(2,1)S(1)}, bf16[40,2048]{1,0:T(8,128)(2,1)S(1)}, u32[]{:S(2)}, u32[]{:S(2)}) collective-permute-start(bf16[40,2048]{1,0:T(8,128)(2,1)S(1)} %get-tuple-element.43.refs_6_), channel_id=1, source_target_pairs={{0,16},{4,20},{8,24},{12,28},{16,0},{20,4},{24,8},{28,12},{32,48},... | collective-permute-start | bytes 491528 | tf_op jit(solution)/shard_map/ppermute | solution.py:367
  37.2 7.6 %collective-permute-start.11 = (bf16[40,2048]{1,0:T(8,128)(2,1)S(1)}, bf16[40,2048]{1,0:T(8,128)(2,1)S(1)}, u32[]{:S(2)}, u32[]{:S(2)}) collective-permute-start(bf16[40,2048]{1,0:T(8,128)(2,1)S(1)} %get-tuple-element.44.refs_7_), channel_id=1, source_target_pairs={{0,96},{4,100},{8,104},{12,108},{16,112},{20,116},{24,120},{28,124... | collective-permute-start | bytes 491528 | tf_op jit(solution)/shard_map/ppermute | solution.py:367
  40.2 6.9 %collective-permute-start.7 = (bf16[40,2048]{1,0:T(8,128)(2,1)S(1)}, bf16[40,2048]{1,0:T(8,128)(2,1)S(1)}, u32[]{:S(2)}, u32[]{:S(2)}) collective-permute-start(bf16[40,2048]{1,0:T(8,128)(2,1)S(1)} %get-tuple-element.44.refs_7_), channel_id=1, source_target_pairs={{0,64},{4,68},{8,72},{12,76},{16,80},{20,84},{24,88},{28,92},{32,9... | collective-permute-start | bytes 491528 | tf_op jit(solution)/shard_map/ppermute | solution.py:367
  40.9 6.5 %collective-permute-start.8 = (bf16[40,2048]{1,0:T(8,128)(2,1)S(1)}, bf16[40,2048]{1,0:T(8,128)(2,1)S(1)}, u32[]{:S(2)}, u32[]{:S(2)}) collective-permute-start(bf16[40,2048]{1,0:T(8,128)(2,1)S(1)} %get-tuple-element.43.refs_6_), channel_id=1, source_target_pairs={{0,8},{4,12},{8,16},{12,20},{16,24},{20,28},{24,0},{28,4},{32,40},... | collective-permute-start | bytes 491528 | tf_op jit(solution)/shard_map/ppermute | solution.py:367
  41.7 7.1 %collective-permute-start.9 = (bf16[40,2048]{1,0:T(8,128)(2,1)S(1)}, bf16[40,2048]{1,0:T(8,128)(2,1)S(1)}, u32[]{:S(2)}, u32[]{:S(2)}) collective-permute-start(bf16[40,2048]{1,0:T(8,128)(2,1)S(1)} %get-tuple-element.44.refs_7_), channel_id=1, source_target_pairs={{0,32},{4,36},{8,40},{12,44},{16,48},{20,52},{24,56},{28,60},{32,6... | collective-permute-start | bytes 491528 | tf_op jit(solution)/shard_map/ppermute | solution.py:367
  51.1 8.0 %collective-permute-start.12 = (bf16[64,2048]{1,0:T(8,128)(2,1)S(1)}, bf16[64,2048]{1,0:T(8,128)(2,1)S(1)}, u32[]{:S(2)}, u32[]{:S(2)}) collective-permute-start(bf16[64,2048]{1,0:T(8,128)(2,1)S(1)} %get-tuple-element.45), channel_id=1, source_target_pairs={{0,64},{4,68},{8,72},{12,76},{16,80},{20,84},{24,88},{28,92},{32,9... | collective-permute-start | bytes 786440 | tf_op jit(solution)/shard_map/ppermute | solution.py:367
  52.7 9.3 %collective-permute-start.13 = (bf16[64,2048]{1,0:T(8,128)(2,1)S(1)}, bf16[64,2048]{1,0:T(8,128)(2,1)S(1)}, u32[]{:S(2)}, u32[]{:S(2)}) collective-permute-start(bf16[64,2048]{1,0:T(8,128)(2,1)S(1)} %get-tuple-element.46), channel_id=1, source_target_pairs={{0,16},{4,20},{8,24},{12,28},{16,0},{20,4},{24,8},{28,12},{32,48},... | collective-permute-start | bytes 786440 | tf_op jit(solution)/shard_map/ppermute | solution.py:367
  54.5 10.2 %collective-permute-start.14 = (bf16[64,2048]{1,0:T(8,128)(2,1)S(1)}, bf16[64,2048]{1,0:T(8,128)(2,1)S(1)}, u32[]{:S(2)}, u32[]{:S(2)}) collective-permute-start(bf16[64,2048]{1,0:T(8,128)(2,1)S(1)} %get-tuple-element.47), channel_id=1, source_target_pairs={{0,68},{4,64},{8,76},{12,72},{16,84},{20,80},{24,92},{28,88},{32,1... | collective-permute-start | bytes 786440 | tf_op jit(solution)/shard_map/ppermute | solution.py:367
  54.5 12.5 %collective-permute-start.15 = (bf16[64,2048]{1,0:T(8,128)(2,1)S(1)}, bf16[64,2048]{1,0:T(8,128)(2,1)S(1)}, u32[]{:S(2)}, u32[]{:S(2)}) collective-permute-start(bf16[64,2048]{1,0:T(8,128)(2,1)S(1)} %get-tuple-element.48), channel_id=1, source_target_pairs={{0,20},{4,16},{8,28},{12,24},{16,4},{20,0},{24,12},{28,8},{32,52},... | collective-permute-start | bytes 786440 | tf_op jit(solution)/shard_map/ppermute | solution.py:367
  58.0 12.3 %collective-permute-start.16 = (bf16[64,2048]{1,0:T(8,128)(2,1)S(1)}, bf16[64,2048]{1,0:T(8,128)(2,1)S(1)}, u32[]{:S(2)}, u32[]{:S(2)}) collective-permute-start(bf16[64,2048]{1,0:T(8,128)(2,1)S(1)} %get-tuple-element.49), channel_id=1, source_target_pairs={{0,32},{4,36},{8,40},{12,44},{16,48},{20,52},{24,56},{28,60},{32,6... | collective-permute-start | bytes 786440 | tf_op jit(solution)/shard_map/ppermute | solution.py:367
  59.1 12.7 %collective-permute-start.17 = (bf16[64,2048]{1,0:T(8,128)(2,1)S(1)}, bf16[64,2048]{1,0:T(8,128)(2,1)S(1)}, u32[]{:S(2)}, u32[]{:S(2)}) collective-permute-start(bf16[64,2048]{1,0:T(8,128)(2,1)S(1)} %get-tuple-element.50), channel_id=1, source_target_pairs={{0,8},{4,12},{8,16},{12,20},{16,24},{20,28},{24,0},{28,4},{32,40},... | collective-permute-start | bytes 786440 | tf_op jit(solution)/shard_map/ppermute | solution.py:367
  61.9 9.9 %collective-permute-start.18 = (bf16[64,2048]{1,0:T(8,128)(2,1)S(1)}, bf16[64,2048]{1,0:T(8,128)(2,1)S(1)}, u32[]{:S(2)}, u32[]{:S(2)}) collective-permute-start(bf16[64,2048]{1,0:T(8,128)(2,1)S(1)} %get-tuple-element.51), channel_id=1, source_target_pairs={{0,96},{4,100},{8,104},{12,108},{16,112},{20,116},{24,120},{28,124... | collective-permute-start | bytes 786440 | tf_op jit(solution)/shard_map/ppermute | solution.py:367
  64.8 9.2 %collective-permute-start.19 = (bf16[64,2048]{1,0:T(8,128)(2,1)S(1)}, bf16[64,2048]{1,0:T(8,128)(2,1)S(1)}, u32[]{:S(2)}, u32[]{:S(2)}) collective-permute-start(bf16[64,2048]{1,0:T(8,128)(2,1)S(1)} %get-tuple-element.52), channel_id=1, source_target_pairs={{0,24},{4,28},{8,0},{12,4},{16,8},{20,12},{24,16},{28,20},{32,56},... | collective-permute-start | bytes 786440 | tf_op jit(solution)/shard_map/ppermute | solution.py:367
  67.0 9.1 %collective-permute-start.20 = (bf16[64,2048]{1,0:T(8,128)(2,1)S(1)}, bf16[64,2048]{1,0:T(8,128)(2,1)S(1)}, u32[]{:S(2)}, u32[]{:S(2)}) collective-permute-start(bf16[64,2048]{1,0:T(8,128)(2,1)S(1)} %get-tuple-element.53), channel_id=1, source_target_pairs={{0,36},{4,32},{8,44},{12,40},{16,52},{20,48},{24,60},{28,56},{32,6... | collective-permute-start | bytes 786440 | tf_op jit(solution)/shard_map/ppermute | solution.py:367
  70.3 9.6 %collective-permute-start.21 = (bf16[64,2048]{1,0:T(8,128)(2,1)S(1)}, bf16[64,2048]{1,0:T(8,128)(2,1)S(1)}, u32[]{:S(2)}, u32[]{:S(2)}) collective-permute-start(bf16[64,2048]{1,0:T(8,128)(2,1)S(1)} %get-tuple-element.54), channel_id=1, source_target_pairs={{0,12},{4,8},{8,20},{12,16},{16,28},{20,24},{24,4},{28,0},{32,44},... | collective-permute-start | bytes 786440 | tf_op jit(solution)/shard_map/ppermute | solution.py:367
  71.8 10.8 %collective-permute-start.22 = (bf16[64,2048]{1,0:T(8,128)(2,1)S(1)}, bf16[64,2048]{1,0:T(8,128)(2,1)S(1)}, u32[]{:S(2)}, u32[]{:S(2)}) collective-permute-start(bf16[64,2048]{1,0:T(8,128)(2,1)S(1)} %get-tuple-element.55), channel_id=1, source_target_pairs={{0,100},{4,96},{8,108},{12,104},{16,116},{20,112},{24,124},{28,120... | collective-permute-start | bytes 786440 | tf_op jit(solution)/shard_map/ppermute | solution.py:367
  71.8 10.8 %collective-permute-start.23 = (bf16[64,2048]{1,0:T(8,128)(2,1)S(1)}, bf16[64,2048]{1,0:T(8,128)(2,1)S(1)}, u32[]{:S(2)}, u32[]{:S(2)}) collective-permute-start(bf16[64,2048]{1,0:T(8,128)(2,1)S(1)} %get-tuple-element.56), channel_id=1, source_target_pairs={{0,28},{4,24},{8,4},{12,0},{16,12},{20,8},{24,20},{28,16},{32,60},... | collective-permute-start | bytes 786440 | tf_op jit(solution)/shard_map/ppermute | solution.py:367
  74.0 63.5 %collective-permute-start.29 = (bf16[2,256,1024]{2,1,0:T(8,128)(2,1)}, bf16[2,256,1024]{2,1,0:T(8,128)(2,1)S(1)}, u32[]{:S(2)}, u32[]{:S(2)}) collective-permute-start(bf16[2,256,1024]{2,1,0:T(8,128)(2,1)} %get-tuple-element.64), channel_id=1, source_target_pairs={{0,1},{1,2},{2,3},{3,0},{4,5},{5,6},{6,7},{7,4},{8,9},{9,10},{10,1... | collective-permute-start | bytes 3145736 | tf_op jit(solution)/shard_map/ppermute | solution.py:357
  76.1 61.4 %collective-permute-start.30 = (bf16[2,256,1024]{2,1,0:T(8,128)(2,1)}, bf16[2,256,1024]{2,1,0:T(8,128)(2,1)S(1)}, u32[]{:S(2)}, u32[]{:S(2)}) collective-permute-start(bf16[2,256,1024]{2,1,0:T(8,128)(2,1)} %get-tuple-element.65), channel_id=1, source_target_pairs={{0,2},{1,3},{2,0},{3,1},{4,6},{5,7},{6,4},{7,5},{8,10},{9,11},{10,... | collective-permute-start | bytes 3145736 | tf_op jit(solution)/shard_map/ppermute | solution.py:357
  79.9 57.6 %collective-permute-start.31 = (bf16[2,256,1024]{2,1,0:T(8,128)(2,1)S(1)}, bf16[2,256,1024]{2,1,0:T(8,128)(2,1)S(1)}, u32[]{:S(2)}, u32[]{:S(2)}) collective-permute-start(bf16[2,256,1024]{2,1,0:T(8,128)(2,1)S(1)} %get-tuple-element.66), channel_id=1, source_target_pairs={{0,3},{1,0},{2,1},{3,2},{4,7},{5,4},{6,5},{7,6},{8,11},{9,8},{10,9... | collective-permute-start | bytes 3145736 | tf_op jit(solution)/shard_map/ppermute | solution.py:357
  82.6 4.0 %collective-permute-start.25 = (bf16[64,2048]{1,0:T(8,128)(2,1)S(1)}, bf16[64,2048]{1,0:T(8,128)(2,1)S(1)}, u32[]{:S(2)}, u32[]{:S(2)}) collective-permute-start(bf16[64,2048]{1,0:T(8,128)(2,1)S(1)} %get-tuple-element.58), channel_id=1, source_target_pairs={{0,4},{4,0},{8,12},{12,8},{16,20},{20,16},{24,28},{28,24},{32,36},... | collective-permute-start | bytes 786440 | tf_op jit(solution)/shard_map/ppermute | solution.py:367
  89.7 38.9 %collective-permute-start.26 = (bf16[2,256,256]{2,1,0:T(8,128)(2,1)S(1)}, bf16[2,256,256]{2,1,0:T(8,128)(2,1)S(1)}, u32[]{:S(2)}, u32[]{:S(2)}) collective-permute-start(bf16[2,256,256]{2,1,0:T(8,128)(2,1)S(1)} %gate_up.1.refs_0_), channel_id=1, source_target_pairs={{0,1},{1,2},{2,3},{3,0},{4,5},{5,6},{6,7},{7,4},{8,9},{9,10},{10,1... | collective-permute-start | bytes 786440 | tf_op jit(solution)/shard_map/ppermute | solution.py:357
  89.8 45.3 %collective-permute-start.27 = (bf16[2,256,256]{2,1,0:T(8,128)(2,1)S(1)}, bf16[2,256,256]{2,1,0:T(8,128)(2,1)S(1)}, u32[]{:S(2)}, u32[]{:S(2)}) collective-permute-start(bf16[2,256,256]{2,1,0:T(8,128)(2,1)S(1)} %gate_up.1.refs_0_), channel_id=1, source_target_pairs={{0,2},{1,3},{2,0},{3,1},{4,6},{5,7},{6,4},{7,5},{8,10},{9,11},{10,... | collective-permute-start | bytes 786440 | tf_op jit(solution)/shard_map/ppermute | solution.py:357
  128.6 8.9 %collective-permute-start.28 = (bf16[2,256,256]{2,1,0:T(8,128)(2,1)S(1)}, bf16[2,256,256]{2,1,0:T(8,128)(2,1)S(1)}, u32[]{:S(2)}, u32[]{:S(2)}) collective-permute-start(bf16[2,256,256]{2,1,0:T(8,128)(2,1)S(1)} %gate_up.1.refs_0_), channel_id=1, source_target_pairs={{0,3},{1,0},{2,1},{3,2},{4,7},{5,4},{6,5},{7,6},{8,11},{9,8},{10,9... | collective-permute-start | bytes 786440 | tf_op jit(solution)/shard_map/ppermute | solution.py:357
  139.7 22.1 %all-to-all-start = ((bf16[32,16,1024]{2,1,0:T(8,128)(2,1)}), bf16[32,16,1024]{2,1,0:T(8,128)(2,1)S(1)}, u32[]{:S(2)}, u32[]{:S(2)}) async-start(bf16[32,16,1024]{2,1,0:T(8,128)(2,1)} %down.1), calls=%async_computation | async-start | bytes 2097152 | tf_op jit(solution)/shard_map/all_to_all | solution.py:432
  (4 other events, 80.5 us)

commit v2 on v1

--- a/solution.py
+++ b/solution.py
@@ -14,81 +14,97 @@
 FAR_ORDER = ((2, 0), (2, 1), (1, 0), (3, 0), (1, 1), (3, 1), (0, 1), (0, 0))
 
 
-def attend_kernel(lengths, place, q_ref, k_ref, v_ref, nk_ref, nv_ref, proj_hbm, *outs):
-    *out_refs, rows_ref, proj_ref, sems = outs
-    step = pl.program_id(0)
-    steps = pl.num_programs(0)
-    parts = sems.shape[0]
+def attend_kernel(lengths, place, q_ref, k_hbm, v_hbm, nk_ref, nv_ref, proj_hbm, *outs):
+    *out_refs, k_ref, v_ref, rows_ref, proj_ref, sum_ref, cache_sems, proj_sems = outs
+    steps, parts = cache_sems.shape[1], proj_sems.shape[0]
     depth = proj_ref.shape[0] // parts
+
+    def cached(g, kind):
+        cut = pl.ds(g * GROUP, GROUP)
+        source, target = ((k_hbm, k_ref), (v_hbm, v_ref))[kind]
+        return pltpu.make_async_copy(source.at[cut, 0], target.at[cut], cache_sems.at[kind, g])
 
     def part(i):
         cut = pl.ds(i * depth, depth)
-        return pltpu.make_async_copy(proj_hbm.at[cut], proj_ref.at[cut], sems.at[i])
-
-    @pl.when(step == 0)
-    def _():
-        for i in range(parts):
-            part(i).start()
-
+        return pltpu.make_async_copy(proj_hbm.at[cut], proj_ref.at[cut], proj_sems.at[i])
+
+    for g in range(steps):
+        for kind in range(2):
+            cached(g, kind).start()
+    for g in range(steps):
+        for kind in range(2):
+            cached(g, kind).wait()
+        part(g).start()
+        attend_group(g * GROUP, lengths, q_ref, k_ref, v_ref, nk_ref, nv_ref, rows_ref)
+    attn = rows_ref[...].astype(BF16)
+    groups = len(out_refs)
+    share = out_refs[0].shape[1]
+    for i in range(parts):
+        part(i).wait()
+        cut = slice(i * depth, (i + 1) * depth)
+        for ahead in range(groups):
+            column = lax.rem(place[HEAD] + ahead, groups) * share
+            weight = proj_ref[cut, pl.ds(pl.multiple_of(column, share), share)]
+            terms = jnp.dot(attn[:, cut], weight, preferred_element_type=F32)
+            if i:
+                terms = terms + sum_ref[ahead]
+            if i < parts - 1:
+                sum_ref[ahead] = terms
+            else:
+                out_refs[ahead][...] = terms.astype(out_refs[ahead].dtype)
+
+
+def attend_group(base, lengths, q_ref, k_ref, v_ref, nk_ref, nv_ref, rows_ref):
     size = nk_ref.shape[1]
     heads = q_ref.shape[1] // size
-    slots = k_ref.shape[2]
+    slots = k_ref.shape[1]
     scale = size ** (-0.5)
-    base = pl.multiple_of(step * GROUP, GROUP)
     queries = q_ref[pl.ds(base, GROUP), :].astype(F32)
     new_keys = nk_ref[pl.ds(base, GROUP), :].astype(F32)
     new_values = nv_ref[pl.ds(base, GROUP), :].astype(F32)
     slot_of = lax.broadcasted_iota(jnp.int32, (heads, slots), 1)
-    done = []
     blank = jnp.zeros((heads, size), F32)
+    split = [
+        jnp.concatenate([queries[j : j + 1, i * size : (i + 1) * size] for i in range(heads)], 0)
+        for j in range(GROUP)
+    ]
+    scores = []
     for j in range(0, GROUP, 2):
-        pair = [
-            jnp.concatenate([queries[k : k + 1, i * size : (i + 1) * size] for i in range(heads)], 0)
-            for k in (j, j + 1)
-        ]
         spread = jnp.concatenate(
-            [jnp.concatenate([pair[0], blank], 1), jnp.concatenate([blank, pair[1]], 1)], 0
+            [jnp.concatenate([split[j], blank], 1), jnp.concatenate([blank, split[j + 1]], 1)], 0
         )
-        keys = jnp.concatenate([k_ref[j, 0], k_ref[j + 1, 0]], 1)
-        values = jnp.concatenate([v_ref[j, 0], v_ref[j + 1, 0]], 1)
-        scores = (
+        keys = jnp.concatenate([k_ref[base + j], k_ref[base + j + 1]], 1)
+        scores.append(
             lax.dot_general(
                 spread.astype(BF16), keys, (((1,), (1,)), ((), ())), preferred_element_type=F32
             )
-            * scale
         )
-        fresh = [
-            jnp.sum(pair[k] * new_keys[j + k : j + k + 1], 1, keepdims=True) for k in range(2)
-        ]
-        fresh = jnp.concatenate(fresh, 0) * scale
-        live = jnp.concatenate([slot_of < lengths[base + j + k] for k in range(2)], 0)
-        scores = jnp.where(live, scores, -1e30)
-        highest = jnp.maximum(jnp.max(scores, 1, keepdims=True), fresh)
-        weights = jnp.where(live, jnp.exp(scores - highest), 0.0)
-        own = jnp.exp(fresh - highest)
-        total = jnp.sum(weights, 1, keepdims=True) + own
-        share = 1.0 / total
-        probs = (weights * share).astype(BF16)
-        own = (own * share).astype(BF16).astype(F32)
-        mixed = jnp.dot(probs, values, preferred_element_type=F32)
-        for k in range(2):
-            rows = slice(k * heads, (k + 1) * heads)
-            part_sum = mixed[rows, k * size : (k + 1) * size] + own[rows] * new_values[j + k : j + k + 1]
-            done.append(jnp.concatenate([part_sum[i : i + 1] for i in range(heads)], 1))
+    scores = jnp.concatenate(scores, 0) * scale
+    new_keys, new_values = (
+        jnp.concatenate([jnp.broadcast_to(new[j : j + 1], (heads, size)) for j in range(GROUP)], 0)
+        for new in (new_keys, new_values)
+    )
+    fresh = jnp.sum(jnp.concatenate(split, 0) * new_keys, 1, keepdims=True) * scale
+    live = jnp.concatenate([slot_of < lengths[base + j] for j in range(GROUP)], 0)
+    scores = jnp.where(live, scores, -1e30)
+    highest = jnp.maximum(jnp.max(scores, 1, keepdims=True), fresh)
+    weights = jnp.where(live, jnp.exp(scores - highest), 0.0)
+    own = jnp.exp(fresh - highest)
+    total = jnp.sum(weights, 1, keepdims=True) + own
+    share = 1.0 / total
+    probs = (weights * share).astype(BF16)
+    own = (own * share).astype(BF16).astype(F32) * new_values
+    mixed = []
+    for j in range(0, GROUP, 2):
+        values = jnp.concatenate([v_ref[base + j], v_ref[base + j + 1]], 1)
+        rows = slice(j * heads, (j + 2) * heads)
+        pair = jnp.dot(probs[rows], values, preferred_element_type=F32)
+        mixed += [pair[:heads, :size], pair[heads:, size:]]
+    done = []
+    for j in range(GROUP):
+        mix = mixed[j] + own[j * heads : (j + 1) * heads]
+        done.append(jnp.concatenate([mix[i : i + 1] for i in range(heads)], 1))
     rows_ref[pl.ds(base, GROUP), :] = jnp.concatenate(done, 0)
-
-    @pl.when(step == steps - 1)
-    def _():
-        attn = rows_ref[...].astype(BF16)
-        for i in range(parts):
-            part(i).wait()
-        groups = len(out_refs)
-        share = out_refs[0].shape[1]
-        for ahead in [*range(1, groups), 0]:
-            column = lax.rem(place[HEAD] + ahead, groups) * share
-            weight = proj_ref[:, pl.ds(pl.multiple_of(column, share), share)]
-            terms = jnp.dot(attn, weight, preferred_element_type=F32)
-            out_refs[ahead][...] = terms.astype(out_refs[ahead].dtype)
 
 
 def in_hbm(value):
@@ -104,34 +120,26 @@
     size = new_key.shape[1]
     slots = key_cache.shape[2]
     share = out_proj.shape[1] // groups
-    whole = lambda shape: pl.BlockSpec(shape, lambda s, *_: (0, 0))
-    cache = pl.BlockSpec((GROUP, 1, slots, size), lambda s, *_: (s, 0, 0, 0))
+    vmem = pl.BlockSpec(memory_space=pltpu.VMEM)
+    smem = pl.BlockSpec(memory_space=pltpu.SMEM)
+    hbm = pl.BlockSpec(memory_space=pl.ANY)
     return pl.pallas_call(
         attend_kernel,
         out_shape=[
             jax.ShapeDtypeStruct((rows, share), BF16 if ahead else F32) for ahead in range(groups)
         ],
-        grid_spec=pltpu.PrefetchScalarGridSpec(
-            num_scalar_prefetch=2,
-            grid=(rows // GROUP,),
-            in_specs=[
-                whole((rows, wide)),
-                cache,
-                cache,
-                whole((rows, size)),
-                whole((rows, size)),
-                pl.BlockSpec(memory_space=pl.ANY),
-            ],
-            out_specs=[whole((rows, share))] * groups,
-            scratch_shapes=[
-                pltpu.VMEM((rows, wide), F32),
-                pltpu.VMEM(out_proj.shape, BF16),
-                pltpu.SemaphoreType.DMA((4,)),
-            ],
-        ),
-        compiler_params=pltpu.CompilerParams(
-            dimension_semantics=("arbitrary",), vmem_limit_bytes=24 << 20
-        ),
+        in_specs=[smem, smem, vmem, hbm, hbm, vmem, vmem, hbm],
+        out_specs=[vmem] * groups,
+        scratch_shapes=[
+            pltpu.VMEM((rows, slots, size), BF16),
+            pltpu.VMEM((rows, slots, size), BF16),
+            pltpu.VMEM((rows, wide), F32),
+            pltpu.VMEM(out_proj.shape, BF16),
+            pltpu.VMEM((groups, rows, share), F32),
+            pltpu.SemaphoreType.DMA((2, rows // GROUP)),
+            pltpu.SemaphoreType.DMA((rows // GROUP,)),
+        ],
+        compiler_params=pltpu.CompilerParams(vmem_limit_bytes=24 << 20),
         name="attend_project",
     )(
         in_hbm(lengths),
@@ -259,6 +267,36 @@
         compiler_params=pltpu.CompilerParams(vmem_limit_bytes=1 << 20),
         name="load",
     )(*[in_hbm(value) for value in values])
+
+
+def cut_kernel(place, source, *refs):
+    *targets, sems = refs
+    groups = len(targets) + 1
+    share = targets[0].shape[2]
+    copies = []
+    for ahead, target in enumerate(targets, 1):
+        column = pl.multiple_of(lax.rem(place[HEAD] + ahead, groups) * share, share)
+        copies.append(
+            pltpu.make_async_copy(source.at[:, :, pl.ds(column, share)], target, sems.at[ahead - 1])
+        )
+    for copy in copies:
+        copy.start()
+    for copy in copies:
+        copy.wait()
+
+
+def cut_columns(value, place, groups):
+    experts, depth, width = value.shape
+    shape = (experts, depth, width // groups)
+    return pl.pallas_call(
+        cut_kernel,
+        out_shape=[pltpu.VMEM(shape, value.dtype)] * (groups - 1),
+        in_specs=[pl.BlockSpec(memory_space=pltpu.SMEM), pl.BlockSpec(memory_space=pl.ANY)],
+        out_specs=[pl.BlockSpec(memory_space=pltpu.VMEM)] * (groups - 1),
+        scratch_shapes=[pltpu.SemaphoreType.DMA((groups - 1,))],
+        compiler_params=pltpu.CompilerParams(vmem_limit_bytes=8 << 20),
+        name="cut_columns",
+    )(place, in_hbm(value))
 
 
 def gate_up_kernel(place, *refs):
@@ -318,7 +356,7 @@
     )(place, *in_vmem([part[step * 2 + flip] for step, flip in FAR_ORDER for part in (first, second)]), *in_vmem([w_gate, w_up]))
 
 
-def down_kernel(*refs):
+def down_kernel(place, *refs):
     *ins, out_ref = refs
     count = len(ins) // 2
     total = 0.0
@@ -327,21 +365,25 @@
     out_ref[...] = total.astype(out_ref.dtype).reshape(out_ref.shape)
 
 
-def down(acts, weights, pools, capacity):
+def down(acts, w_down, moved, place, pools, capacity):
     experts, rows, units = acts[0].shape
-    share = weights[0].shape[2]
+    share = moved[0].shape[2]
     return pl.pallas_call(
         down_kernel,
         out_shape=jax.ShapeDtypeStruct((pools, experts * capacity, share), BF16),
-        grid=(experts,),
-        in_specs=[pl.BlockSpec((1, rows, units), lambda e: (e, 0, 0))] * len(acts)
-        + [pl.BlockSpec((1, units, share), lambda e: (e, 0, 0))] * len(weights),
-        out_specs=pl.BlockSpec((pools, capacity, share), lambda e: (0, e, 0)),
+        grid_spec=pltpu.PrefetchScalarGridSpec(
+            num_scalar_prefetch=1,
+            grid=(experts,),
+            in_specs=[pl.BlockSpec((1, rows, units), lambda e, p: (e, 0, 0))] * len(acts)
+            + [pl.BlockSpec((1, units, share), lambda e, p: (e, 0, p[HEAD]))]
+            + [pl.BlockSpec((1, units, share), lambda e, p: (e, 0, 0))] * len(moved),
+            out_specs=pl.BlockSpec((pools, capacity, share), lambda e, p: (0, e, 0)),
+        ),
         compiler_params=pltpu.CompilerParams(
             dimension_semantics=("arbitrary",), vmem_limit_bytes=16 << 20
         ),
         name="down",
-    )(*in_vmem([*acts, *weights]))
+    )(place, *in_vmem(acts), in_hbm(w_down), *in_vmem(moved))
 
 
 def route_slots(expert_ids, capacity):
@@ -405,16 +447,13 @@
     take_high = take.astype(BF16)
     take_low = (take - take_high.astype(F32)).astype(BF16)
     ids = jnp.tile(expert_ids.T.astype(BF16), (1, 128 // rows))
-    columns = [
-        lax.dynamic_slice_in_dim(w_down, lax.rem(head + step, groups) * share, share, 2)
-        for step in range(groups)
-    ]
+    columns = cut_columns(w_down, place, groups)
     others, columns = lax.optimization_barrier((others, columns))
     hidden = lax.dynamic_slice_in_dim(x_rows, head * share, share, 1).astype(F32) + own
     for other in others:
         hidden = hidden + other.astype(F32)
     slices = [turned(hidden.astype(BF16), step) for step in steps]
-    moved = [turned(piece, step) for step, piece in zip(steps, columns[1:])]
+    moved = [turned(piece, step) for step, piece in zip(steps, columns)]
     first, second = norm_rows(hidden, slices, norm_gain, ids, place)
     along_x = [first] + [moved_in_plane(first, 0, step, 0) for step in (1, 2, 3)]
     along_y = [second] + [moved_in_plane(second, step, 0, 0) for step in (1, 2, 3)]
@@ -428,7 +467,7 @@
     gate_near, up_near = load(w_gate, w_up)
     act = gate_up(from_y, from_x, gate_near, up_near, place, pools, capacity)
     acts = [act] + [turned(act, step) for step in steps]
-    produced = down(acts, [columns[0]] + moved, pools, capacity)
+    produced = down(acts, w_down, moved, place, pools, capacity)
     returned = lax.all_to_all(produced, "pool", split_axis=0, concat_axis=0, tiled=True)
     returned = returned.reshape(pools * slots, share)
     moe = jnp.dot(take_high, returned, preferred_element_type=F32) + jnp.dot(
@@ -454,4 +493,6 @@
         P("pool", None, "head"),
         P("pool", "head", None),
     )
-    return jax.shard_map(body, mesh=mesh, in_specs=placed, out_specs=P("pool", "head"), check_vma=False)
+    return jax.shard_map(
+        body, mesh=mesh, in_specs=placed, out_specs=P("pool", "head"), check_vma=False
+    )

time: 164 us -> 160 us (0.976)
  waiting for transfers between devices: 80.2 us -> 85 us
  local copies, waits for them, and re-layouts: 4.56 us -> 0.45 us
  starting transfers between devices: 49.8 us -> 46.4 us
  Pallas kernels: 25.8 us -> 23.4 us
    pallas_call x1, Pallas kernels: 13.9 us -> 7.52 us  [attend_project(): pl.pallas_call(attend_kernel, out_shape=[jax.ShapeDtypeStruct((rows, shar...]
    dynamic_slice x1 -> x0, local copies, waits for them, and re-layouts: 4.12 us -> none  [body(): lax.dynamic_slice_in_dim(w_down, lax.rem(head + step, groups) * share, sh...]
    ppermute x12, waiting for transfers between devices: 47 us -> 49.9 us  [turned(): lax.ppermute(value, 'head', [(i, (i + step) % groups) for i in range(grou...]
    ppermute x12, starting transfers between devices: 19.8 us -> 17 us  [turned(): lax.ppermute(value, 'head', [(i, (i + step) % groups) for i in range(grou...]
    pallas_call x0 -> x1, Pallas kernels: none -> 2.44 us  [cut_columns(): pl.pallas_call(cut_kernel, out_shape=[pltpu.VMEM(shape, value.dtype)] * (...]
    ppermute x20, waiting for transfers between devices: 16.8 us -> 18.7 us  [moved_in_plane(): return lax.ppermute(value, 'pool', pairs)]
  transfers between devices with their start and end apart: 33 -> 33, of which waited for: 18 -> 19; matrix products, arithmetic and copies ran while one was open for 3% -> 1% of each run, Pallas kernels for 4% -> 6%
where the time goes in v2:
time: 160 us; the launch traced here: 159 us
  waiting for transfers between devices  85 us (53%)
  starting transfers between devices  46.4 us (29%)
  Pallas kernels  23.4 us (15%)
  other arithmetic  2.1 us (1%)
    ppermute x12, waiting for transfers between devices, turned(): lax.ppermute(value, 'head', [(i, (i + step) % groups) for i in range(grou...  49.9 us
    ppermute x20, starting transfers between devices, moved_in_plane(): return lax.ppermute(value, 'pool', pairs)  24 us
    ppermute x20, waiting for transfers between devices, moved_in_plane(): return lax.ppermute(value, 'pool', pairs)  18.7 us
    ppermute x12, starting transfers between devices, turned(): lax.ppermute(value, 'head', [(i, (i + step) % groups) for i in range(grou...  17 us
    all_to_all x1, waiting for transfers between devices, body(): lax.all_to_all(produced, 'pool', split_axis=0, concat_axis=0, tiled=True)  16.4 us
    pallas_call x1, Pallas kernels, attend_project(): pl.pallas_call(attend_kernel, out_shape=[jax.ShapeDtypeStruct((rows, shar...  7.52 us
    all_to_all x1, starting transfers between devices, body(): lax.all_to_all(produced, 'pool', split_axis=0, concat_axis=0, tiled=True)  5.48 us
    pallas_call x1, Pallas kernels, down(): pl.pallas_call(down_kernel, out_shape=jax.ShapeDtypeStruct((pools, expert...  3.86 us
  transfers between devices with their start and end apart: 33, of which 19 were waited for; matrix products, arithmetic and copies ran while one was open for 1% of the time, Pallas kernels for 6%

profile of v2, /device:TPU:0, one launch (start us, length us, event | category | flops | bytes accessed | tf_op | source)
XLA Modules:
  0.0 158.8 jit_solution(4249620220526528025)
XLA Ops:
  0.1 7.5 %attend_project.1 = (f32[32,1024]{1,0:T(8,128)S(1)}, bf16[32,1024]{1,0:T(8,128)(2,1)S(1)}, bf16[32,1024]{1,0:T(8,128)(2,1)S(1)}, bf16[32,1024]{1,0:T(8,128)(2,1)S(1)}) custom-call(s32[32]{0:T(128)} %lengths.1, s32[4]{0:T(128)S(1)} %pad_add_fusion.place, bf16[32,1024]{1,0:T(8,128)(2,1)} %q_ref.1, bf16[32,1,512,128]{3,2,1,0:T(8,128)(2,1)} %k_hbm.1, ...), custom_call_target="tpu_custom_call" | custom-call | tf_op jit(solution)/shard_map/attend_project/pallas_call | solution.py:126
  7.6 2.1 %collective-permute-start = (bf16[32,1024]{1,0:T(8,128)(2,1)S(1)}, bf16[32,1024]{1,0:T(8,128)(2,1)}, u32[]{:S(2)}, u32[]{:S(2)}) collective-permute-start(bf16[32,1024]{1,0:T(8,128)(2,1)S(1)} %get-tuple-element.39), channel_id=1, source_target_pairs={{0,1},{1,2},{2,3},{3,0},{4,5},{5,6},{6,7},{7,4},{8,9},{9,10},{10,1... | collective-permute-start | bytes 196616 | tf_op jit(solution)/shard_map/ppermute | solution.py:399
  9.7 3.6 %collective-permute-start.1 = (bf16[32,1024]{1,0:T(8,128)(2,1)S(1)}, bf16[32,1024]{1,0:T(8,128)(2,1)}, u32[]{:S(2)}, u32[]{:S(2)}) collective-permute-start(bf16[32,1024]{1,0:T(8,128)(2,1)S(1)} %get-tuple-element.40), channel_id=1, source_target_pairs={{0,2},{1,3},{2,0},{3,1},{4,6},{5,7},{6,4},{7,5},{8,10},{9,11},{10,... | collective-permute-start | bytes 196616 | tf_op jit(solution)/shard_map/ppermute | solution.py:399
  14.3 2.4 %cut_columns.1 = (bf16[2,256,1024]{2,1,0:T(8,128)(2,1)S(1)}, bf16[2,256,1024]{2,1,0:T(8,128)(2,1)S(1)}, bf16[2,256,1024]{2,1,0:T(8,128)(2,1)S(1)}) custom-call(s32[4]{0:T(128)S(1)} %pad_add_fusion.place, bf16[2,256,4096]{2,1,0:T(8,128)(2,1)} %refs_4_.1), custom_call_target="tpu_custom_call" | custom-call | tf_op jit(solution)/shard_map/cut_columns/pallas_call | solution.py:291
  17.7 1.6 %fusion.7 = (bf16[32,1024]{1,0:T(8,128)(2,1)}, f32[32,1024]{1,0:T(8,128)S(1)}) fusion(bf16[32,1024]{1,0:T(8,128)(2,1)} %collective-permute-done.2, bf16[32,1024]{1,0:T(8,128)(2,1)} %collective-permute-done.1, bf16[32,1024]{1,0:T(8,128)(2,1)} %collective-permute-done, f32[32,1024]{1,0:T(8,128)S(1)} %get-tuple-element.38, bf16[32,4096]{1,0:T(8,128)(2,1)} %param.14, ...), kind=kLoop, calls=%fused_computation.16 | loop fusion | flops 294912 | bytes 589828 | tf_op jit(solution)/shard_map/convert_element_type | solution.py:455
  19.5 3.5 %collective-permute-start.4 = (bf16[32,1024]{1,0:T(8,128)(2,1)}, bf16[32,1024]{1,0:T(8,128)(2,1)S(1)}, u32[]{:S(2)}, u32[]{:S(2)}) collective-permute-start(bf16[32,1024]{1,0:T(8,128)(2,1)} %get-tuple-element.71), channel_id=1, source_target_pairs={{0,2},{1,3},{2,0},{3,1},{4,6},{5,7},{6,4},{7,5},{8,10},{9,11},{10,... | collective-permute-start | bytes 196616 | tf_op jit(solution)/shard_map/ppermute | solution.py:399
  28.2 2.8 %collective-permute-start.10 = (bf16[40,2048]{1,0:T(8,128)(2,1)S(1)}, bf16[40,2048]{1,0:T(8,128)(2,1)S(1)}, u32[]{:S(2)}, u32[]{:S(2)}) collective-permute-start(bf16[40,2048]{1,0:T(8,128)(2,1)S(1)} %get-tuple-element.48.refs_6_), channel_id=1, source_target_pairs={{0,24},{4,28},{8,0},{12,4},{16,8},{20,12},{24,16},{28,20},{32,56},... | collective-permute-start | bytes 491528 | tf_op jit(solution)/shard_map/ppermute | solution.py:409
  31.8 3.0 %collective-permute-start.11 = (bf16[40,2048]{1,0:T(8,128)(2,1)S(1)}, bf16[40,2048]{1,0:T(8,128)(2,1)S(1)}, u32[]{:S(2)}, u32[]{:S(2)}) collective-permute-start(bf16[40,2048]{1,0:T(8,128)(2,1)S(1)} %get-tuple-element.49.refs_7_), channel_id=1, source_target_pairs={{0,96},{4,100},{8,104},{12,108},{16,112},{20,116},{24,120},{28,124... | collective-permute-start | bytes 491528 | tf_op jit(solution)/shard_map/ppermute | solution.py:409
  37.3 2.1 %collective-permute-done.11.refs_5_ = bf16[40,2048]{1,0:T(8,128)(2,1)S(1)} collective-permute-done((bf16[40,2048]{1,0:T(8,128)(2,1)S(1)}, bf16[40,2048]{1,0:T(8,128)(2,1)S(1)}, u32[]{:S(2)}, u32[]{:S(2)}) %collective-permute-start.11) | collective-permute-done | bytes 163872 | tf_op jit(solution)/shard_map/ppermute | solution.py:409
  39.4 2.2 %collective-permute-done.7.refs_1_ = bf16[40,2048]{1,0:T(8,128)(2,1)S(1)} collective-permute-done((bf16[40,2048]{1,0:T(8,128)(2,1)S(1)}, bf16[40,2048]{1,0:T(8,128)(2,1)S(1)}, u32[]{:S(2)}, u32[]{:S(2)}) %collective-permute-start.7) | collective-permute-done | bytes 163872 | tf_op jit(solution)/shard_map/ppermute | solution.py:409
  43.4 2.3 %pick_rows.1 = (bf16[64,2048]{1,0:T(8,128)(2,1)S(1)}, bf16[64,2048]{1,0:T(8,128)(2,1)S(1)}, bf16[64,2048]{1,0:T(8,128)(2,1)S(1)}, bf16[64,2048]{1,0:T(8,128)(2,1...) custom-call(s32[4]{0:T(128)S(1)} %pad_add_fusion.place, ...), custom_call_target="tpu_custom_call" | custom-call | tf_op jit(solution)/shard_map/pick_rows/pallas_call | solution.py:235
  45.7 1.6 collective-permute-start.12
  47.3 1.9 %collective-permute-start.13 = (bf16[64,2048]{1,0:T(8,128)(2,1)S(1)}, bf16[64,2048]{1,0:T(8,128)(2,1)S(1)}, u32[]{:S(2)}, u32[]{:S(2)}) collective-permute-start(bf16[64,2048]{1,0:T(8,128)(2,1)S(1)} %get-tuple-element.51), channel_id=1, source_target_pairs={{0,16},{4,20},{8,24},{12,28},{16,0},{20,4},{24,8},{28,12},{32,48},... | collective-permute-start | bytes 786440 | tf_op jit(solution)/shard_map/ppermute | solution.py:409
  49.1 3.4 %collective-permute-start.15 = (bf16[64,2048]{1,0:T(8,128)(2,1)S(1)}, bf16[64,2048]{1,0:T(8,128)(2,1)S(1)}, u32[]{:S(2)}, u32[]{:S(2)}) collective-permute-start(bf16[64,2048]{1,0:T(8,128)(2,1)S(1)} %get-tuple-element.53), channel_id=1, source_target_pairs={{0,20},{4,16},{8,28},{12,24},{16,4},{20,0},{24,12},{28,8},{32,52},... | collective-permute-start | bytes 786440 | tf_op jit(solution)/shard_map/ppermute | solution.py:409
  54.9 1.6 %collective-permute-done.13.refs_1_ = bf16[64,2048]{1,0:T(8,128)(2,1)S(1)} collective-permute-done((bf16[64,2048]{1,0:T(8,128)(2,1)S(1)}, bf16[64,2048]{1,0:T(8,128)(2,1)S(1)}, u32[]{:S(2)}, u32[]{:S(2)}) %collective-permute-start.13) | collective-permute-done | bytes 262176 | tf_op jit(solution)/shard_map/ppermute | solution.py:409
  57.1 2.3 %collective-permute-done.14.refs_2_ = bf16[64,2048]{1,0:T(8,128)(2,1)S(1)} collective-permute-done((bf16[64,2048]{1,0:T(8,128)(2,1)S(1)}, bf16[64,2048]{1,0:T(8,128)(2,1)S(1)}, u32[]{:S(2)}, u32[]{:S(2)}) %collective-permute-start.14) | collective-permute-done | bytes 262176 | tf_op jit(solution)/shard_map/ppermute | solution.py:409
  59.4 2.3 %collective-permute-start.19 = (bf16[64,2048]{1,0:T(8,128)(2,1)S(1)}, bf16[64,2048]{1,0:T(8,128)(2,1)S(1)}, u32[]{:S(2)}, u32[]{:S(2)}) collective-permute-start(bf16[64,2048]{1,0:T(8,128)(2,1)S(1)} %get-tuple-element.57), channel_id=1, source_target_pairs={{0,24},{4,28},{8,0},{12,4},{16,8},{20,12},{24,16},{28,20},{32,56},... | collective-permute-start | bytes 786440 | tf_op jit(solution)/shard_map/ppermute | solution.py:409
  62.3 2.6 %collective-permute-done.16.refs_4_ = bf16[64,2048]{1,0:T(8,128)(2,1)S(1)} collective-permute-done((bf16[64,2048]{1,0:T(8,128)(2,1)S(1)}, bf16[64,2048]{1,0:T(8,128)(2,1)S(1)}, u32[]{:S(2)}, u32[]{:S(2)}) %collective-permute-start.16) | collective-permute-done | bytes 262176 | tf_op jit(solution)/shard_map/ppermute | solution.py:409
  66.5 1.6 %collective-permute-start.23 = (bf16[64,2048]{1,0:T(8,128)(2,1)S(1)}, bf16[64,2048]{1,0:T(8,128)(2,1)S(1)}, u32[]{:S(2)}, u32[]{:S(2)}) collective-permute-start(bf16[64,2048]{1,0:T(8,128)(2,1)S(1)} %get-tuple-element.61), channel_id=1, source_target_pairs={{0,28},{4,24},{8,4},{12,0},{16,12},{20,8},{24,20},{28,16},{32,60},... | collective-permute-start | bytes 786440 | tf_op jit(solution)/shard_map/ppermute | solution.py:409
  68.6 2.0 %collective-permute-done.20.refs_8_ = bf16[64,2048]{1,0:T(8,128)(2,1)S(1)} collective-permute-done((bf16[64,2048]{1,0:T(8,128)(2,1)S(1)}, bf16[64,2048]{1,0:T(8,128)(2,1)S(1)}, u32[]{:S(2)}, u32[]{:S(2)}) %collective-permute-start.20) | collective-permute-done | bytes 262176 | tf_op jit(solution)/shard_map/ppermute | solution.py:409
  70.6 1.5 collective-permute-start.30
  72.1 2.4 %collective-permute-done.21.refs_9_ = bf16[64,2048]{1,0:T(8,128)(2,1)S(1)} collective-permute-done((bf16[64,2048]{1,0:T(8,128)(2,1)S(1)}, bf16[64,2048]{1,0:T(8,128)(2,1)S(1)}, u32[]{:S(2)}, u32[]{:S(2)}) %collective-permute-start.21) | collective-permute-done | bytes 262176 | tf_op jit(solution)/shard_map/ppermute | solution.py:409
  74.5 1.8 %collective-permute-start.31 = (bf16[2,256,1024]{2,1,0:T(8,128)(2,1)S(1)}, bf16[2,256,1024]{2,1,0:T(8,128)(2,1)S(1)}, u32[]{:S(2)}, u32[]{:S(2)}) collective-permute-start(bf16[2,256,1024]{2,1,0:T(8,128)(2,1)S(1)} %get-tuple-element.70), channel_id=1, source_target_pairs={{0,3},{1,0},{2,1},{3,2},{4,7},{5,4},{6,5},{7,6},{8,11},{9,8},{10,9... | collective-permute-start | bytes 3145736 | tf_op jit(solution)/shard_map/ppermute | solution.py:399
  76.8 3.5 %load.1 = (bf16[2,4096,256]{2,1,0:T(8,128)(2,1)S(1)}, bf16[2,4096,256]{2,1,0:T(8,128)(2,1)S(1)}) custom-call(bf16[2,4096,256]{2,1,0:T(8,128)(2,1)} %refs_0_.1, bf16[2,4096,256]{2,1,0:T(8,128)(2,1)} %refs_1_.1), custom_call_target="tpu_custom_call" | custom-call | tf_op jit(solution)/shard_map/load/pallas_call | solution.py:261
  80.3 3.1 %gate_up.1.refs_0_ = bf16[2,256,256]{2,1,0:T(8,128)(2,1)S(1)} custom-call(s32[4]{0:T(128)S(1)} %pad_add_fusion.place, bf16[64,2048]{1,0:T(8,128)(2,1)S(1)} %collective-permute-done.12.refs_0_, bf16[64,2048]{1,0:T(8,128)(2,1)S(1)} %collective-permute-done.13.refs_1_, bf16[64,2048]{1,0:T(8,128)(2,1)S(1)} %collective-permute-done.14.refs_2_, ...), custom_call_target="tpu_custom_call" | custom-call | tf_op jit(solution)/shard_map/gate_up/pallas_call | solution.py:348
  83.8 1.5 collective-permute-start.27
  85.3 38.2 %collective-permute-done.26.refs_1_ = bf16[2,256,256]{2,1,0:T(8,128)(2,1)S(1)} collective-permute-done((bf16[2,256,256]{2,1,0:T(8,128)(2,1)S(1)}, bf16[2,256,256]{2,1,0:T(8,128)(2,1)S(1)}, u32[]{:S(2)}, u32[]{:S(2)}) %collective-permute-start.26) | collective-permute-done | bytes 262176 | tf_op jit(solution)/shard_map/ppermute | solution.py:399
  124.1 4.5 %collective-permute-done.27.refs_2_ = bf16[2,256,256]{2,1,0:T(8,128)(2,1)S(1)} collective-permute-done((bf16[2,256,256]{2,1,0:T(8,128)(2,1)S(1)}, bf16[2,256,256]{2,1,0:T(8,128)(2,1)S(1)}, u32[]{:S(2)}, u32[]{:S(2)}) %collective-permute-start.27) | collective-permute-done | bytes 262176 | tf_op jit(solution)/shard_map/ppermute | solution.py:399
  128.6 2.3 %collective-permute-done.28.refs_3_ = bf16[2,256,256]{2,1,0:T(8,128)(2,1)S(1)} collective-permute-done((bf16[2,256,256]{2,1,0:T(8,128)(2,1)S(1)}, bf16[2,256,256]{2,1,0:T(8,128)(2,1)S(1)}, u32[]{:S(2)}, u32[]{:S(2)}) %collective-permute-start.28) | collective-permute-done | bytes 262176 | tf_op jit(solution)/shard_map/ppermute | solution.py:399
  131.0 3.9 %down.1 = bf16[32,16,1024]{2,1,0:T(8,128)(2,1)} custom-call(s32[4]{0:T(128)S(1)} %pad_add_fusion.place, bf16[2,256,256]{2,1,0:T(8,128)(2,1)S(1)} %gate_up.1.refs_0_, bf16[2,256,256]{2,1,0:T(8,128)(2,1)S(1)} %collective-permute-done.26.refs_1_, bf16[2,256,256]{2,1,0:T(8,128)(2,1)S(1)} %collective-permute-done.27.refs_2_, ...), custom_call_target="tpu_custom_call" | custom-call | tf_op jit(solution)/shard_map/down/pallas_call | solution.py:371
  134.8 5.5 %all-to-all-start = ((bf16[32,16,1024]{2,1,0:T(8,128)(2,1)}), bf16[32,16,1024]{2,1,0:T(8,128)(2,1)S(1)}, u32[]{:S(2)}, u32[]{:S(2)}) async-start(bf16[32,16,1024]{2,1,0:T(8,128)(2,1)} %down.1), calls=%async_computation | async-start | bytes 2097152 | tf_op jit(solution)/shard_map/all_to_all | solution.py:471
  141.1 16.4 %all-to-all-done = bf16[32,16,1024]{2,1,0:T(8,128)(2,1)S(1)} async-done(((bf16[32,16,1024]{2,1,0:T(8,128)(2,1)}), bf16[32,16,1024]{2,1,0:T(8,128)(2,1)S(1)}, u32[]{:S(2)}, u32[]{:S(2)}) %all-to-all-start) | async-done | bytes 1048608 | tf_op jit(solution)/shard_map/all_to_all | solution.py:471
  (61 shorter events, 21.5 us)
Async XLA Ops:
  7.6 9.1 %collective-permute-start = (bf16[32,1024]{1,0:T(8,128)(2,1)S(1)}, bf16[32,1024]{1,0:T(8,128)(2,1)}, u32[]{:S(2)}, u32[]{:S(2)}) collective-permute-start(bf16[32,1024]{1,0:T(8,128)(2,1)S(1)} %get-tuple-element.39), channel_id=1, source_target_pairs={{0,1},{1,2},{2,3},{3,0},{4,5},{5,6},{6,7},{7,4},{8,9},{9,10},{10,1... | collective-permute-start | bytes 196616 | tf_op jit(solution)/shard_map/ppermute | solution.py:399
  9.7 7.1 %collective-permute-start.1 = (bf16[32,1024]{1,0:T(8,128)(2,1)S(1)}, bf16[32,1024]{1,0:T(8,128)(2,1)}, u32[]{:S(2)}, u32[]{:S(2)}) collective-permute-start(bf16[32,1024]{1,0:T(8,128)(2,1)S(1)} %get-tuple-element.40), channel_id=1, source_target_pairs={{0,2},{1,3},{2,0},{3,1},{4,6},{5,7},{6,4},{7,5},{8,10},{9,11},{10,... | collective-permute-start | bytes 196616 | tf_op jit(solution)/shard_map/ppermute | solution.py:399
  13.3 4.4 %collective-permute-start.2 = (bf16[32,1024]{1,0:T(8,128)(2,1)S(1)}, bf16[32,1024]{1,0:T(8,128)(2,1)}, u32[]{:S(2)}, u32[]{:S(2)}) collective-permute-start(bf16[32,1024]{1,0:T(8,128)(2,1)S(1)} %get-tuple-element.41), channel_id=1, source_target_pairs={{0,3},{1,0},{2,1},{3,2},{4,7},{5,4},{6,5},{7,6},{8,11},{9,8},{10,9... | collective-permute-start | bytes 196616 | tf_op jit(solution)/shard_map/ppermute | solution.py:399
  19.3 5.7 %collective-permute-start.3 = (bf16[32,1024]{1,0:T(8,128)(2,1)}, bf16[32,1024]{1,0:T(8,128)(2,1)S(1)}, u32[]{:S(2)}, u32[]{:S(2)}) collective-permute-start(bf16[32,1024]{1,0:T(8,128)(2,1)} %get-tuple-element.71), channel_id=1, source_target_pairs={{0,1},{1,2},{2,3},{3,0},{4,5},{5,6},{6,7},{7,4},{8,9},{9,10},{10,1... | collective-permute-start | bytes 196616 | tf_op jit(solution)/shard_map/ppermute | solution.py:399
  19.5 6.6 %collective-permute-start.4 = (bf16[32,1024]{1,0:T(8,128)(2,1)}, bf16[32,1024]{1,0:T(8,128)(2,1)S(1)}, u32[]{:S(2)}, u32[]{:S(2)}) collective-permute-start(bf16[32,1024]{1,0:T(8,128)(2,1)} %get-tuple-element.71), channel_id=1, source_target_pairs={{0,2},{1,3},{2,0},{3,1},{4,6},{5,7},{6,4},{7,5},{8,10},{9,11},{10,... | collective-permute-start | bytes 196616 | tf_op jit(solution)/shard_map/ppermute | solution.py:399
  23.0 4.5 %collective-permute-start.5 = (bf16[32,1024]{1,0:T(8,128)(2,1)}, bf16[32,1024]{1,0:T(8,128)(2,1)S(1)}, u32[]{:S(2)}, u32[]{:S(2)}) collective-permute-start(bf16[32,1024]{1,0:T(8,128)(2,1)} %get-tuple-element.71), channel_id=1, source_target_pairs={{0,3},{1,0},{2,1},{3,2},{4,7},{5,4},{6,5},{7,6},{8,11},{9,8},{10,9... | collective-permute-start | bytes 196616 | tf_op jit(solution)/shard_map/ppermute | solution.py:399
  28.2 8.2 %collective-permute-start.10 = (bf16[40,2048]{1,0:T(8,128)(2,1)S(1)}, bf16[40,2048]{1,0:T(8,128)(2,1)S(1)}, u32[]{:S(2)}, u32[]{:S(2)}) collective-permute-start(bf16[40,2048]{1,0:T(8,128)(2,1)S(1)} %get-tuple-element.48.refs_6_), channel_id=1, source_target_pairs={{0,24},{4,28},{8,0},{12,4},{16,8},{20,12},{24,16},{28,20},{32,56},... | collective-permute-start | bytes 491528 | tf_op jit(solution)/shard_map/ppermute | solution.py:409
  31.0 8.4 %collective-permute-start.6 = (bf16[40,2048]{1,0:T(8,128)(2,1)S(1)}, bf16[40,2048]{1,0:T(8,128)(2,1)S(1)}, u32[]{:S(2)}, u32[]{:S(2)}) collective-permute-start(bf16[40,2048]{1,0:T(8,128)(2,1)S(1)} %get-tuple-element.48.refs_6_), channel_id=1, source_target_pairs={{0,16},{4,20},{8,24},{12,28},{16,0},{20,4},{24,8},{28,12},{32,48},... | collective-permute-start | bytes 491528 | tf_op jit(solution)/shard_map/ppermute | solution.py:409
  31.8 7.6 %collective-permute-start.11 = (bf16[40,2048]{1,0:T(8,128)(2,1)S(1)}, bf16[40,2048]{1,0:T(8,128)(2,1)S(1)}, u32[]{:S(2)}, u32[]{:S(2)}) collective-permute-start(bf16[40,2048]{1,0:T(8,128)(2,1)S(1)} %get-tuple-element.49.refs_7_), channel_id=1, source_target_pairs={{0,96},{4,100},{8,104},{12,108},{16,112},{20,116},{24,120},{28,124... | collective-permute-start | bytes 491528 | tf_op jit(solution)/shard_map/ppermute | solution.py:409
  34.8 6.9 %collective-permute-start.7 = (bf16[40,2048]{1,0:T(8,128)(2,1)S(1)}, bf16[40,2048]{1,0:T(8,128)(2,1)S(1)}, u32[]{:S(2)}, u32[]{:S(2)}) collective-permute-start(bf16[40,2048]{1,0:T(8,128)(2,1)S(1)} %get-tuple-element.49.refs_7_), channel_id=1, source_target_pairs={{0,64},{4,68},{8,72},{12,76},{16,80},{20,84},{24,88},{28,92},{32,9... | collective-permute-start | bytes 491528 | tf_op jit(solution)/shard_map/ppermute | solution.py:409
  35.4 6.5 %collective-permute-start.8 = (bf16[40,2048]{1,0:T(8,128)(2,1)S(1)}, bf16[40,2048]{1,0:T(8,128)(2,1)S(1)}, u32[]{:S(2)}, u32[]{:S(2)}) collective-permute-start(bf16[40,2048]{1,0:T(8,128)(2,1)S(1)} %get-tuple-element.48.refs_6_), channel_id=1, source_target_pairs={{0,8},{4,12},{8,16},{12,20},{16,24},{20,28},{24,0},{28,4},{32,40},... | collective-permute-start | bytes 491528 | tf_op jit(solution)/shard_map/ppermute | solution.py:409
  36.3 7.1 %collective-permute-start.9 = (bf16[40,2048]{1,0:T(8,128)(2,1)S(1)}, bf16[40,2048]{1,0:T(8,128)(2,1)S(1)}, u32[]{:S(2)}, u32[]{:S(2)}) collective-permute-start(bf16[40,2048]{1,0:T(8,128)(2,1)S(1)} %get-tuple-element.49.refs_7_), channel_id=1, source_target_pairs={{0,32},{4,36},{8,40},{12,44},{16,48},{20,52},{24,56},{28,60},{32,6... | collective-permute-start | bytes 491528 | tf_op jit(solution)/shard_map/ppermute | solution.py:409
  45.7 8.0 %collective-permute-start.12 = (bf16[64,2048]{1,0:T(8,128)(2,1)S(1)}, bf16[64,2048]{1,0:T(8,128)(2,1)S(1)}, u32[]{:S(2)}, u32[]{:S(2)}) collective-permute-start(bf16[64,2048]{1,0:T(8,128)(2,1)S(1)} %get-tuple-element.50), channel_id=1, source_target_pairs={{0,64},{4,68},{8,72},{12,76},{16,80},{20,84},{24,88},{28,92},{32,9... | collective-permute-start | bytes 786440 | tf_op jit(solution)/shard_map/ppermute | solution.py:409
  47.3 9.3 %collective-permute-start.13 = (bf16[64,2048]{1,0:T(8,128)(2,1)S(1)}, bf16[64,2048]{1,0:T(8,128)(2,1)S(1)}, u32[]{:S(2)}, u32[]{:S(2)}) collective-permute-start(bf16[64,2048]{1,0:T(8,128)(2,1)S(1)} %get-tuple-element.51), channel_id=1, source_target_pairs={{0,16},{4,20},{8,24},{12,28},{16,0},{20,4},{24,8},{28,12},{32,48},... | collective-permute-start | bytes 786440 | tf_op jit(solution)/shard_map/ppermute | solution.py:409
  49.1 10.2 %collective-permute-start.14 = (bf16[64,2048]{1,0:T(8,128)(2,1)S(1)}, bf16[64,2048]{1,0:T(8,128)(2,1)S(1)}, u32[]{:S(2)}, u32[]{:S(2)}) collective-permute-start(bf16[64,2048]{1,0:T(8,128)(2,1)S(1)} %get-tuple-element.52), channel_id=1, source_target_pairs={{0,68},{4,64},{8,76},{12,72},{16,84},{20,80},{24,92},{28,88},{32,1... | collective-permute-start | bytes 786440 | tf_op jit(solution)/shard_map/ppermute | solution.py:409
  49.1 12.5 %collective-permute-start.15 = (bf16[64,2048]{1,0:T(8,128)(2,1)S(1)}, bf16[64,2048]{1,0:T(8,128)(2,1)S(1)}, u32[]{:S(2)}, u32[]{:S(2)}) collective-permute-start(bf16[64,2048]{1,0:T(8,128)(2,1)S(1)} %get-tuple-element.53), channel_id=1, source_target_pairs={{0,20},{4,16},{8,28},{12,24},{16,4},{20,0},{24,12},{28,8},{32,52},... | collective-permute-start | bytes 786440 | tf_op jit(solution)/shard_map/ppermute | solution.py:409
  52.6 12.3 %collective-permute-start.16 = (bf16[64,2048]{1,0:T(8,128)(2,1)S(1)}, bf16[64,2048]{1,0:T(8,128)(2,1)S(1)}, u32[]{:S(2)}, u32[]{:S(2)}) collective-permute-start(bf16[64,2048]{1,0:T(8,128)(2,1)S(1)} %get-tuple-element.54), channel_id=1, source_target_pairs={{0,32},{4,36},{8,40},{12,44},{16,48},{20,52},{24,56},{28,60},{32,6... | collective-permute-start | bytes 786440 | tf_op jit(solution)/shard_map/ppermute | solution.py:409
  53.7 12.7 %collective-permute-start.17 = (bf16[64,2048]{1,0:T(8,128)(2,1)S(1)}, bf16[64,2048]{1,0:T(8,128)(2,1)S(1)}, u32[]{:S(2)}, u32[]{:S(2)}) collective-permute-start(bf16[64,2048]{1,0:T(8,128)(2,1)S(1)} %get-tuple-element.55), channel_id=1, source_target_pairs={{0,8},{4,12},{8,16},{12,20},{16,24},{20,28},{24,0},{28,4},{32,40},... | collective-permute-start | bytes 786440 | tf_op jit(solution)/shard_map/ppermute | solution.py:409
  56.5 10.0 %collective-permute-start.18 = (bf16[64,2048]{1,0:T(8,128)(2,1)S(1)}, bf16[64,2048]{1,0:T(8,128)(2,1)S(1)}, u32[]{:S(2)}, u32[]{:S(2)}) collective-permute-start(bf16[64,2048]{1,0:T(8,128)(2,1)S(1)} %get-tuple-element.56), channel_id=1, source_target_pairs={{0,96},{4,100},{8,104},{12,108},{16,112},{20,116},{24,120},{28,124... | collective-permute-start | bytes 786440 | tf_op jit(solution)/shard_map/ppermute | solution.py:409
  59.4 8.8 %collective-permute-start.19 = (bf16[64,2048]{1,0:T(8,128)(2,1)S(1)}, bf16[64,2048]{1,0:T(8,128)(2,1)S(1)}, u32[]{:S(2)}, u32[]{:S(2)}) collective-permute-start(bf16[64,2048]{1,0:T(8,128)(2,1)S(1)} %get-tuple-element.57), channel_id=1, source_target_pairs={{0,24},{4,28},{8,0},{12,4},{16,8},{20,12},{24,16},{28,20},{32,56},... | collective-permute-start | bytes 786440 | tf_op jit(solution)/shard_map/ppermute | solution.py:409
  61.6 9.0 %collective-permute-start.20 = (bf16[64,2048]{1,0:T(8,128)(2,1)S(1)}, bf16[64,2048]{1,0:T(8,128)(2,1)S(1)}, u32[]{:S(2)}, u32[]{:S(2)}) collective-permute-start(bf16[64,2048]{1,0:T(8,128)(2,1)S(1)} %get-tuple-element.58), channel_id=1, source_target_pairs={{0,36},{4,32},{8,44},{12,40},{16,52},{20,48},{24,60},{28,56},{32,6... | collective-permute-start | bytes 786440 | tf_op jit(solution)/shard_map/ppermute | solution.py:409
  64.9 9.6 %collective-permute-start.21 = (bf16[64,2048]{1,0:T(8,128)(2,1)S(1)}, bf16[64,2048]{1,0:T(8,128)(2,1)S(1)}, u32[]{:S(2)}, u32[]{:S(2)}) collective-permute-start(bf16[64,2048]{1,0:T(8,128)(2,1)S(1)} %get-tuple-element.59), channel_id=1, source_target_pairs={{0,12},{4,8},{8,20},{12,16},{16,28},{20,24},{24,4},{28,0},{32,44},... | collective-permute-start | bytes 786440 | tf_op jit(solution)/shard_map/ppermute | solution.py:409
  66.4 9.9 %collective-permute-start.22 = (bf16[64,2048]{1,0:T(8,128)(2,1)S(1)}, bf16[64,2048]{1,0:T(8,128)(2,1)S(1)}, u32[]{:S(2)}, u32[]{:S(2)}) collective-permute-start(bf16[64,2048]{1,0:T(8,128)(2,1)S(1)} %get-tuple-element.60), channel_id=1, source_target_pairs={{0,100},{4,96},{8,108},{12,104},{16,116},{20,112},{24,124},{28,120... | collective-permute-start | bytes 786440 | tf_op jit(solution)/shard_map/ppermute | solution.py:409
  66.5 9.8 %collective-permute-start.23 = (bf16[64,2048]{1,0:T(8,128)(2,1)S(1)}, bf16[64,2048]{1,0:T(8,128)(2,1)S(1)}, u32[]{:S(2)}, u32[]{:S(2)}) collective-permute-start(bf16[64,2048]{1,0:T(8,128)(2,1)S(1)} %get-tuple-element.61), channel_id=1, source_target_pairs={{0,28},{4,24},{8,4},{12,0},{16,12},{20,8},{24,20},{28,16},{32,60},... | collective-permute-start | bytes 786440 | tf_op jit(solution)/shard_map/ppermute | solution.py:409
  68.2 62.8 %collective-permute-start.29 = (bf16[2,256,1024]{2,1,0:T(8,128)(2,1)S(1)}, bf16[2,256,1024]{2,1,0:T(8,128)(2,1)S(1)}, u32[]{:S(2)}, u32[]{:S(2)}) collective-permute-start(bf16[2,256,1024]{2,1,0:T(8,128)(2,1)S(1)} %get-tuple-element.68), channel_id=1, source_target_pairs={{0,1},{1,2},{2,3},{3,0},{4,5},{5,6},{6,7},{7,4},{8,9},{9,10},{10,1... | collective-permute-start | bytes 3145736 | tf_op jit(solution)/shard_map/ppermute | solution.py:399
  70.6 60.4 %collective-permute-start.30 = (bf16[2,256,1024]{2,1,0:T(8,128)(2,1)S(1)}, bf16[2,256,1024]{2,1,0:T(8,128)(2,1)S(1)}, u32[]{:S(2)}, u32[]{:S(2)}) collective-permute-start(bf16[2,256,1024]{2,1,0:T(8,128)(2,1)S(1)} %get-tuple-element.69), channel_id=1, source_target_pairs={{0,2},{1,3},{2,0},{3,1},{4,6},{5,7},{6,4},{7,5},{8,10},{9,11},{10,... | collective-permute-start | bytes 3145736 | tf_op jit(solution)/shard_map/ppermute | solution.py:399
  74.5 56.5 %collective-permute-start.31 = (bf16[2,256,1024]{2,1,0:T(8,128)(2,1)S(1)}, bf16[2,256,1024]{2,1,0:T(8,128)(2,1)S(1)}, u32[]{:S(2)}, u32[]{:S(2)}) collective-permute-start(bf16[2,256,1024]{2,1,0:T(8,128)(2,1)S(1)} %get-tuple-element.70), channel_id=1, source_target_pairs={{0,3},{1,0},{2,1},{3,2},{4,7},{5,4},{6,5},{7,6},{8,11},{9,8},{10,9... | collective-permute-start | bytes 3145736 | tf_op jit(solution)/shard_map/ppermute | solution.py:399
  76.3 4.0 %collective-permute-start.25 = (bf16[64,2048]{1,0:T(8,128)(2,1)S(1)}, bf16[64,2048]{1,0:T(8,128)(2,1)S(1)}, u32[]{:S(2)}, u32[]{:S(2)}) collective-permute-start(bf16[64,2048]{1,0:T(8,128)(2,1)S(1)} %get-tuple-element.63), channel_id=1, source_target_pairs={{0,4},{4,0},{8,12},{12,8},{16,20},{20,16},{24,28},{28,24},{32,36},... | collective-permute-start | bytes 786440 | tf_op jit(solution)/shard_map/ppermute | solution.py:409
  83.4 40.0 %collective-permute-start.26 = (bf16[2,256,256]{2,1,0:T(8,128)(2,1)S(1)}, bf16[2,256,256]{2,1,0:T(8,128)(2,1)S(1)}, u32[]{:S(2)}, u32[]{:S(2)}) collective-permute-start(bf16[2,256,256]{2,1,0:T(8,128)(2,1)S(1)} %gate_up.1.refs_0_), channel_id=1, source_target_pairs={{0,1},{1,2},{2,3},{3,0},{4,5},{5,6},{6,7},{7,4},{8,9},{9,10},{10,1... | collective-permute-start | bytes 786440 | tf_op jit(solution)/shard_map/ppermute | solution.py:399
  83.8 44.9 %collective-permute-start.27 = (bf16[2,256,256]{2,1,0:T(8,128)(2,1)S(1)}, bf16[2,256,256]{2,1,0:T(8,128)(2,1)S(1)}, u32[]{:S(2)}, u32[]{:S(2)}) collective-permute-start(bf16[2,256,256]{2,1,0:T(8,128)(2,1)S(1)} %gate_up.1.refs_0_), channel_id=1, source_target_pairs={{0,2},{1,3},{2,0},{3,1},{4,6},{5,7},{6,4},{7,5},{8,10},{9,11},{10,... | collective-permute-start | bytes 786440 | tf_op jit(solution)/shard_map/ppermute | solution.py:399
  123.5 7.5 %collective-permute-start.28 = (bf16[2,256,256]{2,1,0:T(8,128)(2,1)S(1)}, bf16[2,256,256]{2,1,0:T(8,128)(2,1)S(1)}, u32[]{:S(2)}, u32[]{:S(2)}) collective-permute-start(bf16[2,256,256]{2,1,0:T(8,128)(2,1)S(1)} %gate_up.1.refs_0_), channel_id=1, source_target_pairs={{0,3},{1,0},{2,1},{3,2},{4,7},{5,4},{6,5},{7,6},{8,11},{9,8},{10,9... | collective-permute-start | bytes 786440 | tf_op jit(solution)/shard_map/ppermute | solution.py:399
  134.8 22.7 %all-to-all-start = ((bf16[32,16,1024]{2,1,0:T(8,128)(2,1)}), bf16[32,16,1024]{2,1,0:T(8,128)(2,1)S(1)}, u32[]{:S(2)}, u32[]{:S(2)}) async-start(bf16[32,16,1024]{2,1,0:T(8,128)(2,1)} %down.1), calls=%async_computation | async-start | bytes 2097152 | tf_op jit(solution)/shard_map/all_to_all | solution.py:471
  (4 other events, 97.0 us)

commit v3 on v2

--- a/solution.py
+++ b/solution.py
@@ -267,36 +267,6 @@
         compiler_params=pltpu.CompilerParams(vmem_limit_bytes=1 << 20),
         name="load",
     )(*[in_hbm(value) for value in values])
-
-
-def cut_kernel(place, source, *refs):
-    *targets, sems = refs
-    groups = len(targets) + 1
-    share = targets[0].shape[2]
-    copies = []
-    for ahead, target in enumerate(targets, 1):
-        column = pl.multiple_of(lax.rem(place[HEAD] + ahead, groups) * share, share)
-        copies.append(
-            pltpu.make_async_copy(source.at[:, :, pl.ds(column, share)], target, sems.at[ahead - 1])
-        )
-    for copy in copies:
-        copy.start()
-    for copy in copies:
-        copy.wait()
-
-
-def cut_columns(value, place, groups):
-    experts, depth, width = value.shape
-    shape = (experts, depth, width // groups)
-    return pl.pallas_call(
-        cut_kernel,
-        out_shape=[pltpu.VMEM(shape, value.dtype)] * (groups - 1),
-        in_specs=[pl.BlockSpec(memory_space=pltpu.SMEM), pl.BlockSpec(memory_space=pl.ANY)],
-        out_specs=[pl.BlockSpec(memory_space=pltpu.VMEM)] * (groups - 1),
-        scratch_shapes=[pltpu.SemaphoreType.DMA((groups - 1,))],
-        compiler_params=pltpu.CompilerParams(vmem_limit_bytes=8 << 20),
-        name="cut_columns",
-    )(place, in_hbm(value))
 
 
 def gate_up_kernel(place, *refs):
@@ -447,7 +417,10 @@
     take_high = take.astype(BF16)
     take_low = (take - take_high.astype(F32)).astype(BF16)
     ids = jnp.tile(expert_ids.T.astype(BF16), (1, 128 // rows))
-    columns = cut_columns(w_down, place, groups)
+    columns = [
+        lax.dynamic_slice_in_dim(w_down, lax.rem(head + step, groups) * share, share, 2)
+        for step in steps
+    ]
     others, columns = lax.optimization_barrier((others, columns))
     hidden = lax.dynamic_slice_in_dim(x_rows, head * share, share, 1).astype(F32) + own
     for other in others:

time: 160 us -> 160 us (level)
  local copies, waits for them, and re-layouts: 0.45 us -> 2.88 us
  Pallas kernels: 23.4 us -> 21 us
    pallas_call x1 -> x0, Pallas kernels: 2.44 us -> none  [cut_columns(): pl.pallas_call(cut_kernel, out_shape=[pltpu.VMEM(shape, value.dtype)] * (...]
    dynamic_slice x0 -> x1, local copies, waits for them, and re-layouts: none -> 2.43 us  [body(): lax.dynamic_slice_in_dim(w_down, lax.rem(head + step, groups) * share, sh...]
  transfers between devices with their start and end apart: 33 -> 33, of which waited for: 19 -> 19; matrix products, arithmetic and copies ran while one was open for 1% -> 2% of each run, Pallas kernels for 6% -> 4%
where the time goes in v3:
time: 160 us; the launch traced here: 159 us
  waiting for transfers between devices  85 us (53%)
  starting transfers between devices  46.4 us (29%)
  Pallas kernels  21 us (13%)
  local copies, waits for them, and re-layouts  2.88 us (2%)
  other arithmetic  2.1 us (1%)
    ppermute x12, waiting for transfers between devices, turned(): lax.ppermute(value, 'head', [(i, (i + step) % groups) for i in range(grou...  49.9 us
    ppermute x20, starting transfers between devices, moved_in_plane(): return lax.ppermute(value, 'pool', pairs)  24 us
    ppermute x20, waiting for transfers between devices, moved_in_plane(): return lax.ppermute(value, 'pool', pairs)  18.7 us
    ppermute x12, starting transfers between devices, turned(): lax.ppermute(value, 'head', [(i, (i + step) % groups) for i in range(grou...  17 us
    all_to_all x1, waiting for transfers between devices, body(): lax.all_to_all(produced, 'pool', split_axis=0, concat_axis=0, tiled=True)  16.4 us
    pallas_call x1, Pallas kernels, attend_project(): pl.pallas_call(attend_kernel, out_shape=[jax.ShapeDtypeStruct((rows, shar...  7.52 us
    all_to_all x1, starting transfers between devices, body(): lax.all_to_all(produced, 'pool', split_axis=0, concat_axis=0, tiled=True)  5.48 us
    pallas_call x1, Pallas kernels, down(): pl.pallas_call(down_kernel, out_shape=jax.ShapeDtypeStruct((pools, expert...  3.86 us
  transfers between devices with their start and end apart: 33, of which 19 were waited for; matrix products, arithmetic and copies ran while one was open for 2% of the time, Pallas kernels for 4%

profile of v3, /device:TPU:0, one launch (start us, length us, event | category | flops | bytes accessed | tf_op | source)
XLA Modules:
  0.0 158.8 jit_solution(16336743222360294338)
XLA Ops:
  0.1 7.5 %attend_project.1 = (f32[32,1024]{1,0:T(8,128)S(1)}, bf16[32,1024]{1,0:T(8,128)(2,1)S(1)}, bf16[32,1024]{1,0:T(8,128)(2,1)S(1)}, bf16[32,1024]{1,0:T(8,128)(2,1)S(1)}) custom-call(s32[32]{0:T(128)} %lengths.1, s32[4]{0:T(128)S(1)} %pad_add_fusion.place, bf16[32,1024]{1,0:T(8,128)(2,1)} %q_ref.1, bf16[32,1,512,128]{3,2,1,0:T(8,128)(2,1)} %k_hbm.1, ...), custom_call_target="tpu_custom_call" | custom-call | tf_op jit(solution)/shard_map/attend_project/pallas_call | solution.py:126
  7.6 2.1 %collective-permute-start = (bf16[32,1024]{1,0:T(8,128)(2,1)S(1)}, bf16[32,1024]{1,0:T(8,128)(2,1)}, u32[]{:S(2)}, u32[]{:S(2)}) collective-permute-start(bf16[32,1024]{1,0:T(8,128)(2,1)S(1)} %get-tuple-element.36), channel_id=1, source_target_pairs={{0,1},{1,2},{2,3},{3,0},{4,5},{5,6},{6,7},{7,4},{8,9},{9,10},{10,1... | collective-permute-start | bytes 196616 | tf_op jit(solution)/shard_map/ppermute | solution.py:369
  9.7 3.6 %collective-permute-start.1 = (bf16[32,1024]{1,0:T(8,128)(2,1)S(1)}, bf16[32,1024]{1,0:T(8,128)(2,1)}, u32[]{:S(2)}, u32[]{:S(2)}) collective-permute-start(bf16[32,1024]{1,0:T(8,128)(2,1)S(1)} %get-tuple-element.37), channel_id=1, source_target_pairs={{0,2},{1,3},{2,0},{3,1},{4,6},{5,7},{6,4},{7,5},{8,10},{9,11},{10,... | collective-permute-start | bytes 196616 | tf_op jit(solution)/shard_map/ppermute | solution.py:369
  14.3 2.4 %constant_dynamic-slice_fusion = (bf16[2,256,1024]{2,1,0:T(8,128)(2,1)S(1)}, bf16[2,256,1024]{2,1,0:T(8,128)(2,1)S(1)}, bf16[2,256,1024]{2,1,0:T(8,128)(2,1)S(1)}) fusion(bf16[2,256,4096]{2,1,0:T(8,128)(2,1)} %refs_4_.1, s32[]{:T(128)S(6)} %select_n.19, s32[]{:T(128)S(6)} %select_n.18, s32[]{:T(128)S(6)} %select_n.17), kind=kLoop, calls=%fused_computation.15 | loop fusion | bytes 6291468 | tf_op jit(solution)/shard_map/dynamic_slice | solution.py:421
  17.7 1.6 %fusion.7 = (bf16[32,1024]{1,0:T(8,128)(2,1)}, f32[32,1024]{1,0:T(8,128)S(1)}) fusion(bf16[32,1024]{1,0:T(8,128)(2,1)} %collective-permute-done.2, bf16[32,1024]{1,0:T(8,128)(2,1)} %collective-permute-done.1, bf16[32,1024]{1,0:T(8,128)(2,1)} %collective-permute-done, f32[32,1024]{1,0:T(8,128)S(1)} %get-tuple-element.35, bf16[32,4096]{1,0:T(8,128)(2,1)} %param.14, ...), kind=kLoop, calls=%fused_computation.19 | loop fusion | flops 294912 | bytes 589828 | tf_op jit(solution)/shard_map/convert_element_type | solution.py:428
  19.5 3.5 %collective-permute-start.4 = (bf16[32,1024]{1,0:T(8,128)(2,1)}, bf16[32,1024]{1,0:T(8,128)(2,1)S(1)}, u32[]{:S(2)}, u32[]{:S(2)}) collective-permute-start(bf16[32,1024]{1,0:T(8,128)(2,1)} %get-tuple-element.65), channel_id=1, source_target_pairs={{0,2},{1,3},{2,0},{3,1},{4,6},{5,7},{6,4},{7,5},{8,10},{9,11},{10,... | collective-permute-start | bytes 196616 | tf_op jit(solution)/shard_map/ppermute | solution.py:369
  28.2 2.8 %collective-permute-start.10 = (bf16[40,2048]{1,0:T(8,128)(2,1)S(1)}, bf16[40,2048]{1,0:T(8,128)(2,1)S(1)}, u32[]{:S(2)}, u32[]{:S(2)}) collective-permute-start(bf16[40,2048]{1,0:T(8,128)(2,1)S(1)} %get-tuple-element.42.refs_6_), channel_id=1, source_target_pairs={{0,24},{4,28},{8,0},{12,4},{16,8},{20,12},{24,16},{28,20},{32,56},... | collective-permute-start | bytes 491528 | tf_op jit(solution)/shard_map/ppermute | solution.py:379
  31.8 3.0 %collective-permute-start.11 = (bf16[40,2048]{1,0:T(8,128)(2,1)S(1)}, bf16[40,2048]{1,0:T(8,128)(2,1)S(1)}, u32[]{:S(2)}, u32[]{:S(2)}) collective-permute-start(bf16[40,2048]{1,0:T(8,128)(2,1)S(1)} %get-tuple-element.43.refs_7_), channel_id=1, source_target_pairs={{0,96},{4,100},{8,104},{12,108},{16,112},{20,116},{24,120},{28,124... | collective-permute-start | bytes 491528 | tf_op jit(solution)/shard_map/ppermute | solution.py:379
  37.3 2.1 %collective-permute-done.11.refs_5_ = bf16[40,2048]{1,0:T(8,128)(2,1)S(1)} collective-permute-done((bf16[40,2048]{1,0:T(8,128)(2,1)S(1)}, bf16[40,2048]{1,0:T(8,128)(2,1)S(1)}, u32[]{:S(2)}, u32[]{:S(2)}) %collective-permute-start.11) | collective-permute-done | bytes 163872 | tf_op jit(solution)/shard_map/ppermute | solution.py:379
  39.4 2.2 %collective-permute-done.7.refs_1_ = bf16[40,2048]{1,0:T(8,128)(2,1)S(1)} collective-permute-done((bf16[40,2048]{1,0:T(8,128)(2,1)S(1)}, bf16[40,2048]{1,0:T(8,128)(2,1)S(1)}, u32[]{:S(2)}, u32[]{:S(2)}) %collective-permute-start.7) | collective-permute-done | bytes 163872 | tf_op jit(solution)/shard_map/ppermute | solution.py:379
  43.4 2.3 %pick_rows.1 = (bf16[64,2048]{1,0:T(8,128)(2,1)S(1)}, bf16[64,2048]{1,0:T(8,128)(2,1)S(1)}, bf16[64,2048]{1,0:T(8,128)(2,1)S(1)}, bf16[64,2048]{1,0:T(8,128)(2,1...) custom-call(s32[4]{0:T(128)S(1)} %pad_add_fusion.place, ...), custom_call_target="tpu_custom_call" | custom-call | tf_op jit(solution)/shard_map/pick_rows/pallas_call | solution.py:235
  45.7 1.6 collective-permute-start.12
  47.3 1.9 %collective-permute-start.13 = (bf16[64,2048]{1,0:T(8,128)(2,1)S(1)}, bf16[64,2048]{1,0:T(8,128)(2,1)S(1)}, u32[]{:S(2)}, u32[]{:S(2)}) collective-permute-start(bf16[64,2048]{1,0:T(8,128)(2,1)S(1)} %get-tuple-element.45), channel_id=1, source_target_pairs={{0,16},{4,20},{8,24},{12,28},{16,0},{20,4},{24,8},{28,12},{32,48},... | collective-permute-start | bytes 786440 | tf_op jit(solution)/shard_map/ppermute | solution.py:379
  49.1 3.4 %collective-permute-start.15 = (bf16[64,2048]{1,0:T(8,128)(2,1)S(1)}, bf16[64,2048]{1,0:T(8,128)(2,1)S(1)}, u32[]{:S(2)}, u32[]{:S(2)}) collective-permute-start(bf16[64,2048]{1,0:T(8,128)(2,1)S(1)} %get-tuple-element.47), channel_id=1, source_target_pairs={{0,20},{4,16},{8,28},{12,24},{16,4},{20,0},{24,12},{28,8},{32,52},... | collective-permute-start | bytes 786440 | tf_op jit(solution)/shard_map/ppermute | solution.py:379
  54.9 1.6 %collective-permute-done.13.refs_1_ = bf16[64,2048]{1,0:T(8,128)(2,1)S(1)} collective-permute-done((bf16[64,2048]{1,0:T(8,128)(2,1)S(1)}, bf16[64,2048]{1,0:T(8,128)(2,1)S(1)}, u32[]{:S(2)}, u32[]{:S(2)}) %collective-permute-start.13) | collective-permute-done | bytes 262176 | tf_op jit(solution)/shard_map/ppermute | solution.py:379
  57.1 2.3 %collective-permute-done.14.refs_2_ = bf16[64,2048]{1,0:T(8,128)(2,1)S(1)} collective-permute-done((bf16[64,2048]{1,0:T(8,128)(2,1)S(1)}, bf16[64,2048]{1,0:T(8,128)(2,1)S(1)}, u32[]{:S(2)}, u32[]{:S(2)}) %collective-permute-start.14) | collective-permute-done | bytes 262176 | tf_op jit(solution)/shard_map/ppermute | solution.py:379
  59.4 2.3 %collective-permute-start.19 = (bf16[64,2048]{1,0:T(8,128)(2,1)S(1)}, bf16[64,2048]{1,0:T(8,128)(2,1)S(1)}, u32[]{:S(2)}, u32[]{:S(2)}) collective-permute-start(bf16[64,2048]{1,0:T(8,128)(2,1)S(1)} %get-tuple-element.51), channel_id=1, source_target_pairs={{0,24},{4,28},{8,0},{12,4},{16,8},{20,12},{24,16},{28,20},{32,56},... | collective-permute-start | bytes 786440 | tf_op jit(solution)/shard_map/ppermute | solution.py:379
  62.3 2.6 %collective-permute-done.16.refs_4_ = bf16[64,2048]{1,0:T(8,128)(2,1)S(1)} collective-permute-done((bf16[64,2048]{1,0:T(8,128)(2,1)S(1)}, bf16[64,2048]{1,0:T(8,128)(2,1)S(1)}, u32[]{:S(2)}, u32[]{:S(2)}) %collective-permute-start.16) | collective-permute-done | bytes 262176 | tf_op jit(solution)/shard_map/ppermute | solution.py:379
  66.5 1.6 %collective-permute-start.23 = (bf16[64,2048]{1,0:T(8,128)(2,1)S(1)}, bf16[64,2048]{1,0:T(8,128)(2,1)S(1)}, u32[]{:S(2)}, u32[]{:S(2)}) collective-permute-start(bf16[64,2048]{1,0:T(8,128)(2,1)S(1)} %get-tuple-element.55), channel_id=1, source_target_pairs={{0,28},{4,24},{8,4},{12,0},{16,12},{20,8},{24,20},{28,16},{32,60},... | collective-permute-start | bytes 786440 | tf_op jit(solution)/shard_map/ppermute | solution.py:379
  68.6 2.0 %collective-permute-done.20.refs_8_ = bf16[64,2048]{1,0:T(8,128)(2,1)S(1)} collective-permute-done((bf16[64,2048]{1,0:T(8,128)(2,1)S(1)}, bf16[64,2048]{1,0:T(8,128)(2,1)S(1)}, u32[]{:S(2)}, u32[]{:S(2)}) %collective-permute-start.20) | collective-permute-done | bytes 262176 | tf_op jit(solution)/shard_map/ppermute | solution.py:379
  70.6 1.5 collective-permute-start.30
  72.1 2.4 %collective-permute-done.21.refs_9_ = bf16[64,2048]{1,0:T(8,128)(2,1)S(1)} collective-permute-done((bf16[64,2048]{1,0:T(8,128)(2,1)S(1)}, bf16[64,2048]{1,0:T(8,128)(2,1)S(1)}, u32[]{:S(2)}, u32[]{:S(2)}) %collective-permute-start.21) | collective-permute-done | bytes 262176 | tf_op jit(solution)/shard_map/ppermute | solution.py:379
  74.5 1.8 %collective-permute-start.31 = (bf16[2,256,1024]{2,1,0:T(8,128)(2,1)S(1)}, bf16[2,256,1024]{2,1,0:T(8,128)(2,1)S(1)}, u32[]{:S(2)}, u32[]{:S(2)}) collective-permute-start(bf16[2,256,1024]{2,1,0:T(8,128)(2,1)S(1)} %get-tuple-element.64), channel_id=1, source_target_pairs={{0,3},{1,0},{2,1},{3,2},{4,7},{5,4},{6,5},{7,6},{8,11},{9,8},{10,9... | collective-permute-start | bytes 3145736 | tf_op jit(solution)/shard_map/ppermute | solution.py:369
  76.8 3.5 %load.1 = (bf16[2,4096,256]{2,1,0:T(8,128)(2,1)S(1)}, bf16[2,4096,256]{2,1,0:T(8,128)(2,1)S(1)}) custom-call(bf16[2,4096,256]{2,1,0:T(8,128)(2,1)} %refs_0_.1, bf16[2,4096,256]{2,1,0:T(8,128)(2,1)} %refs_1_.1), custom_call_target="tpu_custom_call" | custom-call | tf_op jit(solution)/shard_map/load/pallas_call | solution.py:261
  80.3 3.1 %gate_up.1.refs_0_ = bf16[2,256,256]{2,1,0:T(8,128)(2,1)S(1)} custom-call(s32[4]{0:T(128)S(1)} %pad_add_fusion.place, bf16[64,2048]{1,0:T(8,128)(2,1)S(1)} %collective-permute-done.12.refs_0_, bf16[64,2048]{1,0:T(8,128)(2,1)S(1)} %collective-permute-done.13.refs_1_, bf16[64,2048]{1,0:T(8,128)(2,1)S(1)} %collective-permute-done.14.refs_2_, ...), custom_call_target="tpu_custom_call" | custom-call | tf_op jit(solution)/shard_map/gate_up/pallas_call | solution.py:318
  83.8 1.5 collective-permute-start.27
  85.3 38.2 %collective-permute-done.26.refs_1_ = bf16[2,256,256]{2,1,0:T(8,128)(2,1)S(1)} collective-permute-done((bf16[2,256,256]{2,1,0:T(8,128)(2,1)S(1)}, bf16[2,256,256]{2,1,0:T(8,128)(2,1)S(1)}, u32[]{:S(2)}, u32[]{:S(2)}) %collective-permute-start.26) | collective-permute-done | bytes 262176 | tf_op jit(solution)/shard_map/ppermute | solution.py:369
  124.1 4.5 %collective-permute-done.27.refs_2_ = bf16[2,256,256]{2,1,0:T(8,128)(2,1)S(1)} collective-permute-done((bf16[2,256,256]{2,1,0:T(8,128)(2,1)S(1)}, bf16[2,256,256]{2,1,0:T(8,128)(2,1)S(1)}, u32[]{:S(2)}, u32[]{:S(2)}) %collective-permute-start.27) | collective-permute-done | bytes 262176 | tf_op jit(solution)/shard_map/ppermute | solution.py:369
  128.6 2.3 %collective-permute-done.28.refs_3_ = bf16[2,256,256]{2,1,0:T(8,128)(2,1)S(1)} collective-permute-done((bf16[2,256,256]{2,1,0:T(8,128)(2,1)S(1)}, bf16[2,256,256]{2,1,0:T(8,128)(2,1)S(1)}, u32[]{:S(2)}, u32[]{:S(2)}) %collective-permute-start.28) | collective-permute-done | bytes 262176 | tf_op jit(solution)/shard_map/ppermute | solution.py:369
  131.0 3.9 %down.1 = bf16[32,16,1024]{2,1,0:T(8,128)(2,1)} custom-call(s32[4]{0:T(128)S(1)} %pad_add_fusion.place, bf16[2,256,256]{2,1,0:T(8,128)(2,1)S(1)} %gate_up.1.refs_0_, bf16[2,256,256]{2,1,0:T(8,128)(2,1)S(1)} %collective-permute-done.26.refs_1_, bf16[2,256,256]{2,1,0:T(8,128)(2,1)S(1)} %collective-permute-done.27.refs_2_, ...), custom_call_target="tpu_custom_call" | custom-call | tf_op jit(solution)/shard_map/down/pallas_call | solution.py:341
  134.8 5.5 %all-to-all-start = ((bf16[32,16,1024]{2,1,0:T(8,128)(2,1)}), bf16[32,16,1024]{2,1,0:T(8,128)(2,1)S(1)}, u32[]{:S(2)}, u32[]{:S(2)}) async-start(bf16[32,16,1024]{2,1,0:T(8,128)(2,1)} %down.1), calls=%async_computation | async-start | bytes 2097152 | tf_op jit(solution)/shard_map/all_to_all | solution.py:444
  141.1 16.4 %all-to-all-done = bf16[32,16,1024]{2,1,0:T(8,128)(2,1)S(1)} async-done(((bf16[32,16,1024]{2,1,0:T(8,128)(2,1)}), bf16[32,16,1024]{2,1,0:T(8,128)(2,1)S(1)}, u32[]{:S(2)}, u32[]{:S(2)}) %all-to-all-start) | async-done | bytes 1048608 | tf_op jit(solution)/shard_map/all_to_all | solution.py:444
  (61 shorter events, 21.5 us)
Async XLA Ops:
  7.6 9.1 %collective-permute-start = (bf16[32,1024]{1,0:T(8,128)(2,1)S(1)}, bf16[32,1024]{1,0:T(8,128)(2,1)}, u32[]{:S(2)}, u32[]{:S(2)}) collective-permute-start(bf16[32,1024]{1,0:T(8,128)(2,1)S(1)} %get-tuple-element.36), channel_id=1, source_target_pairs={{0,1},{1,2},{2,3},{3,0},{4,5},{5,6},{6,7},{7,4},{8,9},{9,10},{10,1... | collective-permute-start | bytes 196616 | tf_op jit(solution)/shard_map/ppermute | solution.py:369
  9.7 7.1 %collective-permute-start.1 = (bf16[32,1024]{1,0:T(8,128)(2,1)S(1)}, bf16[32,1024]{1,0:T(8,128)(2,1)}, u32[]{:S(2)}, u32[]{:S(2)}) collective-permute-start(bf16[32,1024]{1,0:T(8,128)(2,1)S(1)} %get-tuple-element.37), channel_id=1, source_target_pairs={{0,2},{1,3},{2,0},{3,1},{4,6},{5,7},{6,4},{7,5},{8,10},{9,11},{10,... | collective-permute-start | bytes 196616 | tf_op jit(solution)/shard_map/ppermute | solution.py:369
  13.3 4.4 %collective-permute-start.2 = (bf16[32,1024]{1,0:T(8,128)(2,1)S(1)}, bf16[32,1024]{1,0:T(8,128)(2,1)}, u32[]{:S(2)}, u32[]{:S(2)}) collective-permute-start(bf16[32,1024]{1,0:T(8,128)(2,1)S(1)} %get-tuple-element.38), channel_id=1, source_target_pairs={{0,3},{1,0},{2,1},{3,2},{4,7},{5,4},{6,5},{7,6},{8,11},{9,8},{10,9... | collective-permute-start | bytes 196616 | tf_op jit(solution)/shard_map/ppermute | solution.py:369
  19.3 5.7 %collective-permute-start.3 = (bf16[32,1024]{1,0:T(8,128)(2,1)}, bf16[32,1024]{1,0:T(8,128)(2,1)S(1)}, u32[]{:S(2)}, u32[]{:S(2)}) collective-permute-start(bf16[32,1024]{1,0:T(8,128)(2,1)} %get-tuple-element.65), channel_id=1, source_target_pairs={{0,1},{1,2},{2,3},{3,0},{4,5},{5,6},{6,7},{7,4},{8,9},{9,10},{10,1... | collective-permute-start | bytes 196616 | tf_op jit(solution)/shard_map/ppermute | solution.py:369
  19.5 6.6 %collective-permute-start.4 = (bf16[32,1024]{1,0:T(8,128)(2,1)}, bf16[32,1024]{1,0:T(8,128)(2,1)S(1)}, u32[]{:S(2)}, u32[]{:S(2)}) collective-permute-start(bf16[32,1024]{1,0:T(8,128)(2,1)} %get-tuple-element.65), channel_id=1, source_target_pairs={{0,2},{1,3},{2,0},{3,1},{4,6},{5,7},{6,4},{7,5},{8,10},{9,11},{10,... | collective-permute-start | bytes 196616 | tf_op jit(solution)/shard_map/ppermute | solution.py:369
  23.0 4.5 %collective-permute-start.5 = (bf16[32,1024]{1,0:T(8,128)(2,1)}, bf16[32,1024]{1,0:T(8,128)(2,1)S(1)}, u32[]{:S(2)}, u32[]{:S(2)}) collective-permute-start(bf16[32,1024]{1,0:T(8,128)(2,1)} %get-tuple-element.65), channel_id=1, source_target_pairs={{0,3},{1,0},{2,1},{3,2},{4,7},{5,4},{6,5},{7,6},{8,11},{9,8},{10,9... | collective-permute-start | bytes 196616 | tf_op jit(solution)/shard_map/ppermute | solution.py:369
  28.2 8.2 %collective-permute-start.10 = (bf16[40,2048]{1,0:T(8,128)(2,1)S(1)}, bf16[40,2048]{1,0:T(8,128)(2,1)S(1)}, u32[]{:S(2)}, u32[]{:S(2)}) collective-permute-start(bf16[40,2048]{1,0:T(8,128)(2,1)S(1)} %get-tuple-element.42.refs_6_), channel_id=1, source_target_pairs={{0,24},{4,28},{8,0},{12,4},{16,8},{20,12},{24,16},{28,20},{32,56},... | collective-permute-start | bytes 491528 | tf_op jit(solution)/shard_map/ppermute | solution.py:379
  31.0 8.4 %collective-permute-start.6 = (bf16[40,2048]{1,0:T(8,128)(2,1)S(1)}, bf16[40,2048]{1,0:T(8,128)(2,1)S(1)}, u32[]{:S(2)}, u32[]{:S(2)}) collective-permute-start(bf16[40,2048]{1,0:T(8,128)(2,1)S(1)} %get-tuple-element.42.refs_6_), channel_id=1, source_target_pairs={{0,16},{4,20},{8,24},{12,28},{16,0},{20,4},{24,8},{28,12},{32,48},... | collective-permute-start | bytes 491528 | tf_op jit(solution)/shard_map/ppermute | solution.py:379
  31.8 7.6 %collective-permute-start.11 = (bf16[40,2048]{1,0:T(8,128)(2,1)S(1)}, bf16[40,2048]{1,0:T(8,128)(2,1)S(1)}, u32[]{:S(2)}, u32[]{:S(2)}) collective-permute-start(bf16[40,2048]{1,0:T(8,128)(2,1)S(1)} %get-tuple-element.43.refs_7_), channel_id=1, source_target_pairs={{0,96},{4,100},{8,104},{12,108},{16,112},{20,116},{24,120},{28,124... | collective-permute-start | bytes 491528 | tf_op jit(solution)/shard_map/ppermute | solution.py:379
  34.8 6.9 %collective-permute-start.7 = (bf16[40,2048]{1,0:T(8,128)(2,1)S(1)}, bf16[40,2048]{1,0:T(8,128)(2,1)S(1)}, u32[]{:S(2)}, u32[]{:S(2)}) collective-permute-start(bf16[40,2048]{1,0:T(8,128)(2,1)S(1)} %get-tuple-element.43.refs_7_), channel_id=1, source_target_pairs={{0,64},{4,68},{8,72},{12,76},{16,80},{20,84},{24,88},{28,92},{32,9... | collective-permute-start | bytes 491528 | tf_op jit(solution)/shard_map/ppermute | solution.py:379
  35.4 6.5 %collective-permute-start.8 = (bf16[40,2048]{1,0:T(8,128)(2,1)S(1)}, bf16[40,2048]{1,0:T(8,128)(2,1)S(1)}, u32[]{:S(2)}, u32[]{:S(2)}) collective-permute-start(bf16[40,2048]{1,0:T(8,128)(2,1)S(1)} %get-tuple-element.42.refs_6_), channel_id=1, source_target_pairs={{0,8},{4,12},{8,16},{12,20},{16,24},{20,28},{24,0},{28,4},{32,40},... | collective-permute-start | bytes 491528 | tf_op jit(solution)/shard_map/ppermute | solution.py:379
  36.3 7.1 %collective-permute-start.9 = (bf16[40,2048]{1,0:T(8,128)(2,1)S(1)}, bf16[40,2048]{1,0:T(8,128)(2,1)S(1)}, u32[]{:S(2)}, u32[]{:S(2)}) collective-permute-start(bf16[40,2048]{1,0:T(8,128)(2,1)S(1)} %get-tuple-element.43.refs_7_), channel_id=1, source_target_pairs={{0,32},{4,36},{8,40},{12,44},{16,48},{20,52},{24,56},{28,60},{32,6... | collective-permute-start | bytes 491528 | tf_op jit(solution)/shard_map/ppermute | solution.py:379
  45.7 8.0 %collective-permute-start.12 = (bf16[64,2048]{1,0:T(8,128)(2,1)S(1)}, bf16[64,2048]{1,0:T(8,128)(2,1)S(1)}, u32[]{:S(2)}, u32[]{:S(2)}) collective-permute-start(bf16[64,2048]{1,0:T(8,128)(2,1)S(1)} %get-tuple-element.44), channel_id=1, source_target_pairs={{0,64},{4,68},{8,72},{12,76},{16,80},{20,84},{24,88},{28,92},{32,9... | collective-permute-start | bytes 786440 | tf_op jit(solution)/shard_map/ppermute | solution.py:379
  47.3 9.3 %collective-permute-start.13 = (bf16[64,2048]{1,0:T(8,128)(2,1)S(1)}, bf16[64,2048]{1,0:T(8,128)(2,1)S(1)}, u32[]{:S(2)}, u32[]{:S(2)}) collective-permute-start(bf16[64,2048]{1,0:T(8,128)(2,1)S(1)} %get-tuple-element.45), channel_id=1, source_target_pairs={{0,16},{4,20},{8,24},{12,28},{16,0},{20,4},{24,8},{28,12},{32,48},... | collective-permute-start | bytes 786440 | tf_op jit(solution)/shard_map/ppermute | solution.py:379
  49.1 10.2 %collective-permute-start.14 = (bf16[64,2048]{1,0:T(8,128)(2,1)S(1)}, bf16[64,2048]{1,0:T(8,128)(2,1)S(1)}, u32[]{:S(2)}, u32[]{:S(2)}) collective-permute-start(bf16[64,2048]{1,0:T(8,128)(2,1)S(1)} %get-tuple-element.46), channel_id=1, source_target_pairs={{0,68},{4,64},{8,76},{12,72},{16,84},{20,80},{24,92},{28,88},{32,1... | collective-permute-start | bytes 786440 | tf_op jit(solution)/shard_map/ppermute | solution.py:379
  49.1 12.5 %collective-permute-start.15 = (bf16[64,2048]{1,0:T(8,128)(2,1)S(1)}, bf16[64,2048]{1,0:T(8,128)(2,1)S(1)}, u32[]{:S(2)}, u32[]{:S(2)}) collective-permute-start(bf16[64,2048]{1,0:T(8,128)(2,1)S(1)} %get-tuple-element.47), channel_id=1, source_target_pairs={{0,20},{4,16},{8,28},{12,24},{16,4},{20,0},{24,12},{28,8},{32,52},... | collective-permute-start | bytes 786440 | tf_op jit(solution)/shard_map/ppermute | solution.py:379
  52.6 12.3 %collective-permute-start.16 = (bf16[64,2048]{1,0:T(8,128)(2,1)S(1)}, bf16[64,2048]{1,0:T(8,128)(2,1)S(1)}, u32[]{:S(2)}, u32[]{:S(2)}) collective-permute-start(bf16[64,2048]{1,0:T(8,128)(2,1)S(1)} %get-tuple-element.48), channel_id=1, source_target_pairs={{0,32},{4,36},{8,40},{12,44},{16,48},{20,52},{24,56},{28,60},{32,6... | collective-permute-start | bytes 786440 | tf_op jit(solution)/shard_map/ppermute | solution.py:379
  53.7 12.7 %collective-permute-start.17 = (bf16[64,2048]{1,0:T(8,128)(2,1)S(1)}, bf16[64,2048]{1,0:T(8,128)(2,1)S(1)}, u32[]{:S(2)}, u32[]{:S(2)}) collective-permute-start(bf16[64,2048]{1,0:T(8,128)(2,1)S(1)} %get-tuple-element.49), channel_id=1, source_target_pairs={{0,8},{4,12},{8,16},{12,20},{16,24},{20,28},{24,0},{28,4},{32,40},... | collective-permute-start | bytes 786440 | tf_op jit(solution)/shard_map/ppermute | solution.py:379
  56.5 10.0 %collective-permute-start.18 = (bf16[64,2048]{1,0:T(8,128)(2,1)S(1)}, bf16[64,2048]{1,0:T(8,128)(2,1)S(1)}, u32[]{:S(2)}, u32[]{:S(2)}) collective-permute-start(bf16[64,2048]{1,0:T(8,128)(2,1)S(1)} %get-tuple-element.50), channel_id=1, source_target_pairs={{0,96},{4,100},{8,104},{12,108},{16,112},{20,116},{24,120},{28,124... | collective-permute-start | bytes 786440 | tf_op jit(solution)/shard_map/ppermute | solution.py:379
  59.4 8.8 %collective-permute-start.19 = (bf16[64,2048]{1,0:T(8,128)(2,1)S(1)}, bf16[64,2048]{1,0:T(8,128)(2,1)S(1)}, u32[]{:S(2)}, u32[]{:S(2)}) collective-permute-start(bf16[64,2048]{1,0:T(8,128)(2,1)S(1)} %get-tuple-element.51), channel_id=1, source_target_pairs={{0,24},{4,28},{8,0},{12,4},{16,8},{20,12},{24,16},{28,20},{32,56},... | collective-permute-start | bytes 786440 | tf_op jit(solution)/shard_map/ppermute | solution.py:379
  61.6 9.0 %collective-permute-start.20 = (bf16[64,2048]{1,0:T(8,128)(2,1)S(1)}, bf16[64,2048]{1,0:T(8,128)(2,1)S(1)}, u32[]{:S(2)}, u32[]{:S(2)}) collective-permute-start(bf16[64,2048]{1,0:T(8,128)(2,1)S(1)} %get-tuple-element.52), channel_id=1, source_target_pairs={{0,36},{4,32},{8,44},{12,40},{16,52},{20,48},{24,60},{28,56},{32,6... | collective-permute-start | bytes 786440 | tf_op jit(solution)/shard_map/ppermute | solution.py:379
  64.9 9.6 %collective-permute-start.21 = (bf16[64,2048]{1,0:T(8,128)(2,1)S(1)}, bf16[64,2048]{1,0:T(8,128)(2,1)S(1)}, u32[]{:S(2)}, u32[]{:S(2)}) collective-permute-start(bf16[64,2048]{1,0:T(8,128)(2,1)S(1)} %get-tuple-element.53), channel_id=1, source_target_pairs={{0,12},{4,8},{8,20},{12,16},{16,28},{20,24},{24,4},{28,0},{32,44},... | collective-permute-start | bytes 786440 | tf_op jit(solution)/shard_map/ppermute | solution.py:379
  66.4 9.9 %collective-permute-start.22 = (bf16[64,2048]{1,0:T(8,128)(2,1)S(1)}, bf16[64,2048]{1,0:T(8,128)(2,1)S(1)}, u32[]{:S(2)}, u32[]{:S(2)}) collective-permute-start(bf16[64,2048]{1,0:T(8,128)(2,1)S(1)} %get-tuple-element.54), channel_id=1, source_target_pairs={{0,100},{4,96},{8,108},{12,104},{16,116},{20,112},{24,124},{28,120... | collective-permute-start | bytes 786440 | tf_op jit(solution)/shard_map/ppermute | solution.py:379
  66.5 9.8 %collective-permute-start.23 = (bf16[64,2048]{1,0:T(8,128)(2,1)S(1)}, bf16[64,2048]{1,0:T(8,128)(2,1)S(1)}, u32[]{:S(2)}, u32[]{:S(2)}) collective-permute-start(bf16[64,2048]{1,0:T(8,128)(2,1)S(1)} %get-tuple-element.55), channel_id=1, source_target_pairs={{0,28},{4,24},{8,4},{12,0},{16,12},{20,8},{24,20},{28,16},{32,60},... | collective-permute-start | bytes 786440 | tf_op jit(solution)/shard_map/ppermute | solution.py:379
  68.2 62.8 %collective-permute-start.29 = (bf16[2,256,1024]{2,1,0:T(8,128)(2,1)S(1)}, bf16[2,256,1024]{2,1,0:T(8,128)(2,1)S(1)}, u32[]{:S(2)}, u32[]{:S(2)}) collective-permute-start(bf16[2,256,1024]{2,1,0:T(8,128)(2,1)S(1)} %get-tuple-element.62), channel_id=1, source_target_pairs={{0,1},{1,2},{2,3},{3,0},{4,5},{5,6},{6,7},{7,4},{8,9},{9,10},{10,1... | collective-permute-start | bytes 3145736 | tf_op jit(solution)/shard_map/ppermute | solution.py:369
  70.6 60.4 %collective-permute-start.30 = (bf16[2,256,1024]{2,1,0:T(8,128)(2,1)S(1)}, bf16[2,256,1024]{2,1,0:T(8,128)(2,1)S(1)}, u32[]{:S(2)}, u32[]{:S(2)}) collective-permute-start(bf16[2,256,1024]{2,1,0:T(8,128)(2,1)S(1)} %get-tuple-element.63), channel_id=1, source_target_pairs={{0,2},{1,3},{2,0},{3,1},{4,6},{5,7},{6,4},{7,5},{8,10},{9,11},{10,... | collective-permute-start | bytes 3145736 | tf_op jit(solution)/shard_map/ppermute | solution.py:369
  74.5 56.5 %collective-permute-start.31 = (bf16[2,256,1024]{2,1,0:T(8,128)(2,1)S(1)}, bf16[2,256,1024]{2,1,0:T(8,128)(2,1)S(1)}, u32[]{:S(2)}, u32[]{:S(2)}) collective-permute-start(bf16[2,256,1024]{2,1,0:T(8,128)(2,1)S(1)} %get-tuple-element.64), channel_id=1, source_target_pairs={{0,3},{1,0},{2,1},{3,2},{4,7},{5,4},{6,5},{7,6},{8,11},{9,8},{10,9... | collective-permute-start | bytes 3145736 | tf_op jit(solution)/shard_map/ppermute | solution.py:369
  76.3 4.0 %collective-permute-start.25 = (bf16[64,2048]{1,0:T(8,128)(2,1)S(1)}, bf16[64,2048]{1,0:T(8,128)(2,1)S(1)}, u32[]{:S(2)}, u32[]{:S(2)}) collective-permute-start(bf16[64,2048]{1,0:T(8,128)(2,1)S(1)} %get-tuple-element.57), channel_id=1, source_target_pairs={{0,4},{4,0},{8,12},{12,8},{16,20},{20,16},{24,28},{28,24},{32,36},... | collective-permute-start | bytes 786440 | tf_op jit(solution)/shard_map/ppermute | solution.py:379
  83.4 40.0 %collective-permute-start.26 = (bf16[2,256,256]{2,1,0:T(8,128)(2,1)S(1)}, bf16[2,256,256]{2,1,0:T(8,128)(2,1)S(1)}, u32[]{:S(2)}, u32[]{:S(2)}) collective-permute-start(bf16[2,256,256]{2,1,0:T(8,128)(2,1)S(1)} %gate_up.1.refs_0_), channel_id=1, source_target_pairs={{0,1},{1,2},{2,3},{3,0},{4,5},{5,6},{6,7},{7,4},{8,9},{9,10},{10,1... | collective-permute-start | bytes 786440 | tf_op jit(solution)/shard_map/ppermute | solution.py:369
  83.8 44.9 %collective-permute-start.27 = (bf16[2,256,256]{2,1,0:T(8,128)(2,1)S(1)}, bf16[2,256,256]{2,1,0:T(8,128)(2,1)S(1)}, u32[]{:S(2)}, u32[]{:S(2)}) collective-permute-start(bf16[2,256,256]{2,1,0:T(8,128)(2,1)S(1)} %gate_up.1.refs_0_), channel_id=1, source_target_pairs={{0,2},{1,3},{2,0},{3,1},{4,6},{5,7},{6,4},{7,5},{8,10},{9,11},{10,... | collective-permute-start | bytes 786440 | tf_op jit(solution)/shard_map/ppermute | solution.py:369
  123.5 7.5 %collective-permute-start.28 = (bf16[2,256,256]{2,1,0:T(8,128)(2,1)S(1)}, bf16[2,256,256]{2,1,0:T(8,128)(2,1)S(1)}, u32[]{:S(2)}, u32[]{:S(2)}) collective-permute-start(bf16[2,256,256]{2,1,0:T(8,128)(2,1)S(1)} %gate_up.1.refs_0_), channel_id=1, source_target_pairs={{0,3},{1,0},{2,1},{3,2},{4,7},{5,4},{6,5},{7,6},{8,11},{9,8},{10,9... | collective-permute-start | bytes 786440 | tf_op jit(solution)/shard_map/ppermute | solution.py:369
  134.8 22.7 %all-to-all-start = ((bf16[32,16,1024]{2,1,0:T(8,128)(2,1)}), bf16[32,16,1024]{2,1,0:T(8,128)(2,1)S(1)}, u32[]{:S(2)}, u32[]{:S(2)}) async-start(bf16[32,16,1024]{2,1,0:T(8,128)(2,1)} %down.1), calls=%async_computation | async-start | bytes 2097152 | tf_op jit(solution)/shard_map/all_to_all | solution.py:444
  (4 other events, 97.0 us)
